TPU v7x, 32 devices: a whole 2x2x4 slice. The times are simulated.
32 devices in a mesh: head: 4 (over y, x), frame: 8 (over z, core).
Axes of the slice: x: 2, y: 2, z: 4, core: 2. Of those that a mesh axis runs over, the one named last changes fastest.
Arguments:
- query_tok: bfloat16 [6144, 3072], P('frame', 'head'), may hold values from -200 to 200
- key_tok: bfloat16 [6144, 3072], P('frame', 'head'), may hold values from -8 to 8
- value_tok: bfloat16 [6144, 3072], P('frame', 'head'), may hold values from -6 to 6
- head_span: int32 [24], P('head'), may hold values from 0 to 3
- out_weight: bfloat16 [3072, 3072], P('head'), may hold values from -0.109375 to 0.109375
Outputs:
- projected: bfloat16 [6144, 3072], P('frame', 'head')
All inputs are finite; a program needn't handle non-finite values.
Results may differ from a plain program's by a relative error of at most 0.012.
Values may be sent and summed in bfloat16 or wider, within the bound.
No kernel may reach another device: no remote copies, remote signals or barrier semaphores. Data moves between devices by JAX's collectives and lax.ppermute only.
A program may use at most 128 MiB of HBM per device.

v0:
```python
import jax
import jax.numpy as jnp
from jax import lax
from jax.sharding import PartitionSpec as P

HD = 128
FRAME_TOK = 384


def from_behind(value, axis, steps):
    count = lax.axis_size(axis)
    leading, last = (max(0, -steps), min(count, count - steps))
    return lax.ppermute(value, axis, [(source, source + steps) for source in range(leading, last)])


def attend_frame(query_frame, key_rows, value_rows, frame_pos, head_span, frame_count):
    scale = 1.0 / HD**0.5
    scores = (
        jnp.einsum("qhd,khd->hqk", query_frame, key_rows, preferred_element_type=jnp.float32)
        * scale
    )
    offsets = jnp.arange(7, dtype=jnp.int32) - 3
    allowed = (
        (jnp.abs(offsets)[None, :] <= head_span[:, None])
        & (frame_pos + offsets >= 0)[None, :]
        & (frame_pos + offsets < frame_count)[None, :]
    )
    visible = jnp.repeat(allowed, FRAME_TOK, axis=1)[:, None, :]
    scores = jnp.where(visible, scores, -1e30)
    rowmax = jnp.max(scores, axis=2, keepdims=True)
    weights = jnp.where(visible, jnp.exp(scores - rowmax), 0.0)
    total = jnp.sum(weights, axis=2)
    probs = weights.astype(jnp.bfloat16)
    mixed = jnp.einsum("hqk,khd->qhd", probs, value_rows, preferred_element_type=jnp.float32)
    return (mixed / jnp.transpose(total)[:, :, None]).astype(jnp.bfloat16)


def body(query_tok, key_tok, value_tok, head_span, out_weight):
    local_frames = key_tok.shape[0] // FRAME_TOK
    heads_here = head_span.shape[0]
    width = key_tok.shape[1]
    key_local = key_tok.reshape(local_frames, FRAME_TOK, width)
    value_local = value_tok.reshape(local_frames, FRAME_TOK, width)
    received = {}
    for offset in (1, -1):
        received[offset] = from_behind((key_local, value_local), "frame", offset)
    for offset, picked in ((2, 1), (-2, 0)):
        received[offset] = from_behind(
            (key_local[picked : picked + 1], value_local[picked : picked + 1]), "frame", offset
        )
    lower = received[2]
    upper = received[-2]
    key_window = jnp.concatenate(
        [lower[0], received[1][0], key_local, received[-1][0], upper[0]], axis=0
    )
    value_window = jnp.concatenate(
        [lower[1], received[1][1], value_local, received[-1][1], upper[1]], axis=0
    )
    frame_count = lax.axis_size("frame") * local_frames
    first_frame = lax.axis_index("frame") * local_frames
    query_all = query_tok.reshape(local_frames, FRAME_TOK, heads_here, HD)
    outputs = []
    for local in range(local_frames):
        key_rows = key_window[local : local + 7].reshape(7 * FRAME_TOK, heads_here, HD)
        value_rows = value_window[local : local + 7].reshape(7 * FRAME_TOK, heads_here, HD)
        outputs.append(
            attend_frame(
                query_all[local], key_rows, value_rows, first_frame + local, head_span, frame_count
            )
        )
    attended = jnp.concatenate(outputs, axis=0).reshape(local_frames * FRAME_TOK, width)
    terms = jnp.dot(attended, out_weight, preferred_element_type=jnp.float32)
    return lax.psum_scatter(terms.astype(jnp.bfloat16), "head", scatter_dimension=1, tiled=True)


def solution(mesh):
    return jax.shard_map(
        body,
        mesh=mesh,
        in_specs=(
            P("frame", "head"),
            P("frame", "head"),
            P("frame", "head"),
            P("head"),
            P("head", None),
        ),
        out_specs=P("frame", "head"),
        check_vma=False,
    )
```

profile of v0, /device:TPU:0, one launch (start us, length us, event | category | flops | bytes accessed | tf_op | source)
XLA Modules:
  0.0 265.4 jit_solution(7419553783181557122)
XLA Ops:
  6.5 3.8 %copy.14 = bf16[2,384,768]{1,0,2:T(2,128)(2,1)S(1)} copy(bf16[2,384,768]{2,1,0:T(8,128)(2,1)} %bitcast.81) | data formatting | bytes 2359296 | tf_op jit(solution)/shard_map/reshape | solution.py:43
  10.3 1.3 collective-permute-start.2
  11.6 4.1 %collective-permute-start.1 = (bf16[2,384,768]{1,0,2:T(2,128)(2,1)S(1)}, bf16[2,384,768]{1,0,2:T(2,128)(2,1)}, u32[]{:S(2)}, u32[]{:S(2)}) collective-permute-start(bf16[2,384,768]{1,0,2:T(2,128)(2,1)S(1)} %copy.14), channel_id=1, source_target_pairs={{0,1},{1,2},{2,3},{3,4},{4,5},{5,6},{6,7},{8,9},{9,10},{10,11},{11... | collective-permute-start | bytes 3538952 | tf_op jit(solution)/shard_map/ppermute | solution.py:13
  15.7 2.4 slice_bitcast_fusion.2
  18.0 4.8 %collective-permute-start.3 = (bf16[1,384,768]{2,1,0:T(8,128)(2,1)}, bf16[1,384,768]{2,1,0:T(8,128)(2,1)}, u32[]{:S(2)}, u32[]{:S(2)}) collective-permute-start(bf16[1,384,768]{2,1,0:T(8,128)(2,1)} %get-tuple-element.11), channel_id=1, source_target_pairs={{0,2},{1,3},{2,4},{3,5},{4,6},{5,7},{8,10},{9,11},{10,12},{11,13},... | collective-permute-start | bytes 1769480 | tf_op jit(solution)/shard_map/ppermute | solution.py:13
  22.8 1.3 collective-permute-start.7
  24.1 1.1 slice_bitcast_fusion.3
  25.2 5.4 %collective-permute-start = (bf16[1,384,768]{2,1,0:T(8,128)(2,1)}, bf16[1,384,768]{2,1,0:T(8,128)(2,1)}, u32[]{:S(2)}, u32[]{:S(2)}) collective-permute-start(bf16[1,384,768]{2,1,0:T(8,128)(2,1)} %get-tuple-element.13), channel_id=1, source_target_pairs={{0,2},{1,3},{2,4},{3,5},{4,6},{5,7},{8,10},{9,11},{10,12},{11,13},... | collective-permute-start | bytes 1769480 | tf_op jit(solution)/shard_map/ppermute | solution.py:13
  30.6 0.1 fusion.44
  30.7 5.3 %collective-permute-done.3 = bf16[1,384,768]{2,1,0:T(8,128)(2,1)} collective-permute-done((bf16[1,384,768]{2,1,0:T(8,128)(2,1)}, bf16[1,384,768]{2,1,0:T(8,128)(2,1)}, u32[]{:S(2)}, u32[]{:S(2)}) %collective-permute-start.3) | collective-permute-done | bytes 589856 | tf_op jit(solution)/shard_map/ppermute | solution.py:13
  36.0 1.3 collective-permute-start.6
  37.3 0.7 broadcast_bitcast_fusion.1
  38.0 1.4 copy.18
  39.4 2.8 %collective-permute-done.7 = bf16[1,384,768]{2,1,0:T(8,128)(2,1)} collective-permute-done((bf16[1,384,768]{2,1,0:T(8,128)(2,1)}, bf16[1,384,768]{2,1,0:T(8,128)(2,1)}, u32[]{:S(2)}, u32[]{:S(2)}) %collective-permute-start.7) | collective-permute-done | bytes 589856 | tf_op jit(solution)/shard_map/ppermute | solution.py:13
  42.2 1.3 collective-permute-start.5
  43.5 5.1 %collective-permute-done = bf16[1,384,768]{2,1,0:T(8,128)(2,1)} collective-permute-done((bf16[1,384,768]{2,1,0:T(8,128)(2,1)}, bf16[1,384,768]{2,1,0:T(8,128)(2,1)}, u32[]{:S(2)}, u32[]{:S(2)}) %collective-permute-start) | collective-permute-done | bytes 589856 | tf_op jit(solution)/shard_map/ppermute | solution.py:13
  48.6 10.1 %collective-permute-start.4 = (bf16[2,384,768]{1,0,2:T(2,128)(2,1)S(1)}, bf16[2,384,768]{1,0,2:T(2,128)(2,1)}, u32[]{:S(2)}, u32[]{:S(2)}) collective-permute-start(bf16[2,384,768]{1,0,2:T(2,128)(2,1)S(1)} %copy.18), channel_id=1, source_target_pairs={{0,1},{1,2},{2,3},{3,4},{4,5},{5,6},{6,7},{8,9},{9,10},{10,11},{11... | collective-permute-start | bytes 3538952 | tf_op jit(solution)/shard_map/ppermute | solution.py:13
  58.8 0.1 broadcast_bitcast_fusion
  58.8 1.3 copy.42
  60.2 0.6 copy.43
  60.8 1.3 fusion.57
  62.1 1.0 copy.40
  63.2 1.1 copy.41
  64.2 3.5 %copy.20 = bf16[1,384,768]{1,0,2:T(2,128)(2,1)S(1)} copy(bf16[1,384,768]{2,1,0:T(8,128)(2,1)} %collective-permute-done.3) | data formatting | bytes 1179648 | tf_op jit(solution)/shard_map/ppermute | solution.py:13
  67.7 4.6 %copy.29 = bf16[1,384,768]{1,0,2:T(2,128)(2,1)} copy(bf16[1,384,768]{2,1,0:T(8,128)(2,1)} %collective-permute-done.7) | data formatting | bytes 1179648 | tf_op jit(solution)/shard_map/ppermute | solution.py:13
  72.4 4.6 %copy.16 = bf16[1,384,768]{1,0,2:T(2,128)(2,1)} copy(bf16[1,384,768]{2,1,0:T(8,128)(2,1)} %collective-permute-done) | data formatting | bytes 1179648 | tf_op jit(solution)/shard_map/ppermute | solution.py:13
  77.0 0.0 collective-permute-done.6
  77.0 4.6 %copy.27 = bf16[1,384,768]{1,0,2:T(2,128)(2,1)} copy(bf16[1,384,768]{2,1,0:T(8,128)(2,1)} %collective-permute-done.6) | data formatting | bytes 1179648 | tf_op jit(solution)/shard_map/ppermute | solution.py:13
  81.6 0.0 collective-permute-done.2
  81.6 0.0 collective-permute-done.1
  81.6 13.8 %pad_maximum_fusion = (bf16[7,384,768]{1,0,2:T(8,128)(2,1)}, bf16[7,384,768]{1,0,2:T(8,128)(2,1)}) fusion(bf16[2,384,768]{1,0,2:T(2,128)(2,1)} %collective-permute-done.2, bf16[2,384,768]{1,0,2:T(2,128)(2,1)S(1)} %copy.14, bf16[2,384,768]{1,0,2:T(2,128)(2,1)} %collective-permute-done.1, bf16[1,384,768]{1,0,2:T(2,128)(2,1)} %copy.16, ...), kind=kLoop, calls=%fused_computation.25 | loop fusion | flops 33030144 | bytes 12976128 | tf_op jit(solution)/shard_map/concatenate | solution.py:56
  95.5 8.9 %reshape.57 = bf16[2688,6,128]{0,2,1:T(8,128)(2,1)} reshape(bf16[7,384,768]{1,0,2:T(8,128)(2,1)} %get-tuple-element.7) | data formatting | bytes 8257536 | tf_op jit(solution)/shard_map/reshape | solution.py:65
  104.4 0.0 collective-permute-done.5
  104.4 0.0 collective-permute-done.4
  104.4 0.0 copy-done.2
  104.4 13.8 %pad_maximum_fusion.1 = (bf16[7,384,768]{1,0,2:T(8,128)(2,1)}, bf16[7,384,768]{1,0,2:T(8,128)(2,1)}) fusion(bf16[2,384,768]{1,0,2:T(2,128)(2,1)} %collective-permute-done.5, bf16[2,384,768]{1,0,2:T(2,128)(2,1)S(1)} %copy.18, bf16[2,384,768]{1,0,2:T(2,128)(2,1)} %collective-permute-done.4, bf16[1,384,768]{1,0,2:T(2,128)(2,1)S(1)} %copy.20, ...), kind=kLoop, calls=%fused_computation.26 | loop fusion | flops 33030144 | bytes 12976128 | tf_op jit(solution)/shard_map/concatenate | solution.py:53
  118.2 8.8 %reshape.59 = bf16[2688,6,128]{0,2,1:T(8,128)(2,1)} reshape(bf16[7,384,768]{1,0,2:T(8,128)(2,1)} %get-tuple-element.5) | data formatting | bytes 8257536 | tf_op jit(solution)/shard_map/reshape | solution.py:64
  127.0 8.8 %reshape.61 = bf16[2688,6,128]{0,2,1:T(8,128)(2,1)} reshape(bf16[7,384,768]{1,0,2:T(8,128)(2,1)} %get-tuple-element.6) | data formatting | bytes 8257536 | tf_op jit(solution)/shard_map/reshape | solution.py:64
  135.8 8.9 %reshape.60 = bf16[2688,6,128]{0,2,1:T(8,128)(2,1)} reshape(bf16[7,384,768]{1,0,2:T(8,128)(2,1)} %get-tuple-element.8) | data formatting | bytes 8257536 | tf_op jit(solution)/shard_map/reshape | solution.py:65
  144.7 15.2 %fusion.58 = (f32[6,384]{1,0:T(8,128)S(1)}, bf16[6,384,2688]{1,2,0:T(8,128)(2,1)}) fusion(pred[6,2688]{1,0:T(8,128)(4,1)S(1)} %bitcast.87, bf16[2688,6,128]{0,2,1:T(8,128)(2,1)} %reshape.61, bf16[384,6,128]{0,2,1:T(8,128)(2,1)S(1)} %bitcast.85), kind=kOutput, calls=%fused_computation.61 | convolution fusion | flops 1622608512 | bytes 17130240 | tf_op jit(solution)/shard_map/sub | solution.py:31
  160.0 8.2 %fusion.41 = bf16[384,6,128]{0,2,1:T(8,128)(2,1)S(1)} fusion(bf16[2688,6,128]{0,2,1:T(8,128)(2,1)} %reshape.60, bf16[6,384,2688]{1,2,0:T(8,128)(2,1)} %get-tuple-element.18, f32[384,6]{0,1:T(8,128)S(1)} %bitcast.88), kind=kOutput, calls=%fused_computation.36 | convolution fusion | flops 1586036736 | bytes 17114112 | tf_op jit(solution)/shard_map/hqk,khd->qhd/dot_general | solution.py:34
  168.2 0.0 copy-done.3
  168.2 15.1 %fusion.59 = (f32[6,384]{1,0:T(8,128)S(1)}, bf16[6,384,2688]{1,2,0:T(8,128)(2,1)}) fusion(pred[6,2688]{1,0:T(8,128)(4,1)S(1)} %bitcast.86, bf16[2688,6,128]{0,2,1:T(8,128)(2,1)} %reshape.59, bf16[384,6,128]{0,2,1:T(8,128)(2,1)S(1)} %bitcast.84), kind=kOutput, calls=%fused_computation.62 | convolution fusion | flops 1622608512 | bytes 17130240 | tf_op jit(solution)/shard_map/sub | solution.py:31
  183.3 8.2 %fusion.38 = bf16[384,6,128]{0,2,1:T(8,128)(2,1)S(1)} fusion(bf16[2688,6,128]{0,2,1:T(8,128)(2,1)} %reshape.57, bf16[6,384,2688]{1,2,0:T(8,128)(2,1)} %get-tuple-element.20, f32[384,6]{0,1:T(8,128)S(1)} %bitcast.89), kind=kOutput, calls=%fused_computation.35 | convolution fusion | flops 1586036736 | bytes 17114112 | tf_op jit(solution)/shard_map/hqk,khd->qhd/dot_general | solution.py:34
  191.5 0.1 pad_maximum_fusion.4
  191.6 7.9 %convolution_convert_fusion = bf16[768,3072]{1,0:T(8,128)(2,1)} fusion(bf16[768,768]{0,1:T(8,128)(2,1)S(1)} %bitcast.83, bf16[768,3072]{1,0:T(8,128)(2,1)} %param.9), kind=kOutput, calls=%fused_computation.24 | convolution fusion | flops 3626237952 | bytes 10616832 | tf_op jit(solution)/shard_map/dot_general | solution.py:72
  199.5 0.0 reduce-scatter.2.cloned.1.call-update
  199.5 59.0 %reduce-scatter.2.cloned.1.call-done = bf16[768,768]{1,0:T(8,128)(2,1)} async-done(((bf16[768,3072]{1,0:T(8,128)(2,1)}), bf16[768,768]{1,0:T(8,128)(2,1)}) %reduce-scatter.2.cloned.1.call-update) | async-done | bytes 1179664 | tf_op jit(solution)/shard_map/reduce_scatter | solution.py:73
  (18 shorter events, 0.0 us)
Async XLA Ops:
  6.5 17.5 %copy-start = (bf16[768,768]{1,0:T(8,128)(2,1)S(1)}, bf16[768,768]{1,0:T(8,128)(2,1)}, u32[]{:S(2)}) copy-start(bf16[768,768]{1,0:T(8,128)(2,1)} %param.7) | copy-start | bytes 3538948
  6.5 31.4 %copy-start.1 = (bf16[768,768]{1,0:T(8,128)(2,1)S(1)}, bf16[768,768]{1,0:T(8,128)(2,1)}, u32[]{:S(2)}) copy-start(bf16[768,768]{1,0:T(8,128)(2,1)} %param.6) | copy-start | bytes 3538948
  6.5 24.1 %copy-start.7 = (s32[6]{0:T(128)S(1)}, s32[6]{0:T(128)}, u32[]{:S(2)}) copy-start(s32[6]{0:T(128)} %param.8) | copy-start | bytes 76
  6.5 252.0 %reduce-scatter.2.cloned.1.call-start = ((), (), s32[]{:S(2)}) async-start(), calls=%async_computation.1 | async-start | bytes 5898240 | tf_op jit(solution)/shard_map/reduce_scatter | solution.py:73
  10.3 71.3 %collective-permute-start.2 = (bf16[2,384,768]{1,0,2:T(2,128)(2,1)S(1)}, bf16[2,384,768]{1,0,2:T(2,128)(2,1)}, u32[]{:S(2)}, u32[]{:S(2)}) collective-permute-start(bf16[2,384,768]{1,0,2:T(2,128)(2,1)S(1)} %copy.14), channel_id=1, source_target_pairs={{1,0},{2,1},{3,2},{4,3},{5,4},{6,5},{7,6},{9,8},{10,9},{11,10},{12... | collective-permute-start | bytes 3538952 | tf_op jit(solution)/shard_map/ppermute | solution.py:13
  11.6 70.0 %collective-permute-start.1 = (bf16[2,384,768]{1,0,2:T(2,128)(2,1)S(1)}, bf16[2,384,768]{1,0,2:T(2,128)(2,1)}, u32[]{:S(2)}, u32[]{:S(2)}) collective-permute-start(bf16[2,384,768]{1,0,2:T(2,128)(2,1)S(1)} %copy.14), channel_id=1, source_target_pairs={{0,1},{1,2},{2,3},{3,4},{4,5},{5,6},{6,7},{8,9},{9,10},{10,11},{11... | collective-permute-start | bytes 3538952 | tf_op jit(solution)/shard_map/ppermute | solution.py:13
  18.0 18.0 %collective-permute-start.3 = (bf16[1,384,768]{2,1,0:T(8,128)(2,1)}, bf16[1,384,768]{2,1,0:T(8,128)(2,1)}, u32[]{:S(2)}, u32[]{:S(2)}) collective-permute-start(bf16[1,384,768]{2,1,0:T(8,128)(2,1)} %get-tuple-element.11), channel_id=1, source_target_pairs={{0,2},{1,3},{2,4},{3,5},{4,6},{5,7},{8,10},{9,11},{10,12},{11,13},... | collective-permute-start | bytes 1769480 | tf_op jit(solution)/shard_map/ppermute | solution.py:13
  22.8 19.4 %collective-permute-start.7 = (bf16[1,384,768]{2,1,0:T(8,128)(2,1)}, bf16[1,384,768]{2,1,0:T(8,128)(2,1)}, u32[]{:S(2)}, u32[]{:S(2)}) collective-permute-start(bf16[1,384,768]{2,1,0:T(8,128)(2,1)} %get-tuple-element.12), channel_id=1, source_target_pairs={{2,0},{3,1},{4,2},{5,3},{6,4},{7,5},{10,8},{11,9},{12,10},{13,11},... | collective-permute-start | bytes 1769480 | tf_op jit(solution)/shard_map/ppermute | solution.py:13
  25.2 23.4 %collective-permute-start = (bf16[1,384,768]{2,1,0:T(8,128)(2,1)}, bf16[1,384,768]{2,1,0:T(8,128)(2,1)}, u32[]{:S(2)}, u32[]{:S(2)}) collective-permute-start(bf16[1,384,768]{2,1,0:T(8,128)(2,1)} %get-tuple-element.13), channel_id=1, source_target_pairs={{0,2},{1,3},{2,4},{3,5},{4,6},{5,7},{8,10},{9,11},{10,12},{11,13},... | collective-permute-start | bytes 1769480 | tf_op jit(solution)/shard_map/ppermute | solution.py:13
  36.0 41.0 %collective-permute-start.6 = (bf16[1,384,768]{2,1,0:T(8,128)(2,1)}, bf16[1,384,768]{2,1,0:T(8,128)(2,1)}, u32[]{:S(2)}, u32[]{:S(2)}) collective-permute-start(bf16[1,384,768]{2,1,0:T(8,128)(2,1)} %get-tuple-element.14), channel_id=1, source_target_pairs={{2,0},{3,1},{4,2},{5,3},{6,4},{7,5},{10,8},{11,9},{12,10},{13,11},... | collective-permute-start | bytes 1769480 | tf_op jit(solution)/shard_map/ppermute | solution.py:13
  42.2 62.2 %collective-permute-start.5 = (bf16[2,384,768]{1,0,2:T(2,128)(2,1)S(1)}, bf16[2,384,768]{1,0,2:T(2,128)(2,1)}, u32[]{:S(2)}, u32[]{:S(2)}) collective-permute-start(bf16[2,384,768]{1,0,2:T(2,128)(2,1)S(1)} %copy.18), channel_id=1, source_target_pairs={{1,0},{2,1},{3,2},{4,3},{5,4},{6,5},{7,6},{9,8},{10,9},{11,10},{12... | collective-permute-start | bytes 3538952 | tf_op jit(solution)/shard_map/ppermute | solution.py:13
  48.6 55.8 %collective-permute-start.4 = (bf16[2,384,768]{1,0,2:T(2,128)(2,1)S(1)}, bf16[2,384,768]{1,0,2:T(2,128)(2,1)}, u32[]{:S(2)}, u32[]{:S(2)}) collective-permute-start(bf16[2,384,768]{1,0,2:T(2,128)(2,1)S(1)} %copy.18), channel_id=1, source_target_pairs={{0,1},{1,2},{2,3},{3,4},{4,5},{5,6},{6,7},{8,9},{9,10},{10,11},{11... | collective-permute-start | bytes 3538952 | tf_op jit(solution)/shard_map/ppermute | solution.py:13
  95.5 8.9 %copy-start.2 = (bf16[1,384,768]{1,0,2:T(2,128)(2,1)S(1)}, bf16[1,384,768]{1,0,2:T(2,128)(2,1)}, u32[]{:S(2)}) copy-start(bf16[1,384,768]{1,0,2:T(2,128)(2,1)} %copy.29) | copy-start | bytes 1769476
  135.8 8.9 %copy-start.4 = (bf16[384,768]{0,1:T(8,128)(2,1)S(1)}, bf16[384,768]{0,1:T(8,128)(2,1)}, u32[]{:S(2)}) copy-start(bf16[384,768]{0,1:T(8,128)(2,1)} %copy.41) | copy-start | bytes 1769476
  135.8 8.9 %copy-start.6 = (pred[1,6,7,384]{3,1,2,0:T(8,128)(4,1)S(1)}, pred[1,6,7,384]{3,1,2,0:T(8,128)(4,1)}, u32[]{:S(2)}) copy-start(pred[1,6,7,384]{3,1,2,0:T(8,128)(4,1)} %copy.43) | copy-start | bytes 48388
  160.0 8.3 %copy-start.3 = (bf16[384,768]{0,1:T(8,128)(2,1)S(1)}, bf16[384,768]{0,1:T(8,128)(2,1)}, u32[]{:S(2)}) copy-start(bf16[384,768]{0,1:T(8,128)(2,1)} %copy.40) | copy-start | bytes 1769476
  160.0 8.3 %copy-start.5 = (pred[1,6,7,384]{3,1,2,0:T(8,128)(4,1)S(1)}, pred[1,6,7,384]{3,1,2,0:T(8,128)(4,1)}, u32[]{:S(2)}) copy-start(pred[1,6,7,384]{3,1,2,0:T(8,128)(4,1)} %copy.42) | copy-start | bytes 48388
Sparse Core Ops, SparseCore 0:
  199.6 58.8 reduce-scatter.1
where the time goes:
time: 267 us; the launch traced here: 265 us
  waiting for transfers between devices  72.3 us (27%)
  local copies, waits for them, and re-layouts  67.6 us (25%)
  matrix products  54.6 us (20%)
  starting transfers between devices  29.5 us (11%)
  other arithmetic  27.8 us (10%)
  between operations  13.5 us (5%)
    reduce_scatter x1, waiting for transfers between devices, body(): lax.psum_scatter(terms.astype(jnp.bfloat16), 'head', scatter_dimension=1,...  59 us
    sub x2, matrix products, attend_frame(): weights = jnp.where(visible, jnp.exp(scores - rowmax), 0.0)  30.3 us
    ppermute x8, starting transfers between devices, from_behind(): lax.ppermute(value, axis, [(source, source + steps) for source in range(l...  29.5 us
    reshape x2, local copies, waits for them, and re-layouts, body(): value_window[local:local + 7].reshape(7 * FRAME_TOK, heads_here, HD)  17.8 us
    reshape x2, local copies, waits for them, and re-layouts, body(): key_window[local:local + 7].reshape(7 * FRAME_TOK, heads_here, HD)  17.6 us
    ppermute x4, local copies, waits for them, and re-layouts, from_behind(): lax.ppermute(value, axis, [(source, source + steps) for source in range(l...  17.4 us
    dot_general x2, matrix products, attend_frame(): jnp.einsum('hqk,khd->qhd', probs, value_rows, preferred_element_type=jnp....  16.4 us
    concatenate x1, other arithmetic, body(): jnp.concatenate([lower[1], received[1][1], value_local, received[-1][1],...  13.8 us
  transfers between devices with their start and end apart: 9, of which 4 were waited for; matrix products, arithmetic and copies ran while one was open for 19% of the time, Pallas kernels for 0%

commit v1 on v0

v1 whole, which is shorter than its diff:
```python
import jax
import jax.numpy as jnp
from jax import lax
from jax.experimental import pallas as pl
from jax.experimental.pallas import tpu as pltpu
from jax.sharding import PartitionSpec as P


HD = 128
FRAME_TOK = 384
LOG2E = 1.4426950408889634
F32 = jnp.float32
BF16 = jnp.bfloat16
VMEM_LIMIT = 16 << 20


def params():
    return pltpu.CompilerParams(vmem_limit_bytes=VMEM_LIMIT)


VMEM = pl.BlockSpec(memory_space=pltpu.VMEM)
SMEM = pl.BlockSpec(memory_space=pltpu.SMEM)
HBM = pl.BlockSpec(memory_space=pltpu.HBM)


def pack_frames(key_tok, value_tok):
    width = key_tok.shape[1]

    def kernel(key, value, out_e, out_i, sems):
        parity = lax.axis_index("frame") % 2
        copies = []
        for out, frame in ((out_e, parity), (out_i, 1 - parity)):
            for place, source in enumerate((key, value)):
                copies.append(
                    pltpu.make_async_copy(
                        source.at[pl.ds(pl.multiple_of(frame * FRAME_TOK, FRAME_TOK), FRAME_TOK)],
                        out.at[pl.ds(place * FRAME_TOK, FRAME_TOK)],
                        sems.at[len(copies)],
                    )
                )
        for copy in copies:
            copy.start()
        for copy in copies:
            copy.wait()

    shape = jax.ShapeDtypeStruct((2 * FRAME_TOK, width), BF16)
    return pl.pallas_call(
        kernel,
        out_shape=(shape, shape),
        in_specs=[HBM, HBM],
        out_specs=(VMEM, VMEM),
        scratch_shapes=[pltpu.SemaphoreType.DMA((4,))],
        compiler_params=params(),
        name="pack_frames",
    )(key_tok, value_tok)


def attend_step(table, query_tok, sources, roles, first, last):
    heads = query_tok.shape[1] // HD
    names = list(roles)
    scale = LOG2E / HD**0.5
    per_role = 1 if last else 3

    def kernel(table_ref, query, *refs):
        refs = list(refs)
        loaded = [refs.pop(0) for _ in sources]
        olds = {} if first else {role: [refs.pop(0) for _ in range(3)] for role in names}
        outs = {role: [refs.pop(0) for _ in range(per_role)] for role in names}
        parity = table_ref[0]
        starts = {"E": parity * FRAME_TOK, "I": (1 - parity) * FRAME_TOK}

        def one_head(head, carry):
            column = pl.ds(pl.multiple_of(head * HD, HD), HD)
            span = table_ref[3 + head]

            def emit(role, acc, total, top):
                if last:
                    outs[role][0][:, column] = (acc / total).astype(BF16)
                else:
                    outs[role][0][:, column] = acc
                    outs[role][1][:, column] = total
                    outs[role][2][:, column] = jnp.broadcast_to(top, (FRAME_TOK, HD))

            def update(role, picked):
                if not picked:
                    if last:
                        emit(role, *(ref[:, column] for ref in olds[role]))
                    return
                keys = jnp.concatenate([loaded[i][:FRAME_TOK, column] for i in picked], axis=0)
                values = jnp.concatenate([loaded[i][FRAME_TOK:, column] for i in picked], axis=0)
                values = jnp.concatenate([values, jnp.ones_like(values)], axis=1)
                rows = pl.ds(pl.multiple_of(starts[role], FRAME_TOK), FRAME_TOK)
                scores = lax.dot_general(
                    query[rows, column], keys, (((1,), (1,)), ((), ())), preferred_element_type=F32
                )
                top = jnp.max(scores, axis=1, keepdims=True)
                if not first:
                    old_acc, old_total, old_top = (ref[:, column] for ref in olds[role])
                    top = jnp.maximum(top, old_top[:, :1])
                weights = jnp.exp2((scores - top) * scale).astype(BF16)
                mixed = jnp.dot(weights, values, preferred_element_type=F32)
                acc, total = mixed[:, :HD], mixed[:, HD:]
                if not first:
                    fade = jnp.exp2((old_top - top) * scale)
                    acc = old_acc * fade + acc
                    total = old_total * fade + total
                emit(role, acc, total, top)

            if first:
                for limit in range(4):

                    def both(limit=limit):
                        for role in names:
                            update(role, [i for i, distance, _ in roles[role][1] if distance <= limit])

                    pl.when(span == limit)(both)
            else:
                for role in names:
                    entries = roles[role][1]
                    mask = sum(
                        jnp.where((span >= distance) & (table_ref[slot] > 0), 1 << bit, 0)
                        for bit, (_, distance, slot) in enumerate(entries)
                    )
                    for value in range(1 << len(entries)):
                        picked = [e[0] for bit, e in enumerate(entries) if value >> bit & 1]
                        if picked or last:
                            pl.when(mask == value)(lambda role=role, picked=picked: update(role, picked))
            return carry

        lax.fori_loop(0, heads, one_head, 0)

    operands = [table, query_tok, *sources]
    aliases = {}
    if not first:
        for index, role in enumerate(names):
            if not last:
                aliases.update({len(operands) + i: 3 * index + i for i in range(3)})
            operands += list(roles[role][0])
    shape = jax.ShapeDtypeStruct((FRAME_TOK, heads * HD), BF16 if last else F32)
    count = per_role * len(names)
    out = pl.pallas_call(
        kernel,
        out_shape=(shape,) * count,
        in_specs=[SMEM] + [VMEM] * (len(operands) - 1),
        out_specs=(VMEM,) * count,
        input_output_aliases=aliases,
        compiler_params=params(),
    )(*operands)
    return {role: out[i * per_role : (i + 1) * per_role] for i, role in enumerate(names)}


def project(attended, part, parts, out_weight, slots, received):
    groups = lax.axis_size("head")
    width = out_weight.shape[1] // groups
    rows = attended.shape[0] // parts

    def kernel(left, right, *rest):
        out = rest[-1]
        group = lax.axis_index("head")
        for index, slot in enumerate(slots):
            column = pl.ds(pl.multiple_of((group ^ slot) * width, width), width)
            sums = jnp.dot(
                left[part * rows : (part + 1) * rows, :], right[:, column], preferred_element_type=F32
            )
            for ref, (_, spots) in zip(rest, received):
                sums = sums + ref[:, spots[index] * width : (spots[index] + 1) * width].astype(F32)
            out[:, index * width : (index + 1) * width] = sums.astype(BF16)

    return pl.pallas_call(
        kernel,
        out_shape=jax.ShapeDtypeStruct((rows, len(slots) * width), BF16),
        in_specs=[VMEM] * (2 + len(received)),
        out_specs=VMEM,
        compiler_params=params(),
    )(attended, out_weight, *(array for array, _ in received))


def finish(attended, parts, out_weight, received, is_edge, frames_here, into):
    groups = lax.axis_size("head")
    width = out_weight.shape[1] // groups
    rows = FRAME_TOK // parts
    flat = [(array, spots[0], part) for part in range(parts) for array, spots in received[part]]

    def kernel(left, right, *rest):
        out, buffer, sems = rest[-3:]
        group = lax.axis_index("head")
        parity = lax.axis_index("frame") % 2
        frame = parity if is_edge else 1 - parity
        column = pl.ds(pl.multiple_of(group * width, width), width)
        copies = []
        for part in range(parts):
            span = slice(part * rows, (part + 1) * rows)
            sums = jnp.dot(left[span, :], right[:, column], preferred_element_type=F32)
            for ref, (_, spot, owner) in zip(rest, flat):
                if owner == part:
                    sums = sums + ref[:, spot * width : (spot + 1) * width].astype(F32)
            buffer[span, :] = sums.astype(BF16)
            copies.append(
                pltpu.make_async_copy(
                    buffer.at[pl.ds(part * rows, rows)],
                    out.at[pl.ds(pl.multiple_of(frame * FRAME_TOK + part * rows, rows), rows)],
                    sems.at[part],
                )
            )
            copies[-1].start()
        for copy in copies:
            copy.wait()

    operands = [attended, out_weight, *(array for array, _, _ in flat)]
    in_specs = [VMEM] * len(operands)
    aliases = {}
    if into is not None:
        aliases = {len(operands): 0}
        operands.append(into)
        in_specs.append(HBM)
    return pl.pallas_call(
        kernel,
        out_shape=jax.ShapeDtypeStruct((frames_here * FRAME_TOK, width), BF16),
        in_specs=in_specs,
        out_specs=HBM,
        scratch_shapes=[pltpu.VMEM((FRAME_TOK, width), BF16), pltpu.SemaphoreType.DMA((parts,))],
        input_output_aliases=aliases,
        compiler_params=params(),
    )(*operands)


def body(query_tok, key_tok, value_tok, head_span, out_weight):
    frames = lax.axis_size("frame")
    groups = lax.axis_size("head")
    local_frames = key_tok.shape[0] // FRAME_TOK
    bits = groups.bit_length() - 1
    assert local_frames == 2 and frames % 2 == 0 and groups == 1 << bits and FRAME_TOK % bits == 0
    seat = lax.axis_index("frame")
    parity = seat % 2
    link = jnp.where(parity == 0, seat > 0, seat < frames - 1)
    far_link = jnp.where(parity == 0, seat < frames - 2, seat > 1)
    table = jnp.concatenate(
        [jnp.stack([parity, link, far_link]).astype(jnp.int32), head_span.astype(jnp.int32)]
    )

    def swap(value):
        return lax.ppermute(value, "frame", [(i, i ^ 1) for i in range(frames)])

    def across(value):
        pairs = [(i, i + 1) for i in range(1, frames - 1, 2)]
        return lax.ppermute(value, "frame", pairs + [(b, a) for a, b in pairs])

    edge, inner = pack_frames(key_tok, value_tok)
    near = across(edge)
    partner_inner = swap(inner)
    partner_edge = swap(edge)
    second = across(inner)
    third = across(partner_inner)
    state = attend_step(
        table,
        query_tok,
        [edge, inner, partner_inner, partner_edge],
        {
            "E": (None, [(0, 0, None), (1, 1, None), (2, 2, None), (3, 3, None)]),
            "I": (None, [(1, 0, None), (0, 1, None), (2, 1, None), (3, 2, None)]),
        },
        True,
        False,
    )
    beyond = swap(near)
    state = attend_step(
        table,
        query_tok,
        [near, beyond],
        {"E": (state["E"], [(0, 1, 1)]), "I": (state["I"], [(0, 2, 1), (1, 3, 2)])},
        False,
        False,
    )
    attended = {}
    attended["I"] = attend_step(
        table, query_tok, [second], {"I": (state["I"], [(0, 3, 1)])}, False, True
    )["I"][0]

    def exchange(value, bit):
        return lax.ppermute(value, "head", [(i, i ^ (1 << bit)) for i in range(groups)])

    held = {role: [list(range(groups)) for _ in range(bits)] for role in "IE"}
    received = {role: [[] for _ in range(bits)] for role in "IE"}

    def gathered(role, part, slots):
        return [(array, [kept.index(s) for s in slots]) for array, kept in received[role][part]]

    def halve(role, stage):
        for part in range(bits):
            bit = (part + stage) % bits
            sent = [s for s in held[role][part] if s >> bit & 1]
            kept = [s for s in held[role][part] if not s >> bit & 1]
            terms = project(
                attended[role], part, bits, out_weight, sent, gathered(role, part, sent)
            )
            received[role][part].append((exchange(terms, bit), kept))
            held[role][part] = kept

    halve("I", 0)
    attended["E"] = attend_step(
        table, query_tok, [second, third], {"E": (state["E"], [(0, 2, 1), (1, 3, 1)])}, False, True
    )["E"][0]
    for stage in range(bits):
        halve("E", stage)
        if stage + 1 < bits:
            halve("I", stage + 1)
    result = None
    for role in "IE":
        result = finish(
            attended[role],
            bits,
            out_weight,
            [gathered(role, part, [0]) for part in range(bits)],
            role == "E",
            local_frames,
            result,
        )
    return result


def solution(mesh):
    return jax.shard_map(
        body,
        mesh=mesh,
        in_specs=(
            P("frame", "head"),
            P("frame", "head"),
            P("frame", "head"),
            P("head"),
            P("head", None),
        ),
        out_specs=P("frame", "head"),
        check_vma=False,
    )
```

time: 267 us -> 111 us (0.42)
  the two profiles are of different devices: /device:TPU:0 before, /device:TPU:20 now
where the time goes in v1:
time: 111 us; the launch traced here: 110 us
  waiting for transfers between devices  49.4 us (45%)
  Pallas kernels  42.7 us (38%)
  starting transfers between devices  15 us (14%)
  local copies, waits for them, and re-layouts  2.65 us (2%)
    ppermute x8, waiting for transfers between devices, exchange(): lax.ppermute(value, 'head', [(i, i ^ 1 << bit) for i in range(groups)])  35.3 us
    pallas_call x4, Pallas kernels, attend_step(): pl.pallas_call(kernel, out_shape=(shape,) * count, in_specs=[SMEM] + [VME...  34 us
    ppermute x3, waiting for transfers between devices, across(): return lax.ppermute(value, 'frame', pairs + [(b, a) for a, b in pairs])  14.1 us
    ppermute x3, starting transfers between devices, across(): return lax.ppermute(value, 'frame', pairs + [(b, a) for a, b in pairs])  7.47 us
    ppermute x8, starting transfers between devices, exchange(): lax.ppermute(value, 'head', [(i, i ^ 1 << bit) for i in range(groups)])  5.57 us
    pallas_call x8, Pallas kernels, project(): pl.pallas_call(kernel, out_shape=jax.ShapeDtypeStruct((rows, len(slots) *...  4.35 us
    pallas_call x2, Pallas kernels, finish(): pl.pallas_call(kernel, out_shape=jax.ShapeDtypeStruct((frames_here * FRAM...  2.89 us
    unnamed x12, local copies, waits for them, and re-layouts  2.65 us
  transfers between devices with their start and end apart: 14, of which 5 were waited for; matrix products, arithmetic and copies ran while one was open for 0% of the time, Pallas kernels for 30%

profile of v1, /device:TPU:20, one launch (start us, length us, event | category | flops | bytes accessed | tf_op | source)
XLA Modules:
  0.0 110.3 jit_solution(11814225457363946905)
XLA Ops:
  0.0 1.4 %copy-done.1 = bf16[768,768]{1,0:T(8,128)(2,1)S(1)} copy-done((bf16[768,768]{1,0:T(8,128)(2,1)S(1)}, bf16[768,768]{1,0:T(8,128)(2,1)}, u32[]{:S(2)}) %copy-start.1) | copy-done | bytes 1179672
  1.4 1.3 %copy-done.2 = bf16[768,768]{1,0:T(8,128)(2,1)S(1)} copy-done((bf16[768,768]{1,0:T(8,128)(2,1)S(1)}, bf16[768,768]{1,0:T(8,128)(2,1)}, u32[]{:S(2)}) %copy-start.2) | copy-done | bytes 1179672
  2.6 1.5 %pack_frames.1 = (bf16[768,768]{1,0:T(8,128)(2,1)}, bf16[768,768]{1,0:T(8,128)(2,1)S(1)}) custom-call(bf16[768,768]{1,0:T(8,128)(2,1)S(1)} %copy-done.1, bf16[768,768]{1,0:T(8,128)(2,1)S(1)} %copy-done.2), custom_call_target="tpu_custom_call" | custom-call | tf_op jit(solution)/shard_map/pack_frames/pallas_call | solution.py:47
  4.2 1.9 %collective-permute-start.3 = (bf16[768,768]{1,0:T(8,128)(2,1)}, bf16[768,768]{1,0:T(8,128)(2,1)}, u32[]{:S(2)}, u32[]{:S(2)}) collective-permute-start(bf16[768,768]{1,0:T(8,128)(2,1)} %get-tuple-element.20.refs_0_), channel_id=1, source_target_pairs={{1,2},{3,4},{5,6},{2,1},{4,3},{6,5},{9,10},{11,12},{13,14},{10,9},... | collective-permute-start | bytes 3538952 | tf_op jit(solution)/shard_map/ppermute | solution.py:246
  6.1 1.7 %collective-permute-start.1 = (bf16[768,768]{1,0:T(8,128)(2,1)S(1)}, bf16[768,768]{1,0:T(8,128)(2,1)}, u32[]{:S(2)}, u32[]{:S(2)}) collective-permute-start(bf16[768,768]{1,0:T(8,128)(2,1)S(1)} %get-tuple-element.19.refs_1_), channel_id=1, source_target_pairs={{0,1},{1,0},{2,3},{3,2},{4,5},{5,4},{6,7},{7,6},{8,9},{9,8},{10,11... | collective-permute-start | bytes 3538952 | tf_op jit(solution)/shard_map/ppermute | solution.py:242
  7.9 0.1 collective-permute-start.5
  7.9 14.1 %collective-permute-done.3.refs_0_ = bf16[768,768]{1,0:T(8,128)(2,1)} collective-permute-done((bf16[768,768]{1,0:T(8,128)(2,1)}, bf16[768,768]{1,0:T(8,128)(2,1)}, u32[]{:S(2)}, u32[]{:S(2)}) %collective-permute-start.3) | collective-permute-done | bytes 1179680 | tf_op jit(solution)/shard_map/ppermute | solution.py:246
  22.0 0.1 collective-permute-start.4
  22.1 2.3 %collective-permute-start = (bf16[768,768]{1,0:T(8,128)(2,1)S(1)}, bf16[768,768]{1,0:T(8,128)(2,1)S(1)}, u32[]{:S(2)}, u32[]{:S(2)}) collective-permute-start(bf16[768,768]{1,0:T(8,128)(2,1)S(1)} %get-tuple-element.19.refs_1_), channel_id=1, source_target_pairs={{1,2},{3,4},{5,6},{2,1},{4,3},{6,5},{9,10},{11,12},{13,14},{10,9},... | collective-permute-start | bytes 3538952 | tf_op jit(solution)/shard_map/ppermute | solution.py:246
  24.5 0.0 collective-permute-done.1.refs_2_
  24.5 3.2 %collective-permute-start.2 = (bf16[768,768]{1,0:T(8,128)(2,1)}, bf16[768,768]{1,0:T(8,128)(2,1)}, u32[]{:S(2)}, u32[]{:S(2)}) collective-permute-start(bf16[768,768]{1,0:T(8,128)(2,1)} %collective-permute-done.1.refs_2_), channel_id=1, source_target_pairs={{1,2},{3,4},{5,6},{2,1},{4,3},{6,5},{9,10},{11,12},{13,14},{10,9},... | collective-permute-start | bytes 3538952 | tf_op jit(solution)/shard_map/ppermute | solution.py:246
  27.7 0.0 copy-done.3
  27.8 0.1 pad_add_fusion.table_ref
  27.8 0.0 collective-permute-done.5.refs_3_
  27.8 14.6 %shard_map.55 = (f32[384,768]{1,0:T(8,128)S(1)}, f32[384,768]{1,0:T(8,128)S(1)}, f32[384,768]{1,0:T(8,128)S(1)}, f32[384,768]{1,0:T(8,128)S(1)}, f32[384,768]{1,0:T(8,128)S(1)}, /*index=5*/f32[384,768]{1,0:T(8,128)S(1)}) custom-call(s32[9]{0:T(128)S(1)} %pad_add_fusion.table_ref, bf16[768,768]{1,0:T(8,128)(2,1)S(1)} %copy-done, ...), custom_call_target="tpu_custom_call" | custom-call | tf_op jit(solution)/shard_map/pallas_call | solution.py:141
  42.4 0.0 collective-permute-done.4.refs_1_
  42.4 0.0 slice-start.1
  42.5 10.9 %shard_map.56 = (f32[384,768]{1,0:T(8,128)S(1)}, f32[384,768]{1,0:T(8,128)S(1)}, f32[384,768]{1,0:T(8,128)S(1)}, f32[384,768]{1,0:T(8,128)S(1)}, f32[384,768]{1,0:T(8,128)S(1)}, /*index=5*/f32[384,768]{1,0:T(8,128)S(1)}) custom-call(s32[9]{0:T(128)S(1)} %pad_add_fusion.table_ref, ...), custom_call_target="tpu_custom_call", output_to_operand_aliasing={{0}: (4, {}), {1}: (5, {}), {2}: (6, {}), {3}: (7, {}), {4}... | custom-call | tf_op jit(solution)/shard_map/pallas_call | solution.py:141
  53.4 0.0 collective-permute-done.refs_0_
  53.4 0.0 collective-permute-done.2.refs_1_
  53.4 6.0 %shard_map.57.left = bf16[384,768]{1,0:T(8,128)(2,1)S(1)} custom-call(s32[9]{0:T(128)S(1)} %pad_add_fusion.table_ref, bf16[768,768]{1,0:T(8,128)(2,1)S(1)} %copy-done, bf16[768,768]{1,0:T(8,128)(2,1)S(1)} %collective-permute-done.refs_0_, bf16[768,768]{1,0:T(8,128)(2,1)} %collective-permute-done.2.refs_1_, f32[384,768]{1,0:T(8,128)S(1)} %get-tuple-element.27.refs_2_, ...), custom_call_target="tpu_custom_call" | custom-call | tf_op jit(solution)/shard_map/pallas_call | solution.py:141
  59.4 0.7 shard_map.58
  60.1 0.3 collective-permute-start.6
  60.4 2.5 %shard_map.62.left = bf16[384,768]{1,0:T(8,128)(2,1)S(1)} custom-call(s32[9]{0:T(128)S(1)} %pad_add_fusion.table_ref, bf16[768,768]{1,0:T(8,128)(2,1)S(1)} %copy-done, bf16[768,768]{1,0:T(8,128)(2,1)S(1)} %collective-permute-done.refs_0_, f32[384,768]{1,0:T(8,128)S(1)} %get-tuple-element.30.refs_1_, f32[384,768]{1,0:T(8,128)S(1)} %get-tuple-element.31.refs_2_, ...), custom_call_target="tpu_custom_call" | custom-call | tf_op jit(solution)/shard_map/pallas_call | solution.py:141
  62.8 0.7 shard_map.63
  63.5 2.6 %collective-permute-start.10 = (bf16[192,1536]{1,0:T(8,128)(2,1)S(1)}, bf16[192,1536]{1,0:T(8,128)(2,1)S(1)}, u32[]{:S(2)}, u32[]{:S(2)}) collective-permute-start(bf16[192,1536]{1,0:T(8,128)(2,1)S(1)} %shard_map.63), channel_id=1, source_target_pairs={{0,8},{8,0},{16,24},{24,16},{1,9},{9,1},{17,25},{25,17},{2,10},{10... | collective-permute-start | bytes 1769480 | tf_op jit(solution)/shard_map/ppermute | solution.py:280
  66.1 0.6 shard_map.65
  66.8 0.1 collective-permute-start.12
  66.9 0.7 shard_map.60
  67.5 2.1 %collective-permute-start.8 = (bf16[192,1536]{1,0:T(8,128)(2,1)S(1)}, bf16[192,1536]{1,0:T(8,128)(2,1)S(1)}, u32[]{:S(2)}, u32[]{:S(2)}) collective-permute-start(bf16[192,1536]{1,0:T(8,128)(2,1)S(1)} %shard_map.60), channel_id=1, source_target_pairs={{0,16},{8,24},{16,0},{24,8},{1,17},{9,25},{17,1},{25,9},{2,18},{10... | collective-permute-start | bytes 1769480 | tf_op jit(solution)/shard_map/ppermute | solution.py:280
  69.6 6.8 %collective-permute-done.6.rest_0_ = bf16[192,1536]{1,0:T(8,128)(2,1)S(1)} collective-permute-done((bf16[192,1536]{1,0:T(8,128)(2,1)S(1)}, bf16[192,1536]{1,0:T(8,128)(2,1)S(1)}, u32[]{:S(2)}, u32[]{:S(2)}) %collective-permute-start.6) | collective-permute-done | bytes 589856 | tf_op jit(solution)/shard_map/ppermute | solution.py:280
  76.4 0.4 shard_map.59
  76.8 0.1 collective-permute-start.7
  76.9 11.6 %collective-permute-done.10.rest_0_ = bf16[192,1536]{1,0:T(8,128)(2,1)S(1)} collective-permute-done((bf16[192,1536]{1,0:T(8,128)(2,1)S(1)}, bf16[192,1536]{1,0:T(8,128)(2,1)S(1)}, u32[]{:S(2)}, u32[]{:S(2)}) %collective-permute-start.10) | collective-permute-done | bytes 589856 | tf_op jit(solution)/shard_map/ppermute | solution.py:280
  88.5 0.4 shard_map.64
  88.9 0.1 collective-permute-start.11
  89.0 0.0 collective-permute-done.12.rest_0_.rest_2_
  89.0 0.4 shard_map.66
  89.4 0.3 collective-permute-start.13
  89.7 5.9 %collective-permute-done.8.rest_0_.rest_2_ = bf16[192,1536]{1,0:T(8,128)(2,1)S(1)} collective-permute-done((bf16[192,1536]{1,0:T(8,128)(2,1)S(1)}, bf16[192,1536]{1,0:T(8,128)(2,1)S(1)}, u32[]{:S(2)}, u32[]{:S(2)}) %collective-permute-start.8) | collective-permute-done | bytes 589856 | tf_op jit(solution)/shard_map/ppermute | solution.py:280
  95.7 0.4 shard_map.61
  96.1 0.1 collective-permute-start.9
  96.2 11.0 %collective-permute-done.11.rest_1_ = bf16[192,768]{1,0:T(8,128)(2,1)S(1)} collective-permute-done((bf16[192,768]{1,0:T(8,128)(2,1)S(1)}, bf16[192,768]{1,0:T(8,128)(2,1)S(1)}, u32[]{:S(2)}, u32[]{:S(2)}) %collective-permute-start.11) | collective-permute-done | bytes 294944 | tf_op jit(solution)/shard_map/ppermute | solution.py:280
  107.2 0.0 collective-permute-done.13.rest_3_
  107.2 1.4 %shard_map.67.rest_4_ = bf16[768,768]{1,0:T(8,128)(2,1)} custom-call(bf16[384,768]{1,0:T(8,128)(2,1)S(1)} %shard_map.62.left, bf16[768,3072]{1,0:T(8,128)(2,1)S(1)} %bitcast.4, bf16[192,1536]{1,0:T(8,128)(2,1)S(1)} %collective-permute-done.10.rest_0_, bf16[192,768]{1,0:T(8,128)(2,1)S(1)} %collective-permute-done.11.rest_1_, ...), custom_call_target="tpu_custom_call" | custom-call | tf_op jit(solution)/shard_map/pallas_call | solution.py:216
  108.6 0.0 collective-permute-done.7.rest_1_
  108.6 0.0 collective-permute-done.9.rest_3_
  108.7 1.5 %shard_map.68 = bf16[768,768]{1,0:T(8,128)(2,1)} custom-call(bf16[384,768]{1,0:T(8,128)(2,1)S(1)} %shard_map.57.left, bf16[768,3072]{1,0:T(8,128)(2,1)S(1)} %bitcast.4, bf16[192,1536]{1,0:T(8,128)(2,1)S(1)} %collective-permute-done.6.rest_0_, bf16[192,768]{1,0:T(8,128)(2,1)S(1)} %collective-permute-done.7.rest_1_, ...), custom_call_target="tpu_custom_call", output_to_operand_aliasing={{}: (6, {})} | custom-call | tf_op jit(solution)/shard_map/pallas_call | solution.py:216
  (9 shorter events, 0.0 us)
Async XLA Ops:
  0.0 27.8 %copy-start = (bf16[768,768]{1,0:T(8,128)(2,1)S(1)}, bf16[768,768]{1,0:T(8,128)(2,1)}, u32[]{:S(2)}) copy-start(bf16[768,768]{1,0:T(8,128)(2,1)} %query.7) | copy-start | bytes 3538948
  0.0 1.4 %copy-start.1 = (bf16[768,768]{1,0:T(8,128)(2,1)S(1)}, bf16[768,768]{1,0:T(8,128)(2,1)}, u32[]{:S(2)}) copy-start(bf16[768,768]{1,0:T(8,128)(2,1)} %key.1) | copy-start | bytes 3538948
  1.4 1.3 %copy-start.2 = (bf16[768,768]{1,0:T(8,128)(2,1)S(1)}, bf16[768,768]{1,0:T(8,128)(2,1)}, u32[]{:S(2)}) copy-start(bf16[768,768]{1,0:T(8,128)(2,1)} %value.1) | copy-start | bytes 3538948
  2.6 25.1 %copy-start.3 = (s32[6]{0:T(128)S(1)}, s32[6]{0:T(128)}, u32[]{:S(2)}) copy-start(s32[6]{0:T(128)} %param.8) | copy-start | bytes 76
  4.2 17.8 %collective-permute-start.3 = (bf16[768,768]{1,0:T(8,128)(2,1)}, bf16[768,768]{1,0:T(8,128)(2,1)}, u32[]{:S(2)}, u32[]{:S(2)}) collective-permute-start(bf16[768,768]{1,0:T(8,128)(2,1)} %get-tuple-element.20.refs_0_), channel_id=1, source_target_pairs={{1,2},{3,4},{5,6},{2,1},{4,3},{6,5},{9,10},{11,12},{13,14},{10,9},... | collective-permute-start | bytes 3538952 | tf_op jit(solution)/shard_map/ppermute | solution.py:246
  6.1 18.4 %collective-permute-start.1 = (bf16[768,768]{1,0:T(8,128)(2,1)S(1)}, bf16[768,768]{1,0:T(8,128)(2,1)}, u32[]{:S(2)}, u32[]{:S(2)}) collective-permute-start(bf16[768,768]{1,0:T(8,128)(2,1)S(1)} %get-tuple-element.19.refs_1_), channel_id=1, source_target_pairs={{0,1},{1,0},{2,3},{3,2},{4,5},{5,4},{6,7},{7,6},{8,9},{9,8},{10,11... | collective-permute-start | bytes 3538952 | tf_op jit(solution)/shard_map/ppermute | solution.py:242
  7.9 20.0 %collective-permute-start.5 = (bf16[768,768]{1,0:T(8,128)(2,1)}, bf16[768,768]{1,0:T(8,128)(2,1)}, u32[]{:S(2)}, u32[]{:S(2)}) collective-permute-start(bf16[768,768]{1,0:T(8,128)(2,1)} %get-tuple-element.20.refs_0_), channel_id=1, source_target_pairs={{0,1},{1,0},{2,3},{3,2},{4,5},{5,4},{6,7},{7,6},{8,9},{9,8},{10,11... | collective-permute-start | bytes 3538952 | tf_op jit(solution)/shard_map/ppermute | solution.py:242
  22.0 20.4 %collective-permute-start.4 = (bf16[768,768]{1,0:T(8,128)(2,1)}, bf16[768,768]{1,0:T(8,128)(2,1)}, u32[]{:S(2)}, u32[]{:S(2)}) collective-permute-start(bf16[768,768]{1,0:T(8,128)(2,1)} %collective-permute-done.3.refs_0_), channel_id=1, source_target_pairs={{0,1},{1,0},{2,3},{3,2},{4,5},{5,4},{6,7},{7,6},{8,9},{9,8},{10,11... | collective-permute-start | bytes 3538952 | tf_op jit(solution)/shard_map/ppermute | solution.py:242
  22.1 31.2 %collective-permute-start = (bf16[768,768]{1,0:T(8,128)(2,1)S(1)}, bf16[768,768]{1,0:T(8,128)(2,1)S(1)}, u32[]{:S(2)}, u32[]{:S(2)}) collective-permute-start(bf16[768,768]{1,0:T(8,128)(2,1)S(1)} %get-tuple-element.19.refs_1_), channel_id=1, source_target_pairs={{1,2},{3,4},{5,6},{2,1},{4,3},{6,5},{9,10},{11,12},{13,14},{10,9},... | collective-permute-start | bytes 3538952 | tf_op jit(solution)/shard_map/ppermute | solution.py:246
  24.5 28.9 %collective-permute-start.2 = (bf16[768,768]{1,0:T(8,128)(2,1)}, bf16[768,768]{1,0:T(8,128)(2,1)}, u32[]{:S(2)}, u32[]{:S(2)}) collective-permute-start(bf16[768,768]{1,0:T(8,128)(2,1)} %collective-permute-done.1.refs_2_), channel_id=1, source_target_pairs={{1,2},{3,4},{5,6},{2,1},{4,3},{6,5},{9,10},{11,12},{13,14},{10,9},... | collective-permute-start | bytes 3538952 | tf_op jit(solution)/shard_map/ppermute | solution.py:246
  27.8 31.6 %slice-start = ((s8[4718592]{0:T(1024)(128)(4,1)}), s8[524288]{0:T(1024)(128)(4,1)S(1)}, s32[]{:S(2)}) async-start(s8[4718592]{0:T(1024)(128)(4,1)} %bitcast.3), calls=%async_computation | async-start | bytes 1048576
  42.4 17.0 %slice-start.1 = ((s8[4718592]{0:T(1024)(128)(4,1)}), s8[4194304]{0:T(1024)(128)(4,1)S(1)}, s32[]{:S(2)}) async-start(s8[4718592]{0:T(1024)(128)(4,1)} %bitcast.3), calls=%async_computation.1 | async-start | bytes 8388608
  60.1 16.3 %collective-permute-start.6 = (bf16[192,1536]{1,0:T(8,128)(2,1)S(1)}, bf16[192,1536]{1,0:T(8,128)(2,1)S(1)}, u32[]{:S(2)}, u32[]{:S(2)}) collective-permute-start(bf16[192,1536]{1,0:T(8,128)(2,1)S(1)} %shard_map.58), channel_id=1, source_target_pairs={{0,8},{8,0},{16,24},{24,16},{1,9},{9,1},{17,25},{25,17},{2,10},{10... | collective-permute-start | bytes 1769480 | tf_op jit(solution)/shard_map/ppermute | solution.py:280
  63.5 24.9 %collective-permute-start.10 = (bf16[192,1536]{1,0:T(8,128)(2,1)S(1)}, bf16[192,1536]{1,0:T(8,128)(2,1)S(1)}, u32[]{:S(2)}, u32[]{:S(2)}) collective-permute-start(bf16[192,1536]{1,0:T(8,128)(2,1)S(1)} %shard_map.63), channel_id=1, source_target_pairs={{0,8},{8,0},{16,24},{24,16},{1,9},{9,1},{17,25},{25,17},{2,10},{10... | collective-permute-start | bytes 1769480 | tf_op jit(solution)/shard_map/ppermute | solution.py:280
  66.8 22.2 %collective-permute-start.12 = (bf16[192,1536]{1,0:T(8,128)(2,1)S(1)}, bf16[192,1536]{1,0:T(8,128)(2,1)S(1)}, u32[]{:S(2)}, u32[]{:S(2)}) collective-permute-start(bf16[192,1536]{1,0:T(8,128)(2,1)S(1)} %shard_map.65), channel_id=1, source_target_pairs={{0,16},{8,24},{16,0},{24,8},{1,17},{9,25},{17,1},{25,9},{2,18},{10... | collective-permute-start | bytes 1769480 | tf_op jit(solution)/shard_map/ppermute | solution.py:280
  67.5 28.2 %collective-permute-start.8 = (bf16[192,1536]{1,0:T(8,128)(2,1)S(1)}, bf16[192,1536]{1,0:T(8,128)(2,1)S(1)}, u32[]{:S(2)}, u32[]{:S(2)}) collective-permute-start(bf16[192,1536]{1,0:T(8,128)(2,1)S(1)} %shard_map.60), channel_id=1, source_target_pairs={{0,16},{8,24},{16,0},{24,8},{1,17},{9,25},{17,1},{25,9},{2,18},{10... | collective-permute-start | bytes 1769480 | tf_op jit(solution)/shard_map/ppermute | solution.py:280
  76.8 31.8 %collective-permute-start.7 = (bf16[192,768]{1,0:T(8,128)(2,1)S(1)}, bf16[192,768]{1,0:T(8,128)(2,1)S(1)}, u32[]{:S(2)}, u32[]{:S(2)}) collective-permute-start(bf16[192,768]{1,0:T(8,128)(2,1)S(1)} %shard_map.59), channel_id=1, source_target_pairs={{0,16},{8,24},{16,0},{24,8},{1,17},{9,25},{17,1},{25,9},{2,18},{10... | collective-permute-start | bytes 884744 | tf_op jit(solution)/shard_map/ppermute | solution.py:280
  88.9 18.3 %collective-permute-start.11 = (bf16[192,768]{1,0:T(8,128)(2,1)S(1)}, bf16[192,768]{1,0:T(8,128)(2,1)S(1)}, u32[]{:S(2)}, u32[]{:S(2)}) collective-permute-start(bf16[192,768]{1,0:T(8,128)(2,1)S(1)} %shard_map.64), channel_id=1, source_target_pairs={{0,16},{8,24},{16,0},{24,8},{1,17},{9,25},{17,1},{25,9},{2,18},{10... | collective-permute-start | bytes 884744 | tf_op jit(solution)/shard_map/ppermute | solution.py:280
  89.4 17.8 %collective-permute-start.13 = (bf16[192,768]{1,0:T(8,128)(2,1)S(1)}, bf16[192,768]{1,0:T(8,128)(2,1)S(1)}, u32[]{:S(2)}, u32[]{:S(2)}) collective-permute-start(bf16[192,768]{1,0:T(8,128)(2,1)S(1)} %shard_map.66), channel_id=1, source_target_pairs={{0,8},{8,0},{16,24},{24,16},{1,9},{9,1},{17,25},{25,17},{2,10},{10... | collective-permute-start | bytes 884744 | tf_op jit(solution)/shard_map/ppermute | solution.py:280
  96.1 12.5 %collective-permute-start.9 = (bf16[192,768]{1,0:T(8,128)(2,1)S(1)}, bf16[192,768]{1,0:T(8,128)(2,1)S(1)}, u32[]{:S(2)}, u32[]{:S(2)}) collective-permute-start(bf16[192,768]{1,0:T(8,128)(2,1)S(1)} %shard_map.61), channel_id=1, source_target_pairs={{0,8},{8,0},{16,24},{24,16},{1,9},{9,1},{17,25},{25,17},{2,10},{10... | collective-permute-start | bytes 884744 | tf_op jit(solution)/shard_map/ppermute | solution.py:280

commit v2 on v1

--- a/solution.py
+++ b/solution.py
@@ -12,6 +12,8 @@
 F32 = jnp.float32
 BF16 = jnp.bfloat16
 VMEM_LIMIT = 16 << 20
+CHUNK = 384
+PAIRS = True
 
 
 def params():
@@ -24,110 +26,113 @@
 
 
 def pack_frames(key_tok, value_tok):
-    width = key_tok.shape[1]
-
-    def kernel(key, value, out_e, out_i, sems):
-        parity = lax.axis_index("frame") % 2
-        copies = []
-        for out, frame in ((out_e, parity), (out_i, 1 - parity)):
-            for place, source in enumerate((key, value)):
-                copies.append(
-                    pltpu.make_async_copy(
-                        source.at[pl.ds(pl.multiple_of(frame * FRAME_TOK, FRAME_TOK), FRAME_TOK)],
-                        out.at[pl.ds(place * FRAME_TOK, FRAME_TOK)],
-                        sems.at[len(copies)],
-                    )
-                )
-        for copy in copies:
-            copy.start()
-        for copy in copies:
-            copy.wait()
-
-    shape = jax.ShapeDtypeStruct((2 * FRAME_TOK, width), BF16)
-    return pl.pallas_call(
-        kernel,
-        out_shape=(shape, shape),
-        in_specs=[HBM, HBM],
-        out_specs=(VMEM, VMEM),
-        scratch_shapes=[pltpu.SemaphoreType.DMA((4,))],
-        compiler_params=params(),
-        name="pack_frames",
-    )(key_tok, value_tok)
-
-
-def attend_step(table, query_tok, sources, roles, first, last):
+    parity = lax.axis_index("frame") % 2
+
+    def packed(frame):
+        return jnp.concatenate(
+            [
+                lax.dynamic_slice_in_dim(array, frame * FRAME_TOK, FRAME_TOK, 0)
+                for array in (key_tok, value_tok)
+            ],
+            axis=0,
+        )
+
+    return packed(parity), packed(1 - parity)
+
+
+def attend_step(table, query_tok, sources, states, cases, first, last):
     heads = query_tok.shape[1] // HD
-    names = list(roles)
+    names = list(states)
     scale = LOG2E / HD**0.5
     per_role = 1 if last else 3
 
     def kernel(table_ref, query, *refs):
         refs = list(refs)
+        chosen = refs.pop()
         loaded = [refs.pop(0) for _ in sources]
         olds = {} if first else {role: [refs.pop(0) for _ in range(3)] for role in names}
         outs = {role: [refs.pop(0) for _ in range(per_role)] for role in names}
-        parity = table_ref[0]
+        parity, link, far_link = table_ref[0], table_ref[1] > 0, table_ref[2] > 0
         starts = {"E": parity * FRAME_TOK, "I": (1 - parity) * FRAME_TOK}
 
-        def one_head(head, carry):
-            column = pl.ds(pl.multiple_of(head * HD, HD), HD)
-            span = table_ref[3 + head]
-
-            def emit(role, acc, total, top):
-                if last:
-                    outs[role][0][:, column] = (acc / total).astype(BF16)
-                else:
-                    outs[role][0][:, column] = acc
-                    outs[role][1][:, column] = total
-                    outs[role][2][:, column] = jnp.broadcast_to(top, (FRAME_TOK, HD))
-
-            def update(role, picked):
-                if not picked:
-                    if last:
-                        emit(role, *(ref[:, column] for ref in olds[role]))
-                    return
-                keys = jnp.concatenate([loaded[i][:FRAME_TOK, column] for i in picked], axis=0)
-                values = jnp.concatenate([loaded[i][FRAME_TOK:, column] for i in picked], axis=0)
-                values = jnp.concatenate([values, jnp.ones_like(values)], axis=1)
-                rows = pl.ds(pl.multiple_of(starts[role], FRAME_TOK), FRAME_TOK)
+        def wide(tops, times):
+            return jnp.concatenate([tops] * times, axis=1)
+
+        def take(heads_now, items):
+            work = []
+            for head in heads_now:
+                column = pl.ds(pl.multiple_of(head * HD, HD), HD)
+                for role, picked in items:
+                    keys = jnp.concatenate([loaded[i][:FRAME_TOK, column] for i in picked], axis=0)
+                    values = jnp.concatenate([loaded[i][FRAME_TOK:, column] for i in picked], axis=0)
+                    values = jnp.concatenate([values, jnp.ones_like(values)], axis=1)
+                    for at in range(0, FRAME_TOK, CHUNK):
+                        work.append((role, column, slice(at, at + CHUNK), keys, values, len(picked)))
+            done = []
+            for role, column, rows, keys, values, count in work:
+                here = pl.ds(pl.multiple_of(starts[role] + rows.start, CHUNK), CHUNK)
                 scores = lax.dot_general(
-                    query[rows, column], keys, (((1,), (1,)), ((), ())), preferred_element_type=F32
+                    query[here, column], keys, (((1,), (1,)), ((), ())), preferred_element_type=F32
                 )
-                top = jnp.max(scores, axis=1, keepdims=True)
+                top = jnp.broadcast_to(jnp.max(scores, axis=1, keepdims=True), (CHUNK, HD))
+                fade = None
                 if not first:
-                    old_acc, old_total, old_top = (ref[:, column] for ref in olds[role])
-                    top = jnp.maximum(top, old_top[:, :1])
-                weights = jnp.exp2((scores - top) * scale).astype(BF16)
+                    old_top = olds[role][2][rows, column]
+                    top = jnp.maximum(top, old_top)
+                    fade = jnp.exp2((old_top - top) * scale)
+                times = count * FRAME_TOK // HD
+                weights = jnp.exp2((scores - wide(top, times)) * scale).astype(BF16)
                 mixed = jnp.dot(weights, values, preferred_element_type=F32)
+                done.append((role, column, rows, mixed, top, fade))
+            for role, column, rows, mixed, top, fade in done:
                 acc, total = mixed[:, :HD], mixed[:, HD:]
                 if not first:
-                    fade = jnp.exp2((old_top - top) * scale)
-                    acc = old_acc * fade + acc
-                    total = old_total * fade + total
-                emit(role, acc, total, top)
-
-            if first:
-                for limit in range(4):
-
-                    def both(limit=limit):
-                        for role in names:
-                            update(role, [i for i, distance, _ in roles[role][1] if distance <= limit])
-
-                    pl.when(span == limit)(both)
+                    acc = olds[role][0][rows, column] * fade + acc
+                    total = olds[role][1][rows, column] * fade + total
+                if last:
+                    outs[role][0][rows, column] = (acc / total).astype(BF16)
+                else:
+                    outs[role][0][rows, column] = acc
+                    outs[role][1][rows, column] = total
+                    outs[role][2][rows, column] = top
+
+        def close(head):
+            column = pl.ds(pl.multiple_of(head * HD, HD), HD)
+            for role in names:
+                outs[role][0][:, column] = (olds[role][0][:, column] / olds[role][1][:, column]).astype(BF16)
+
+        def collect(condition):
+            def add(head, count):
+                chosen[count] = head
+                return count + condition(table_ref[3 + head], link, far_link).astype(jnp.int32)
+
+            return lax.fori_loop(0, heads, add, jnp.int32(0))
+
+        for condition, items in cases:
+            count = collect(condition)
+            if items:
+                if PAIRS:
+
+                    def pair(step, carry, items=items):
+                        take((chosen[2 * step], chosen[2 * step + 1]), items)
+                        return carry
+
+                    lax.fori_loop(0, count // 2, pair, 0)
+                    pl.when(count % 2 == 1)(lambda items=items: take((chosen[count - 1],), items))
+                else:
+
+                    def single(step, carry, items=items):
+                        take((chosen[step],), items)
+                        return carry
+
+                    lax.fori_loop(0, count, single, 0)
             else:
-                for role in names:
-                    entries = roles[role][1]
-                    mask = sum(
-                        jnp.where((span >= distance) & (table_ref[slot] > 0), 1 << bit, 0)
-                        for bit, (_, distance, slot) in enumerate(entries)
-                    )
-                    for value in range(1 << len(entries)):
-                        picked = [e[0] for bit, e in enumerate(entries) if value >> bit & 1]
-                        if picked or last:
-                            pl.when(mask == value)(lambda role=role, picked=picked: update(role, picked))
-            return carry
-
-        lax.fori_loop(0, heads, one_head, 0)
+
+                def plain(step, carry):
+                    close(chosen[step])
+                    return carry
+
+                lax.fori_loop(0, count, plain, 0)
 
     operands = [table, query_tok, *sources]
     aliases = {}
@@ -135,7 +140,7 @@
         for index, role in enumerate(names):
             if not last:
                 aliases.update({len(operands) + i: 3 * index + i for i in range(3)})
-            operands += list(roles[role][0])
+            operands += list(states[role])
     shape = jax.ShapeDtypeStruct((FRAME_TOK, heads * HD), BF16 if last else F32)
     count = per_role * len(names)
     out = pl.pallas_call(
@@ -143,10 +148,56 @@
         out_shape=(shape,) * count,
         in_specs=[SMEM] + [VMEM] * (len(operands) - 1),
         out_specs=(VMEM,) * count,
+        scratch_shapes=[pltpu.SMEM((heads + 1,), jnp.int32)],
         input_output_aliases=aliases,
         compiler_params=params(),
     )(*operands)
     return {role: out[i * per_role : (i + 1) * per_role] for i, role in enumerate(names)}
+
+
+def attend_chip(table, query_tok, edge, inner, partner_inner, partner_edge):
+    order = {"E": [0, 1, 2, 3], "I": [1, 0, 2, 3]}
+    reach = {"E": [1, 2, 3, 4], "I": [1, 3, 4, 4]}
+    cases = [
+        (
+            lambda span, link, far_link, limit=limit: span == limit,
+            [(role, order[role][: reach[role][limit]]) for role in "EI"],
+        )
+        for limit in range(4)
+    ]
+    return attend_step(
+        table, query_tok, [edge, inner, partner_inner, partner_edge], {"E": None, "I": None}, cases, True, False
+    )
+
+
+def attend_near(table, query_tok, state, near, beyond):
+    cases = [
+        (lambda span, link, far_link: (span >= 3) & link & far_link, [("E", [0]), ("I", [0, 1])]),
+        (
+            lambda span, link, far_link: link & ((span == 2) | ((span >= 3) & jnp.logical_not(far_link))),
+            [("E", [0]), ("I", [0])],
+        ),
+        (lambda span, link, far_link: (span == 1) & link, [("E", [0])]),
+        (lambda span, link, far_link: (span >= 3) & jnp.logical_not(link) & far_link, [("I", [1])]),
+    ]
+    return attend_step(table, query_tok, [near, beyond], state, cases, False, False)
+
+
+def attend_inner(table, query_tok, state, second):
+    cases = [
+        (lambda span, link, far_link: (span >= 3) & link, [("I", [0])]),
+        (lambda span, link, far_link: (span < 3) | jnp.logical_not(link), []),
+    ]
+    return attend_step(table, query_tok, [second], state, cases, False, True)["I"][0]
+
+
+def attend_edge(table, query_tok, state, second, third):
+    cases = [
+        (lambda span, link, far_link: (span >= 3) & link, [("E", [0, 1])]),
+        (lambda span, link, far_link: (span == 2) & link, [("E", [0])]),
+        (lambda span, link, far_link: (span < 2) | jnp.logical_not(link), []),
+    ]
+    return attend_step(table, query_tok, [second, third], state, cases, False, True)["E"][0]
 
 
 def project(attended, part, parts, out_weight, slots, received):
@@ -251,30 +302,10 @@
     partner_edge = swap(edge)
     second = across(inner)
     third = across(partner_inner)
-    state = attend_step(
-        table,
-        query_tok,
-        [edge, inner, partner_inner, partner_edge],
-        {
-            "E": (None, [(0, 0, None), (1, 1, None), (2, 2, None), (3, 3, None)]),
-            "I": (None, [(1, 0, None), (0, 1, None), (2, 1, None), (3, 2, None)]),
-        },
-        True,
-        False,
-    )
+    state = attend_chip(table, query_tok, edge, inner, partner_inner, partner_edge)
     beyond = swap(near)
-    state = attend_step(
-        table,
-        query_tok,
-        [near, beyond],
-        {"E": (state["E"], [(0, 1, 1)]), "I": (state["I"], [(0, 2, 1), (1, 3, 2)])},
-        False,
-        False,
-    )
-    attended = {}
-    attended["I"] = attend_step(
-        table, query_tok, [second], {"I": (state["I"], [(0, 3, 1)])}, False, True
-    )["I"][0]
+    state = attend_near(table, query_tok, state, near, beyond)
+    attended = {"I": attend_inner(table, query_tok, {"I": state["I"]}, second)}
 
     def exchange(value, bit):
         return lax.ppermute(value, "head", [(i, i ^ (1 << bit)) for i in range(groups)])
@@ -290,16 +321,12 @@
             bit = (part + stage) % bits
             sent = [s for s in held[role][part] if s >> bit & 1]
             kept = [s for s in held[role][part] if not s >> bit & 1]
-            terms = project(
-                attended[role], part, bits, out_weight, sent, gathered(role, part, sent)
-            )
+            terms = project(attended[role], part, bits, out_weight, sent, gathered(role, part, sent))
             received[role][part].append((exchange(terms, bit), kept))
             held[role][part] = kept
 
     halve("I", 0)
-    attended["E"] = attend_step(
-        table, query_tok, [second, third], {"E": (state["E"], [(0, 2, 1), (1, 3, 1)])}, False, True
-    )["E"][0]
+    attended["E"] = attend_edge(table, query_tok, {"E": state["E"]}, second, third)
     for stage in range(bits):
         halve("E", stage)
         if stage + 1 < bits:

time: 111 us -> 105 us (0.946)
  Pallas kernels: 42.7 us -> 34.4 us
  starting transfers between devices: 15 us -> 17.2 us
  waiting for transfers between devices: 49.4 us -> 51.1 us
    pallas_call x4, Pallas kernels: 34 us -> 27.2 us  [attend_step(): pl.pallas_call(kernel, out_shape=(shape,) * count, in_specs=[SMEM] + [VME...]
    ppermute x3, waiting for transfers between devices: 14.1 us -> 18.1 us  [across(): return lax.ppermute(value, 'frame', pairs + [(b, a) for a, b in pairs])]
    unnamed x12 -> x8, local copies, waits for them, and re-layouts: 2.65 us -> 0.02 us
    ppermute x8, waiting for transfers between devices: 35.3 us -> 32.9 us  [exchange(): lax.ppermute(value, 'head', [(i, i ^ 1 << bit) for i in range(groups)])]
    ppermute x8, starting transfers between devices: 5.57 us -> 7.81 us  [exchange(): lax.ppermute(value, 'head', [(i, i ^ 1 << bit) for i in range(groups)])]
    dynamic_slice x0 -> x1, local copies, waits for them, and re-layouts: none -> 1.75 us  [packed(): lax.dynamic_slice_in_dim(array, frame * FRAME_TOK, FRAME_TOK, 0)]
    pallas_call x1 -> x0, Pallas kernels: 1.53 us -> none  [pack_frames(): pl.pallas_call(kernel, out_shape=(shape, shape), in_specs=[HBM, HBM], out...]
  transfers between devices with their start and end apart: 14 -> 14, of which waited for: 5 -> 6; matrix products, arithmetic and copies ran while one was open for 0% -> 0% of each run, Pallas kernels for 30% -> 26%
where the time goes in v2:
time: 105 us
  waiting for transfers between devices  51.1 us (49%)
  Pallas kernels  34.4 us (33%)
  starting transfers between devices  17.2 us (16%)
  local copies, waits for them, and re-layouts  1.77 us (2%)
    ppermute x8, waiting for transfers between devices, exchange(): lax.ppermute(value, 'head', [(i, i ^ 1 << bit) for i in range(groups)])  32.9 us
    pallas_call x4, Pallas kernels, attend_step(): pl.pallas_call(kernel, out_shape=(shape,) * count, in_specs=[SMEM] + [VME...  27.2 us
    ppermute x3, waiting for transfers between devices, across(): return lax.ppermute(value, 'frame', pairs + [(b, a) for a, b in pairs])  18.1 us
    ppermute x8, starting transfers between devices, exchange(): lax.ppermute(value, 'head', [(i, i ^ 1 << bit) for i in range(groups)])  7.81 us
    ppermute x3, starting transfers between devices, across(): return lax.ppermute(value, 'frame', pairs + [(b, a) for a, b in pairs])  7.47 us
    pallas_call x8, Pallas kernels, project(): pl.pallas_call(kernel, out_shape=jax.ShapeDtypeStruct((rows, len(slots) *...  4.33 us
    pallas_call x2, Pallas kernels, finish(): pl.pallas_call(kernel, out_shape=jax.ShapeDtypeStruct((frames_here * FRAM...  2.88 us
  transfers between devices with their start and end apart: 14, of which 6 were waited for; matrix products, arithmetic and copies ran while one was open for 0% of the time, Pallas kernels for 26%

profile of v2, /device:TPU:20, one launch (start us, length us, event | category | flops | bytes accessed | tf_op | source)
XLA Modules:
  0.0 105.2 jit_solution(3889084606075927198)
XLA Ops:
  0.0 1.8 %constant_dynamic-slice_fusion = (bf16[384,768]{1,0:T(8,128)(2,1)S(1)}, bf16[384,768]{1,0:T(8,128)(2,1)S(1)}, bf16[384,768]{1,0:T(8,128)(2,1)S(1)}, bf16[384,768]{1,0:T(8,128)(2,1)S(1)}) fusion(bf16[768,768]{1,0:T(8,128)(2,1)} %param.7, s32[]{:T(128)S(6)} %select_n.28, s32[]{:T(128)S(6)} %select_n.27, bf16[768,768]{1,0:T(8,128)(2,1)} %param.6), kind=kLoop, calls=%fused_computation.2 | loop fusion | bytes 4718600 | tf_op jit(solution)/shard_map/dynamic_slice | solution.py:34
  1.8 0.1 pad_maximum_fusion.1.refs_0_
  1.8 1.9 %collective-permute-start.3 = (bf16[768,768]{1,0:T(8,128)(2,1)S(1)}, bf16[768,768]{1,0:T(8,128)(2,1)}, u32[]{:S(2)}, u32[]{:S(2)}) collective-permute-start(bf16[768,768]{1,0:T(8,128)(2,1)S(1)} %pad_maximum_fusion.1.refs_0_), channel_id=1, source_target_pairs={{1,2},{3,4},{5,6},{2,1},{4,3},{6,5},{9,10},{11,12},{13,14},{10,9},... | collective-permute-start | bytes 3538952 | tf_op jit(solution)/shard_map/ppermute | solution.py:297
  3.8 0.0 copy-start.1
  3.8 0.0 copy-start
  3.8 0.1 pad_maximum_fusion.refs_1_
  3.9 1.7 %collective-permute-start.1 = (bf16[768,768]{1,0:T(8,128)(2,1)S(1)}, bf16[768,768]{1,0:T(8,128)(2,1)}, u32[]{:S(2)}, u32[]{:S(2)}) collective-permute-start(bf16[768,768]{1,0:T(8,128)(2,1)S(1)} %pad_maximum_fusion.refs_1_), channel_id=1, source_target_pairs={{0,1},{1,0},{2,3},{3,2},{4,5},{5,4},{6,7},{7,6},{8,9},{9,8},{10,11... | collective-permute-start | bytes 3538952 | tf_op jit(solution)/shard_map/ppermute | solution.py:293
  5.6 0.1 collective-permute-start.5
  5.7 13.8 %collective-permute-done.3.refs_0_ = bf16[768,768]{1,0:T(8,128)(2,1)} collective-permute-done((bf16[768,768]{1,0:T(8,128)(2,1)S(1)}, bf16[768,768]{1,0:T(8,128)(2,1)}, u32[]{:S(2)}, u32[]{:S(2)}) %collective-permute-start.3) | collective-permute-done | bytes 1179680 | tf_op jit(solution)/shard_map/ppermute | solution.py:297
  19.5 0.1 collective-permute-start.4
  19.6 2.3 %collective-permute-start = (bf16[768,768]{1,0:T(8,128)(2,1)S(1)}, bf16[768,768]{1,0:T(8,128)(2,1)}, u32[]{:S(2)}, u32[]{:S(2)}) collective-permute-start(bf16[768,768]{1,0:T(8,128)(2,1)S(1)} %pad_maximum_fusion.refs_1_), channel_id=1, source_target_pairs={{1,2},{3,4},{5,6},{2,1},{4,3},{6,5},{9,10},{11,12},{13,14},{10,9},... | collective-permute-start | bytes 3538952 | tf_op jit(solution)/shard_map/ppermute | solution.py:297
  21.9 0.0 collective-permute-done.1.refs_2_
  21.9 3.2 %collective-permute-start.2 = (bf16[768,768]{1,0:T(8,128)(2,1)}, bf16[768,768]{1,0:T(8,128)(2,1)}, u32[]{:S(2)}, u32[]{:S(2)}) collective-permute-start(bf16[768,768]{1,0:T(8,128)(2,1)} %collective-permute-done.1.refs_2_), channel_id=1, source_target_pairs={{1,2},{3,4},{5,6},{2,1},{4,3},{6,5},{9,10},{11,12},{13,14},{10,9},... | collective-permute-start | bytes 3538952 | tf_op jit(solution)/shard_map/ppermute | solution.py:297
  25.2 0.1 pad_add_fusion.table_ref
  25.3 0.0 collective-permute-done.5.refs_3_
  25.3 13.3 %shard_map.55 = (f32[384,768]{1,0:T(8,128)S(1)}, f32[384,768]{1,0:T(8,128)S(1)}, f32[384,768]{1,0:T(8,128)S(1)}, f32[384,768]{1,0:T(8,128)S(1)}, f32[384,768]{1,0:T(8,128)S(1)}, /*index=5*/f32[384,768]{1,0:T(8,128)S(1)}) custom-call(s32[9]{0:T(128)S(1)} %pad_add_fusion.table_ref, bf16[768,768]{1,0:T(8,128)(2,1)S(1)} %copy-done, ...), custom_call_target="tpu_custom_call" | custom-call | tf_op jit(solution)/shard_map/pallas_call | solution.py:146
  38.5 0.0 collective-permute-done.4.refs_1_
  38.6 0.0 slice-start.1
  38.6 6.9 %shard_map.56 = (f32[384,768]{1,0:T(8,128)S(1)}, f32[384,768]{1,0:T(8,128)S(1)}, f32[384,768]{1,0:T(8,128)S(1)}, f32[384,768]{1,0:T(8,128)S(1)}, f32[384,768]{1,0:T(8,128)S(1)}, /*index=5*/f32[384,768]{1,0:T(8,128)S(1)}) custom-call(s32[9]{0:T(128)S(1)} %pad_add_fusion.table_ref, ...), custom_call_target="tpu_custom_call", output_to_operand_aliasing={{0}: (4, {}), {1}: (5, {}), {2}: (6, {}), {3}: (7, {}), {4}... | custom-call | tf_op jit(solution)/shard_map/pallas_call | solution.py:146
  45.5 0.0 collective-permute-done.refs_0_
  45.5 4.4 %collective-permute-done.2.refs_1_ = bf16[768,768]{1,0:T(8,128)(2,1)} collective-permute-done((bf16[768,768]{1,0:T(8,128)(2,1)}, bf16[768,768]{1,0:T(8,128)(2,1)}, u32[]{:S(2)}, u32[]{:S(2)}) %collective-permute-start.2) | collective-permute-done | bytes 1179680 | tf_op jit(solution)/shard_map/ppermute | solution.py:297
  49.8 4.7 %shard_map.57.left = bf16[384,768]{1,0:T(8,128)(2,1)S(1)} custom-call(s32[9]{0:T(128)S(1)} %pad_add_fusion.table_ref, bf16[768,768]{1,0:T(8,128)(2,1)S(1)} %copy-done, bf16[768,768]{1,0:T(8,128)(2,1)} %collective-permute-done.refs_0_, bf16[768,768]{1,0:T(8,128)(2,1)} %collective-permute-done.2.refs_1_, f32[384,768]{1,0:T(8,128)S(1)} %get-tuple-element.23.refs_2_, ...), custom_call_target="tpu_custom_call" | custom-call | tf_op jit(solution)/shard_map/pallas_call | solution.py:146
  54.6 0.7 shard_map.58
  55.3 1.7 %collective-permute-start.6 = (bf16[192,1536]{1,0:T(8,128)(2,1)S(1)}, bf16[192,1536]{1,0:T(8,128)(2,1)S(1)}, u32[]{:S(2)}, u32[]{:S(2)}) collective-permute-start(bf16[192,1536]{1,0:T(8,128)(2,1)S(1)} %shard_map.58), channel_id=1, source_target_pairs={{0,8},{8,0},{16,24},{24,16},{1,9},{9,1},{17,25},{25,17},{2,10},{10... | collective-permute-start | bytes 1769480 | tf_op jit(solution)/shard_map/ppermute | solution.py:311
  57.0 2.4 %shard_map.62.left = bf16[384,768]{1,0:T(8,128)(2,1)S(1)} custom-call(s32[9]{0:T(128)S(1)} %pad_add_fusion.table_ref, bf16[768,768]{1,0:T(8,128)(2,1)S(1)} %copy-done, bf16[768,768]{1,0:T(8,128)(2,1)} %collective-permute-done.refs_0_, f32[384,768]{1,0:T(8,128)S(1)} %get-tuple-element.26.refs_1_, f32[384,768]{1,0:T(8,128)S(1)} %get-tuple-element.27.refs_2_, ...), custom_call_target="tpu_custom_call" | custom-call | tf_op jit(solution)/shard_map/pallas_call | solution.py:146
  59.4 0.7 shard_map.63
  60.0 1.0 collective-permute-start.10
  61.0 0.6 shard_map.65
  61.7 0.1 collective-permute-start.12
  61.8 0.7 shard_map.60
  62.4 2.1 %collective-permute-start.8 = (bf16[192,1536]{1,0:T(8,128)(2,1)S(1)}, bf16[192,1536]{1,0:T(8,128)(2,1)S(1)}, u32[]{:S(2)}, u32[]{:S(2)}) collective-permute-start(bf16[192,1536]{1,0:T(8,128)(2,1)S(1)} %shard_map.60), channel_id=1, source_target_pairs={{0,16},{8,24},{16,0},{24,8},{1,17},{9,25},{17,1},{25,9},{2,18},{10... | collective-permute-start | bytes 1769480 | tf_op jit(solution)/shard_map/ppermute | solution.py:311
  64.5 7.0 %collective-permute-done.6.rest_0_ = bf16[192,1536]{1,0:T(8,128)(2,1)S(1)} collective-permute-done((bf16[192,1536]{1,0:T(8,128)(2,1)S(1)}, bf16[192,1536]{1,0:T(8,128)(2,1)S(1)}, u32[]{:S(2)}, u32[]{:S(2)}) %collective-permute-start.6) | collective-permute-done | bytes 589856 | tf_op jit(solution)/shard_map/ppermute | solution.py:311
  71.5 0.4 shard_map.59
  72.0 0.1 collective-permute-start.7
  72.0 11.6 %collective-permute-done.10.rest_0_ = bf16[192,1536]{1,0:T(8,128)(2,1)S(1)} collective-permute-done((bf16[192,1536]{1,0:T(8,128)(2,1)S(1)}, bf16[192,1536]{1,0:T(8,128)(2,1)S(1)}, u32[]{:S(2)}, u32[]{:S(2)}) %collective-permute-start.10) | collective-permute-done | bytes 589856 | tf_op jit(solution)/shard_map/ppermute | solution.py:311
  83.6 0.4 shard_map.64
  84.0 0.1 collective-permute-start.11
  84.1 0.0 collective-permute-done.12.rest_0_.rest_2_
  84.1 0.4 shard_map.66
  84.6 1.7 %collective-permute-start.13 = (bf16[192,768]{1,0:T(8,128)(2,1)S(1)}, bf16[192,768]{1,0:T(8,128)(2,1)S(1)}, u32[]{:S(2)}, u32[]{:S(2)}) collective-permute-start(bf16[192,768]{1,0:T(8,128)(2,1)S(1)} %shard_map.66), channel_id=1, source_target_pairs={{0,8},{8,0},{16,24},{24,16},{1,9},{9,1},{17,25},{25,17},{2,10},{10... | collective-permute-start | bytes 884744 | tf_op jit(solution)/shard_map/ppermute | solution.py:311
  86.2 4.4 %collective-permute-done.8.rest_0_.rest_2_ = bf16[192,1536]{1,0:T(8,128)(2,1)S(1)} collective-permute-done((bf16[192,1536]{1,0:T(8,128)(2,1)S(1)}, bf16[192,1536]{1,0:T(8,128)(2,1)S(1)}, u32[]{:S(2)}, u32[]{:S(2)}) %collective-permute-start.8) | collective-permute-done | bytes 589856 | tf_op jit(solution)/shard_map/ppermute | solution.py:311
  90.6 0.4 shard_map.61
  91.0 1.1 %collective-permute-start.9 = (bf16[192,768]{1,0:T(8,128)(2,1)S(1)}, bf16[192,768]{1,0:T(8,128)(2,1)S(1)}, u32[]{:S(2)}, u32[]{:S(2)}) collective-permute-start(bf16[192,768]{1,0:T(8,128)(2,1)S(1)} %shard_map.61), channel_id=1, source_target_pairs={{0,8},{8,0},{16,24},{24,16},{1,9},{9,1},{17,25},{25,17},{2,10},{10... | collective-permute-start | bytes 884744 | tf_op jit(solution)/shard_map/ppermute | solution.py:311
  92.2 9.9 %collective-permute-done.11.rest_1_ = bf16[192,768]{1,0:T(8,128)(2,1)S(1)} collective-permute-done((bf16[192,768]{1,0:T(8,128)(2,1)S(1)}, bf16[192,768]{1,0:T(8,128)(2,1)S(1)}, u32[]{:S(2)}, u32[]{:S(2)}) %collective-permute-start.11) | collective-permute-done | bytes 294944 | tf_op jit(solution)/shard_map/ppermute | solution.py:311
  102.1 0.0 collective-permute-done.13.rest_3_
  102.1 1.4 %shard_map.67.rest_4_ = bf16[768,768]{1,0:T(8,128)(2,1)} custom-call(bf16[384,768]{1,0:T(8,128)(2,1)S(1)} %shard_map.62.left, bf16[768,3072]{1,0:T(8,128)(2,1)S(1)} %bitcast.4, bf16[192,1536]{1,0:T(8,128)(2,1)S(1)} %collective-permute-done.10.rest_0_, bf16[192,768]{1,0:T(8,128)(2,1)S(1)} %collective-permute-done.11.rest_1_, ...), custom_call_target="tpu_custom_call" | custom-call | tf_op jit(solution)/shard_map/pallas_call | solution.py:267
  103.6 0.0 collective-permute-done.9.rest_3_
  103.6 1.4 %shard_map.68 = bf16[768,768]{1,0:T(8,128)(2,1)} custom-call(bf16[384,768]{1,0:T(8,128)(2,1)S(1)} %shard_map.57.left, bf16[768,3072]{1,0:T(8,128)(2,1)S(1)} %bitcast.4, bf16[192,1536]{1,0:T(8,128)(2,1)S(1)} %collective-permute-done.6.rest_0_, bf16[192,768]{1,0:T(8,128)(2,1)S(1)} %collective-permute-done.7.rest_1_, ...), custom_call_target="tpu_custom_call", output_to_operand_aliasing={{}: (6, {})} | custom-call | tf_op jit(solution)/shard_map/pallas_call | solution.py:267
  (7 shorter events, 0.0 us)
Async XLA Ops:
  1.8 17.6 %collective-permute-start.3 = (bf16[768,768]{1,0:T(8,128)(2,1)S(1)}, bf16[768,768]{1,0:T(8,128)(2,1)}, u32[]{:S(2)}, u32[]{:S(2)}) collective-permute-start(bf16[768,768]{1,0:T(8,128)(2,1)S(1)} %pad_maximum_fusion.1.refs_0_), channel_id=1, source_target_pairs={{1,2},{3,4},{5,6},{2,1},{4,3},{6,5},{9,10},{11,12},{13,14},{10,9},... | collective-permute-start | bytes 3538952 | tf_op jit(solution)/shard_map/ppermute | solution.py:297
  3.8 21.4 %copy-start.1 = (s32[6]{0:T(128)S(1)}, s32[6]{0:T(128)}, u32[]{:S(2)}) copy-start(s32[6]{0:T(128)} %param.8) | copy-start | bytes 76
  3.8 21.5 %copy-start = (bf16[768,768]{1,0:T(8,128)(2,1)S(1)}, bf16[768,768]{1,0:T(8,128)(2,1)}, u32[]{:S(2)}) copy-start(bf16[768,768]{1,0:T(8,128)(2,1)} %query.7) | copy-start | bytes 3538948
  3.9 18.1 %collective-permute-start.1 = (bf16[768,768]{1,0:T(8,128)(2,1)S(1)}, bf16[768,768]{1,0:T(8,128)(2,1)}, u32[]{:S(2)}, u32[]{:S(2)}) collective-permute-start(bf16[768,768]{1,0:T(8,128)(2,1)S(1)} %pad_maximum_fusion.refs_1_), channel_id=1, source_target_pairs={{0,1},{1,0},{2,3},{3,2},{4,5},{5,4},{6,7},{7,6},{8,9},{9,8},{10,11... | collective-permute-start | bytes 3538952 | tf_op jit(solution)/shard_map/ppermute | solution.py:293
  5.6 19.6 %collective-permute-start.5 = (bf16[768,768]{1,0:T(8,128)(2,1)S(1)}, bf16[768,768]{1,0:T(8,128)(2,1)}, u32[]{:S(2)}, u32[]{:S(2)}) collective-permute-start(bf16[768,768]{1,0:T(8,128)(2,1)S(1)} %pad_maximum_fusion.1.refs_0_), channel_id=1, source_target_pairs={{0,1},{1,0},{2,3},{3,2},{4,5},{5,4},{6,7},{7,6},{8,9},{9,8},{10,11... | collective-permute-start | bytes 3538952 | tf_op jit(solution)/shard_map/ppermute | solution.py:293
  19.5 19.1 %collective-permute-start.4 = (bf16[768,768]{1,0:T(8,128)(2,1)}, bf16[768,768]{1,0:T(8,128)(2,1)}, u32[]{:S(2)}, u32[]{:S(2)}) collective-permute-start(bf16[768,768]{1,0:T(8,128)(2,1)} %collective-permute-done.3.refs_0_), channel_id=1, source_target_pairs={{0,1},{1,0},{2,3},{3,2},{4,5},{5,4},{6,7},{7,6},{8,9},{9,8},{10,11... | collective-permute-start | bytes 3538952 | tf_op jit(solution)/shard_map/ppermute | solution.py:293
  19.6 25.9 %collective-permute-start = (bf16[768,768]{1,0:T(8,128)(2,1)S(1)}, bf16[768,768]{1,0:T(8,128)(2,1)}, u32[]{:S(2)}, u32[]{:S(2)}) collective-permute-start(bf16[768,768]{1,0:T(8,128)(2,1)S(1)} %pad_maximum_fusion.refs_1_), channel_id=1, source_target_pairs={{1,2},{3,4},{5,6},{2,1},{4,3},{6,5},{9,10},{11,12},{13,14},{10,9},... | collective-permute-start | bytes 3538952 | tf_op jit(solution)/shard_map/ppermute | solution.py:297
  21.9 27.9 %collective-permute-start.2 = (bf16[768,768]{1,0:T(8,128)(2,1)}, bf16[768,768]{1,0:T(8,128)(2,1)}, u32[]{:S(2)}, u32[]{:S(2)}) collective-permute-start(bf16[768,768]{1,0:T(8,128)(2,1)} %collective-permute-done.1.refs_2_), channel_id=1, source_target_pairs={{1,2},{3,4},{5,6},{2,1},{4,3},{6,5},{9,10},{11,12},{13,14},{10,9},... | collective-permute-start | bytes 3538952 | tf_op jit(solution)/shard_map/ppermute | solution.py:297
  25.3 29.3 %slice-start = ((s8[4718592]{0:T(1024)(128)(4,1)}), s8[524288]{0:T(1024)(128)(4,1)S(1)}, s32[]{:S(2)}) async-start(s8[4718592]{0:T(1024)(128)(4,1)} %bitcast.3), calls=%async_computation | async-start | bytes 1048576
  38.6 16.0 %slice-start.1 = ((s8[4718592]{0:T(1024)(128)(4,1)}), s8[4194304]{0:T(1024)(128)(4,1)S(1)}, s32[]{:S(2)}) async-start(s8[4718592]{0:T(1024)(128)(4,1)} %bitcast.3), calls=%async_computation.1 | async-start | bytes 8388608
  55.3 16.3 %collective-permute-start.6 = (bf16[192,1536]{1,0:T(8,128)(2,1)S(1)}, bf16[192,1536]{1,0:T(8,128)(2,1)S(1)}, u32[]{:S(2)}, u32[]{:S(2)}) collective-permute-start(bf16[192,1536]{1,0:T(8,128)(2,1)S(1)} %shard_map.58), channel_id=1, source_target_pairs={{0,8},{8,0},{16,24},{24,16},{1,9},{9,1},{17,25},{25,17},{2,10},{10... | collective-permute-start | bytes 1769480 | tf_op jit(solution)/shard_map/ppermute | solution.py:311
  60.0 23.6 %collective-permute-start.10 = (bf16[192,1536]{1,0:T(8,128)(2,1)S(1)}, bf16[192,1536]{1,0:T(8,128)(2,1)S(1)}, u32[]{:S(2)}, u32[]{:S(2)}) collective-permute-start(bf16[192,1536]{1,0:T(8,128)(2,1)S(1)} %shard_map.63), channel_id=1, source_target_pairs={{0,8},{8,0},{16,24},{24,16},{1,9},{9,1},{17,25},{25,17},{2,10},{10... | collective-permute-start | bytes 1769480 | tf_op jit(solution)/shard_map/ppermute | solution.py:311
  61.7 22.4 %collective-permute-start.12 = (bf16[192,1536]{1,0:T(8,128)(2,1)S(1)}, bf16[192,1536]{1,0:T(8,128)(2,1)S(1)}, u32[]{:S(2)}, u32[]{:S(2)}) collective-permute-start(bf16[192,1536]{1,0:T(8,128)(2,1)S(1)} %shard_map.65), channel_id=1, source_target_pairs={{0,16},{8,24},{16,0},{24,8},{1,17},{9,25},{17,1},{25,9},{2,18},{10... | collective-permute-start | bytes 1769480 | tf_op jit(solution)/shard_map/ppermute | solution.py:311
  62.4 28.2 %collective-permute-start.8 = (bf16[192,1536]{1,0:T(8,128)(2,1)S(1)}, bf16[192,1536]{1,0:T(8,128)(2,1)S(1)}, u32[]{:S(2)}, u32[]{:S(2)}) collective-permute-start(bf16[192,1536]{1,0:T(8,128)(2,1)S(1)} %shard_map.60), channel_id=1, source_target_pairs={{0,16},{8,24},{16,0},{24,8},{1,17},{9,25},{17,1},{25,9},{2,18},{10... | collective-permute-start | bytes 1769480 | tf_op jit(solution)/shard_map/ppermute | solution.py:311
  72.0 31.6 %collective-permute-start.7 = (bf16[192,768]{1,0:T(8,128)(2,1)S(1)}, bf16[192,768]{1,0:T(8,128)(2,1)S(1)}, u32[]{:S(2)}, u32[]{:S(2)}) collective-permute-start(bf16[192,768]{1,0:T(8,128)(2,1)S(1)} %shard_map.59), channel_id=1, source_target_pairs={{0,16},{8,24},{16,0},{24,8},{1,17},{9,25},{17,1},{25,9},{2,18},{10... | collective-permute-start | bytes 884744 | tf_op jit(solution)/shard_map/ppermute | solution.py:311
  84.0 18.1 %collective-permute-start.11 = (bf16[192,768]{1,0:T(8,128)(2,1)S(1)}, bf16[192,768]{1,0:T(8,128)(2,1)S(1)}, u32[]{:S(2)}, u32[]{:S(2)}) collective-permute-start(bf16[192,768]{1,0:T(8,128)(2,1)S(1)} %shard_map.64), channel_id=1, source_target_pairs={{0,16},{8,24},{16,0},{24,8},{1,17},{9,25},{17,1},{25,9},{2,18},{10... | collective-permute-start | bytes 884744 | tf_op jit(solution)/shard_map/ppermute | solution.py:311
  84.6 17.5 %collective-permute-start.13 = (bf16[192,768]{1,0:T(8,128)(2,1)S(1)}, bf16[192,768]{1,0:T(8,128)(2,1)S(1)}, u32[]{:S(2)}, u32[]{:S(2)}) collective-permute-start(bf16[192,768]{1,0:T(8,128)(2,1)S(1)} %shard_map.66), channel_id=1, source_target_pairs={{0,8},{8,0},{16,24},{24,16},{1,9},{9,1},{17,25},{25,17},{2,10},{10... | collective-permute-start | bytes 884744 | tf_op jit(solution)/shard_map/ppermute | solution.py:311
  91.0 12.5 %collective-permute-start.9 = (bf16[192,768]{1,0:T(8,128)(2,1)S(1)}, bf16[192,768]{1,0:T(8,128)(2,1)S(1)}, u32[]{:S(2)}, u32[]{:S(2)}) collective-permute-start(bf16[192,768]{1,0:T(8,128)(2,1)S(1)} %shard_map.61), channel_id=1, source_target_pairs={{0,8},{8,0},{16,24},{24,16},{1,9},{9,1},{17,25},{25,17},{2,10},{10... | collective-permute-start | bytes 884744 | tf_op jit(solution)/shard_map/ppermute | solution.py:311

commit v3 on v2

--- a/solution.py
+++ b/solution.py
@@ -13,7 +13,6 @@
 BF16 = jnp.bfloat16
 VMEM_LIMIT = 16 << 20
 CHUNK = 384
-PAIRS = True
 
 
 def params():
@@ -40,25 +39,31 @@
     return packed(parity), packed(1 - parity)
 
 
-def attend_step(table, query_tok, sources, states, cases, first, last):
+def attend_step(table, query_tok, sources, states, cases, first=False, closed=None):
     heads = query_tok.shape[1] // HD
     names = list(states)
+    closed = closed or {}
     scale = LOG2E / HD**0.5
-    per_role = 1 if last else 3
+    keep = first or any(items and not close for _, items, close in cases)
 
     def kernel(table_ref, query, *refs):
         refs = list(refs)
         chosen = refs.pop()
         loaded = [refs.pop(0) for _ in sources]
         olds = {} if first else {role: [refs.pop(0) for _ in range(3)] for role in names}
-        outs = {role: [refs.pop(0) for _ in range(per_role)] for role in names}
+        for role in closed:
+            if closed[role] is not None:
+                refs.pop(0)
+        outs = {role: [refs.pop(0) for _ in range(3)] for role in names} if keep else {}
+        results = {role: refs.pop(0) for role in closed}
+        reads = outs if keep and not first else olds
         parity, link, far_link = table_ref[0], table_ref[1] > 0, table_ref[2] > 0
         starts = {"E": parity * FRAME_TOK, "I": (1 - parity) * FRAME_TOK}
 
         def wide(tops, times):
             return jnp.concatenate([tops] * times, axis=1)
 
-        def take(heads_now, items):
+        def take(heads_now, items, close):
             work = []
             for head in heads_now:
                 column = pl.ds(pl.multiple_of(head * HD, HD), HD)
@@ -77,7 +82,7 @@
                 top = jnp.broadcast_to(jnp.max(scores, axis=1, keepdims=True), (CHUNK, HD))
                 fade = None
                 if not first:
-                    old_top = olds[role][2][rows, column]
+                    old_top = reads[role][2][rows, column]
                     top = jnp.maximum(top, old_top)
                     fade = jnp.exp2((old_top - top) * scale)
                 times = count * FRAME_TOK // HD
@@ -87,19 +92,20 @@
             for role, column, rows, mixed, top, fade in done:
                 acc, total = mixed[:, :HD], mixed[:, HD:]
                 if not first:
-                    acc = olds[role][0][rows, column] * fade + acc
-                    total = olds[role][1][rows, column] * fade + total
-                if last:
-                    outs[role][0][rows, column] = (acc / total).astype(BF16)
+                    acc = reads[role][0][rows, column] * fade + acc
+                    total = reads[role][1][rows, column] * fade + total
+                if role in close:
+                    results[role][rows, column] = (acc / total).astype(BF16)
                 else:
                     outs[role][0][rows, column] = acc
                     outs[role][1][rows, column] = total
                     outs[role][2][rows, column] = top
 
-        def close(head):
+        def finish_head(head, roles):
             column = pl.ds(pl.multiple_of(head * HD, HD), HD)
-            for role in names:
-                outs[role][0][:, column] = (olds[role][0][:, column] / olds[role][1][:, column]).astype(BF16)
+            for role in roles:
+                acc, total = reads[role][0][:, column], reads[role][1][:, column]
+                results[role][:, column] = (acc / total).astype(BF16)
 
         def collect(condition):
             def add(head, count):
@@ -108,51 +114,54 @@
 
             return lax.fori_loop(0, heads, add, jnp.int32(0))
 
-        for condition, items in cases:
+        for condition, items, close in cases:
             count = collect(condition)
             if items:
-                if PAIRS:
-
-                    def pair(step, carry, items=items):
-                        take((chosen[2 * step], chosen[2 * step + 1]), items)
-                        return carry
-
-                    lax.fori_loop(0, count // 2, pair, 0)
-                    pl.when(count % 2 == 1)(lambda items=items: take((chosen[count - 1],), items))
-                else:
-
-                    def single(step, carry, items=items):
-                        take((chosen[step],), items)
-                        return carry
-
-                    lax.fori_loop(0, count, single, 0)
+
+                def pair(step, carry, items=items, close=close):
+                    take((chosen[2 * step], chosen[2 * step + 1]), items, close)
+                    return carry
+
+                lax.fori_loop(0, count // 2, pair, 0)
+                pl.when(count % 2 == 1)(
+                    lambda items=items, close=close, count=count: take((chosen[count - 1],), items, close)
+                )
             else:
 
-                def plain(step, carry):
-                    close(chosen[step])
+                def plain(step, carry, close=close):
+                    finish_head(chosen[step], close)
                     return carry
 
                 lax.fori_loop(0, count, plain, 0)
 
     operands = [table, query_tok, *sources]
+    shapes = []
     aliases = {}
     if not first:
         for index, role in enumerate(names):
-            if not last:
+            if keep:
                 aliases.update({len(operands) + i: 3 * index + i for i in range(3)})
             operands += list(states[role])
-    shape = jax.ShapeDtypeStruct((FRAME_TOK, heads * HD), BF16 if last else F32)
-    count = per_role * len(names)
-    out = pl.pallas_call(
-        kernel,
-        out_shape=(shape,) * count,
-        in_specs=[SMEM] + [VMEM] * (len(operands) - 1),
-        out_specs=(VMEM,) * count,
-        scratch_shapes=[pltpu.SMEM((heads + 1,), jnp.int32)],
-        input_output_aliases=aliases,
-        compiler_params=params(),
-    )(*operands)
-    return {role: out[i * per_role : (i + 1) * per_role] for i, role in enumerate(names)}
+    if keep:
+        shapes += [jax.ShapeDtypeStruct((FRAME_TOK, heads * HD), F32)] * (3 * len(names))
+    for role in closed:
+        if closed[role] is not None:
+            aliases[len(operands)] = len(shapes)
+            operands.append(closed[role])
+        shapes.append(jax.ShapeDtypeStruct((FRAME_TOK, heads * HD), BF16))
+    out = list(
+        pl.pallas_call(
+            kernel,
+            out_shape=tuple(shapes),
+            in_specs=[SMEM] + [VMEM] * (len(operands) - 1),
+            out_specs=(VMEM,) * len(shapes),
+            scratch_shapes=[pltpu.SMEM((heads + 1,), jnp.int32)],
+            input_output_aliases=aliases,
+            compiler_params=params(),
+        )(*operands)
+    )
+    new_states = {role: [out.pop(0) for _ in range(3)] for role in names} if keep else {}
+    return new_states, {role: out.pop(0) for role in closed}
 
 
 def attend_chip(table, query_tok, edge, inner, partner_inner, partner_edge):
@@ -162,42 +171,43 @@
         (
             lambda span, link, far_link, limit=limit: span == limit,
             [(role, order[role][: reach[role][limit]]) for role in "EI"],
+            "",
         )
         for limit in range(4)
     ]
     return attend_step(
-        table, query_tok, [edge, inner, partner_inner, partner_edge], {"E": None, "I": None}, cases, True, False
-    )
-
-
-def attend_near(table, query_tok, state, near, beyond):
+        table, query_tok, [edge, inner, partner_inner, partner_edge], {"E": None, "I": None}, cases, first=True
+    )[0]
+
+
+def attend_near(table, query_tok, state, near):
     cases = [
-        (lambda span, link, far_link: (span >= 3) & link & far_link, [("E", [0]), ("I", [0, 1])]),
-        (
-            lambda span, link, far_link: link & ((span == 2) | ((span >= 3) & jnp.logical_not(far_link))),
-            [("E", [0]), ("I", [0])],
-        ),
-        (lambda span, link, far_link: (span == 1) & link, [("E", [0])]),
-        (lambda span, link, far_link: (span >= 3) & jnp.logical_not(link) & far_link, [("I", [1])]),
+        (lambda span, link, far_link: (span >= 2) & link, [("E", [0]), ("I", [0])], ""),
+        (lambda span, link, far_link: (span == 1) & link, [("E", [0])], ""),
     ]
-    return attend_step(table, query_tok, [near, beyond], state, cases, False, False)
-
-
-def attend_inner(table, query_tok, state, second):
+    return attend_step(table, query_tok, [near], state, cases)[0]
+
+
+def attend_beyond(table, query_tok, state, beyond):
     cases = [
-        (lambda span, link, far_link: (span >= 3) & link, [("I", [0])]),
-        (lambda span, link, far_link: (span < 3) | jnp.logical_not(link), []),
+        (lambda span, link, far_link: (span >= 3) & far_link, [("I", [0])], ""),
+        (lambda span, link, far_link: (span < 3) | jnp.logical_not(link), [], "I"),
+        (lambda span, link, far_link: (span < 2) | jnp.logical_not(link), [], "E"),
     ]
-    return attend_step(table, query_tok, [second], state, cases, False, True)["I"][0]
-
-
-def attend_edge(table, query_tok, state, second, third):
+    return attend_step(table, query_tok, [beyond], state, cases, closed={"I": None, "E": None})
+
+
+def attend_inner(table, query_tok, state, second, result):
+    cases = [(lambda span, link, far_link: (span >= 3) & link, [("I", [0])], "I")]
+    return attend_step(table, query_tok, [second], {"I": state}, cases, closed={"I": result})[1]["I"]
+
+
+def attend_edge(table, query_tok, state, second, third, result):
     cases = [
-        (lambda span, link, far_link: (span >= 3) & link, [("E", [0, 1])]),
-        (lambda span, link, far_link: (span == 2) & link, [("E", [0])]),
-        (lambda span, link, far_link: (span < 2) | jnp.logical_not(link), []),
+        (lambda span, link, far_link: (span >= 3) & link, [("E", [0, 1])], "E"),
+        (lambda span, link, far_link: (span == 2) & link, [("E", [0])], "E"),
     ]
-    return attend_step(table, query_tok, [second, third], state, cases, False, True)["E"][0]
+    return attend_step(table, query_tok, [second, third], {"E": state}, cases, closed={"E": result})[1]["E"]
 
 
 def project(attended, part, parts, out_weight, slots, received):
@@ -304,8 +314,9 @@
     third = across(partner_inner)
     state = attend_chip(table, query_tok, edge, inner, partner_inner, partner_edge)
     beyond = swap(near)
-    state = attend_near(table, query_tok, state, near, beyond)
-    attended = {"I": attend_inner(table, query_tok, {"I": state["I"]}, second)}
+    state = attend_near(table, query_tok, state, near)
+    state, attended = attend_beyond(table, query_tok, state, beyond)
+    attended["I"] = attend_inner(table, query_tok, state["I"], second, attended["I"])
 
     def exchange(value, bit):
         return lax.ppermute(value, "head", [(i, i ^ (1 << bit)) for i in range(groups)])
@@ -326,7 +337,7 @@
             held[role][part] = kept
 
     halve("I", 0)
-    attended["E"] = attend_edge(table, query_tok, {"E": state["E"]}, second, third)
+    attended["E"] = attend_edge(table, query_tok, state["E"], second, third, attended["E"])
     for stage in range(bits):
         halve("E", stage)
         if stage + 1 < bits:

time: 105 us -> 105 us (level)
  waiting for transfers between devices: 51.1 us -> 49.6 us
    ppermute x3, waiting for transfers between devices: 18.1 us -> 16.6 us  [across(): return lax.ppermute(value, 'frame', pairs + [(b, a) for a, b in pairs])]
    pallas_call x4 -> x5, Pallas kernels: 27.2 us -> 27.6 us  [attend_step(): pl.pallas_call(kernel, out_shape=tuple(shapes), in_specs=[SMEM] + [VMEM]...]
  transfers between devices with their start and end apart: 14 -> 14, of which waited for: 6 -> 6; matrix products, arithmetic and copies ran while one was open for 0% -> 0% of each run, Pallas kernels for 26% -> 27%
where the time goes in v3:
time: 105 us
  waiting for transfers between devices  49.6 us (47%)
  Pallas kernels  34.8 us (33%)
  starting transfers between devices  17.2 us (16%)
  local copies, waits for them, and re-layouts  1.78 us (2%)
  other arithmetic  1.25 us (1%)
    ppermute x8, waiting for transfers between devices, exchange(): lax.ppermute(value, 'head', [(i, i ^ 1 << bit) for i in range(groups)])  33 us
    pallas_call x5, Pallas kernels, attend_step(): pl.pallas_call(kernel, out_shape=tuple(shapes), in_specs=[SMEM] + [VMEM]...  27.6 us
    ppermute x3, waiting for transfers between devices, across(): return lax.ppermute(value, 'frame', pairs + [(b, a) for a, b in pairs])  16.6 us
    ppermute x8, starting transfers between devices, exchange(): lax.ppermute(value, 'head', [(i, i ^ 1 << bit) for i in range(groups)])  7.78 us
    ppermute x3, starting transfers between devices, across(): return lax.ppermute(value, 'frame', pairs + [(b, a) for a, b in pairs])  7.46 us
    pallas_call x8, Pallas kernels, project(): pl.pallas_call(kernel, out_shape=jax.ShapeDtypeStruct((rows, len(slots) *...  4.33 us
    pallas_call x2, Pallas kernels, finish(): pl.pallas_call(kernel, out_shape=jax.ShapeDtypeStruct((frames_here * FRAM...  2.91 us
  transfers between devices with their start and end apart: 14, of which 6 were waited for; matrix products, arithmetic and copies ran while one was open for 0% of the time, Pallas kernels for 27%

profile of v3, /device:TPU:20, one launch (start us, length us, event | category | flops | bytes accessed | tf_op | source)
XLA Modules:
  0.0 105.1 jit_solution(8192191298307522903)
XLA Ops:
  0.0 1.8 %constant_dynamic-slice_fusion = (bf16[384,768]{1,0:T(8,128)(2,1)S(1)}, bf16[384,768]{1,0:T(8,128)(2,1)S(1)}, bf16[384,768]{1,0:T(8,128)(2,1)S(1)}, bf16[384,768]{1,0:T(8,128)(2,1)S(1)}) fusion(bf16[768,768]{1,0:T(8,128)(2,1)} %param.7, s32[]{:T(128)S(6)} %select_n.28, s32[]{:T(128)S(6)} %select_n.27, bf16[768,768]{1,0:T(8,128)(2,1)} %param.6), kind=kLoop, calls=%fused_computation.2 | loop fusion | bytes 4718600 | tf_op jit(solution)/shard_map/dynamic_slice | solution.py:33
  1.8 1.1 %pad_maximum_fusion.1.refs_0_ = bf16[768,768]{1,0:T(8,128)(2,1)} fusion(bf16[384,768]{1,0:T(8,128)(2,1)S(1)} %get-tuple-element.47, bf16[384,768]{1,0:T(8,128)(2,1)S(1)} %get-tuple-element.50), kind=kLoop, calls=%fused_computation.1 | loop fusion | flops 2359296 | bytes 2359296 | tf_op jit(solution)/shard_map/concatenate | solution.py:31
  2.8 1.9 %collective-permute-start.3 = (bf16[768,768]{1,0:T(8,128)(2,1)}, bf16[768,768]{1,0:T(8,128)(2,1)}, u32[]{:S(2)}, u32[]{:S(2)}) collective-permute-start(bf16[768,768]{1,0:T(8,128)(2,1)} %pad_maximum_fusion.1.refs_0_), channel_id=1, source_target_pairs={{1,2},{3,4},{5,6},{2,1},{4,3},{6,5},{9,10},{11,12},{13,14},{10,9},... | collective-permute-start | bytes 3538952 | tf_op jit(solution)/shard_map/ppermute | solution.py:307
  4.8 0.0 copy-start.1
  4.8 0.0 copy-start
  4.8 0.1 pad_maximum_fusion.refs_1_
  4.9 1.7 %collective-permute-start.1 = (bf16[768,768]{1,0:T(8,128)(2,1)S(1)}, bf16[768,768]{1,0:T(8,128)(2,1)}, u32[]{:S(2)}, u32[]{:S(2)}) collective-permute-start(bf16[768,768]{1,0:T(8,128)(2,1)S(1)} %pad_maximum_fusion.refs_1_), channel_id=1, source_target_pairs={{0,1},{1,0},{2,3},{3,2},{4,5},{5,4},{6,7},{7,6},{8,9},{9,8},{10,11... | collective-permute-start | bytes 3538952 | tf_op jit(solution)/shard_map/ppermute | solution.py:303
  6.6 0.1 collective-permute-start.5
  6.7 14.0 %collective-permute-done.3.refs_0_ = bf16[768,768]{1,0:T(8,128)(2,1)} collective-permute-done((bf16[768,768]{1,0:T(8,128)(2,1)}, bf16[768,768]{1,0:T(8,128)(2,1)}, u32[]{:S(2)}, u32[]{:S(2)}) %collective-permute-start.3) | collective-permute-done | bytes 1179680 | tf_op jit(solution)/shard_map/ppermute | solution.py:307
  20.7 0.1 collective-permute-start.4
  20.8 2.3 %collective-permute-start = (bf16[768,768]{1,0:T(8,128)(2,1)S(1)}, bf16[768,768]{1,0:T(8,128)(2,1)S(1)}, u32[]{:S(2)}, u32[]{:S(2)}) collective-permute-start(bf16[768,768]{1,0:T(8,128)(2,1)S(1)} %pad_maximum_fusion.refs_1_), channel_id=1, source_target_pairs={{1,2},{3,4},{5,6},{2,1},{4,3},{6,5},{9,10},{11,12},{13,14},{10,9},... | collective-permute-start | bytes 3538952 | tf_op jit(solution)/shard_map/ppermute | solution.py:307
  23.1 0.0 collective-permute-done.1.refs_2_
  23.2 3.2 %collective-permute-start.2 = (bf16[768,768]{1,0:T(8,128)(2,1)}, bf16[768,768]{1,0:T(8,128)(2,1)}, u32[]{:S(2)}, u32[]{:S(2)}) collective-permute-start(bf16[768,768]{1,0:T(8,128)(2,1)} %collective-permute-done.1.refs_2_), channel_id=1, source_target_pairs={{1,2},{3,4},{5,6},{2,1},{4,3},{6,5},{9,10},{11,12},{13,14},{10,9},... | collective-permute-start | bytes 3538952 | tf_op jit(solution)/shard_map/ppermute | solution.py:307
  26.4 0.1 pad_add_fusion.table_ref
  26.5 0.0 collective-permute-done.5.refs_3_
  26.5 13.6 %shard_map.55 = (f32[384,768]{1,0:T(8,128)S(1)}, f32[384,768]{1,0:T(8,128)S(1)}, f32[384,768]{1,0:T(8,128)S(1)}, f32[384,768]{1,0:T(8,128)S(1)}, f32[384,768]{1,0:T(8,128)S(1)}, /*index=5*/f32[384,768]{1,0:T(8,128)S(1)}) custom-call(s32[9]{0:T(128)S(1)} %pad_add_fusion.table_ref, bf16[768,768]{1,0:T(8,128)(2,1)S(1)} %copy-done, ...), custom_call_target="tpu_custom_call" | custom-call | tf_op jit(solution)/shard_map/pallas_call | solution.py:153
  40.0 0.0 slice-start
  40.1 5.8 %shard_map.56 = (f32[384,768]{1,0:T(8,128)S(1)}, f32[384,768]{1,0:T(8,128)S(1)}, f32[384,768]{1,0:T(8,128)S(1)}, f32[384,768]{1,0:T(8,128)S(1)}, f32[384,768]{1,0:T(8,128)S(1)}, /*index=5*/f32[384,768]{1,0:T(8,128)S(1)}) custom-call(s32[9]{0:T(128)S(1)} %pad_add_fusion.table_ref, ...), custom_call_target="tpu_custom_call", output_to_operand_aliasing={{0}: (3, {}), {1}: (4, {}), {2}: (5, {}), {3}: (6, {}), {4}... | custom-call | tf_op jit(solution)/shard_map/pallas_call | solution.py:153
  45.8 0.0 collective-permute-done.4.refs_0_
  45.8 0.0 slice-start.1
  45.9 2.6 %shard_map.57 = (f32[384,768]{1,0:T(8,128)S(1)}, f32[384,768]{1,0:T(8,128)S(1)}, f32[384,768]{1,0:T(8,128)S(1)}, f32[384,768]{1,0:T(8,128)S(1)}, f32[384,768]{1,...) custom-call(s32[9]{0:T(128)S(1)} %pad_add_fusion.table_ref, ...), custom_call_target="tpu_custom_call", output_to_operand_aliasing={{0}: (3, {}), {1}: (4, {}), {2}: (5, {}), {3}: (6, {}), {4}... | custom-call | tf_op jit(solution)/shard_map/pallas_call | solution.py:153
  48.4 0.0 collective-permute-done.refs_0_
  48.4 2.6 %collective-permute-done.2.refs_1_ = bf16[768,768]{1,0:T(8,128)(2,1)} collective-permute-done((bf16[768,768]{1,0:T(8,128)(2,1)}, bf16[768,768]{1,0:T(8,128)(2,1)}, u32[]{:S(2)}, u32[]{:S(2)}) %collective-permute-start.2) | collective-permute-done | bytes 1179680 | tf_op jit(solution)/shard_map/ppermute | solution.py:307
  51.0 4.3 %shard_map.58.left = bf16[384,768]{1,0:T(8,128)(2,1)S(1)} custom-call(s32[9]{0:T(128)S(1)} %pad_add_fusion.table_ref, bf16[768,768]{1,0:T(8,128)(2,1)S(1)} %copy-done, bf16[768,768]{1,0:T(8,128)(2,1)S(1)} %collective-permute-done.refs_0_, bf16[768,768]{1,0:T(8,128)(2,1)} %collective-permute-done.2.refs_1_, ...), custom_call_target="tpu_custom_call", output_to_operand_aliasing={{}: (7, {})} | custom-call | tf_op jit(solution)/shard_map/pallas_call | solution.py:153
  55.3 0.7 shard_map.59
  56.0 1.7 %collective-permute-start.6 = (bf16[192,1536]{1,0:T(8,128)(2,1)S(1)}, bf16[192,1536]{1,0:T(8,128)(2,1)S(1)}, u32[]{:S(2)}, u32[]{:S(2)}) collective-permute-start(bf16[192,1536]{1,0:T(8,128)(2,1)S(1)} %shard_map.59), channel_id=1, source_target_pairs={{0,8},{8,0},{16,24},{24,16},{1,9},{9,1},{17,25},{25,17},{2,10},{10... | collective-permute-start | bytes 1769480 | tf_op jit(solution)/shard_map/ppermute | solution.py:322
  57.7 1.4 %shard_map.63.left = bf16[384,768]{1,0:T(8,128)(2,1)S(1)} custom-call(s32[9]{0:T(128)S(1)} %pad_add_fusion.table_ref, bf16[768,768]{1,0:T(8,128)(2,1)S(1)} %copy-done, bf16[768,768]{1,0:T(8,128)(2,1)S(1)} %collective-permute-done.refs_0_, f32[384,768]{1,0:T(8,128)S(1)} %get-tuple-element.41.refs_1_, ...), custom_call_target="tpu_custom_call", output_to_operand_aliasing={{}: (6, {})} | custom-call | tf_op jit(solution)/shard_map/pallas_call | solution.py:153
  59.1 0.7 shard_map.64
  59.8 1.1 %collective-permute-start.10 = (bf16[192,1536]{1,0:T(8,128)(2,1)S(1)}, bf16[192,1536]{1,0:T(8,128)(2,1)S(1)}, u32[]{:S(2)}, u32[]{:S(2)}) collective-permute-start(bf16[192,1536]{1,0:T(8,128)(2,1)S(1)} %shard_map.64), channel_id=1, source_target_pairs={{0,8},{8,0},{16,24},{24,16},{1,9},{9,1},{17,25},{25,17},{2,10},{10... | collective-permute-start | bytes 1769480 | tf_op jit(solution)/shard_map/ppermute | solution.py:322
  60.9 0.6 shard_map.66
  61.5 0.1 collective-permute-start.12
  61.6 0.7 shard_map.61
  62.3 2.1 %collective-permute-start.8 = (bf16[192,1536]{1,0:T(8,128)(2,1)S(1)}, bf16[192,1536]{1,0:T(8,128)(2,1)S(1)}, u32[]{:S(2)}, u32[]{:S(2)}) collective-permute-start(bf16[192,1536]{1,0:T(8,128)(2,1)S(1)} %shard_map.61), channel_id=1, source_target_pairs={{0,16},{8,24},{16,0},{24,8},{1,17},{9,25},{17,1},{25,9},{2,18},{10... | collective-permute-start | bytes 1769480 | tf_op jit(solution)/shard_map/ppermute | solution.py:322
  64.4 7.9 %collective-permute-done.6.rest_0_ = bf16[192,1536]{1,0:T(8,128)(2,1)S(1)} collective-permute-done((bf16[192,1536]{1,0:T(8,128)(2,1)S(1)}, bf16[192,1536]{1,0:T(8,128)(2,1)S(1)}, u32[]{:S(2)}, u32[]{:S(2)}) %collective-permute-start.6) | collective-permute-done | bytes 589856 | tf_op jit(solution)/shard_map/ppermute | solution.py:322
  72.3 0.4 shard_map.60
  72.7 0.1 collective-permute-start.7
  72.8 11.6 %collective-permute-done.10.rest_0_ = bf16[192,1536]{1,0:T(8,128)(2,1)S(1)} collective-permute-done((bf16[192,1536]{1,0:T(8,128)(2,1)S(1)}, bf16[192,1536]{1,0:T(8,128)(2,1)S(1)}, u32[]{:S(2)}, u32[]{:S(2)}) %collective-permute-start.10) | collective-permute-done | bytes 589856 | tf_op jit(solution)/shard_map/ppermute | solution.py:322
  84.4 0.4 shard_map.65
  84.8 0.1 collective-permute-start.11
  84.9 0.4 shard_map.67
  85.3 1.7 %collective-permute-start.13 = (bf16[192,768]{1,0:T(8,128)(2,1)S(1)}, bf16[192,768]{1,0:T(8,128)(2,1)S(1)}, u32[]{:S(2)}, u32[]{:S(2)}) collective-permute-start(bf16[192,768]{1,0:T(8,128)(2,1)S(1)} %shard_map.67), channel_id=1, source_target_pairs={{0,8},{8,0},{16,24},{24,16},{1,9},{9,1},{17,25},{25,17},{2,10},{10... | collective-permute-start | bytes 884744 | tf_op jit(solution)/shard_map/ppermute | solution.py:322
  87.0 3.5 %collective-permute-done.8.rest_0_.rest_2_ = bf16[192,1536]{1,0:T(8,128)(2,1)S(1)} collective-permute-done((bf16[192,1536]{1,0:T(8,128)(2,1)S(1)}, bf16[192,1536]{1,0:T(8,128)(2,1)S(1)}, u32[]{:S(2)}, u32[]{:S(2)}) %collective-permute-start.8) | collective-permute-done | bytes 589856 | tf_op jit(solution)/shard_map/ppermute | solution.py:322
  90.5 0.4 shard_map.62
  90.9 1.1 %collective-permute-start.9 = (bf16[192,768]{1,0:T(8,128)(2,1)S(1)}, bf16[192,768]{1,0:T(8,128)(2,1)S(1)}, u32[]{:S(2)}, u32[]{:S(2)}) collective-permute-start(bf16[192,768]{1,0:T(8,128)(2,1)S(1)} %shard_map.62), channel_id=1, source_target_pairs={{0,8},{8,0},{16,24},{24,16},{1,9},{9,1},{17,25},{25,17},{2,10},{10... | collective-permute-start | bytes 884744 | tf_op jit(solution)/shard_map/ppermute | solution.py:322
  92.0 10.0 %collective-permute-done.11.rest_1_ = bf16[192,768]{1,0:T(8,128)(2,1)S(1)} collective-permute-done((bf16[192,768]{1,0:T(8,128)(2,1)S(1)}, bf16[192,768]{1,0:T(8,128)(2,1)S(1)}, u32[]{:S(2)}, u32[]{:S(2)}) %collective-permute-start.11) | collective-permute-done | bytes 294944 | tf_op jit(solution)/shard_map/ppermute | solution.py:322
  101.9 1.4 %shard_map.68.rest_4_ = bf16[768,768]{1,0:T(8,128)(2,1)} custom-call(bf16[384,768]{1,0:T(8,128)(2,1)S(1)} %shard_map.63.left, bf16[768,3072]{1,0:T(8,128)(2,1)S(1)} %bitcast.4, bf16[192,1536]{1,0:T(8,128)(2,1)S(1)} %collective-permute-done.10.rest_0_, bf16[192,768]{1,0:T(8,128)(2,1)S(1)} %collective-permute-done.11.rest_1_, ...), custom_call_target="tpu_custom_call" | custom-call | tf_op jit(solution)/shard_map/pallas_call | solution.py:277
  103.4 0.0 collective-permute-done.9.rest_3_
  103.4 1.5 %shard_map.69 = bf16[768,768]{1,0:T(8,128)(2,1)} custom-call(bf16[384,768]{1,0:T(8,128)(2,1)S(1)} %shard_map.58.left, bf16[768,3072]{1,0:T(8,128)(2,1)S(1)} %bitcast.4, bf16[192,1536]{1,0:T(8,128)(2,1)S(1)} %collective-permute-done.6.rest_0_, bf16[192,768]{1,0:T(8,128)(2,1)S(1)} %collective-permute-done.7.rest_1_, ...), custom_call_target="tpu_custom_call", output_to_operand_aliasing={{}: (6, {})} | custom-call | tf_op jit(solution)/shard_map/pallas_call | solution.py:277
  (8 shorter events, 0.0 us)
Async XLA Ops:
  2.8 17.8 %collective-permute-start.3 = (bf16[768,768]{1,0:T(8,128)(2,1)}, bf16[768,768]{1,0:T(8,128)(2,1)}, u32[]{:S(2)}, u32[]{:S(2)}) collective-permute-start(bf16[768,768]{1,0:T(8,128)(2,1)} %pad_maximum_fusion.1.refs_0_), channel_id=1, source_target_pairs={{1,2},{3,4},{5,6},{2,1},{4,3},{6,5},{9,10},{11,12},{13,14},{10,9},... | collective-permute-start | bytes 3538952 | tf_op jit(solution)/shard_map/ppermute | solution.py:307
  4.8 21.6 %copy-start.1 = (s32[6]{0:T(128)S(1)}, s32[6]{0:T(128)}, u32[]{:S(2)}) copy-start(s32[6]{0:T(128)} %param.8) | copy-start | bytes 76
  4.8 21.7 %copy-start = (bf16[768,768]{1,0:T(8,128)(2,1)S(1)}, bf16[768,768]{1,0:T(8,128)(2,1)}, u32[]{:S(2)}) copy-start(bf16[768,768]{1,0:T(8,128)(2,1)} %query.9) | copy-start | bytes 3538948
  4.9 18.3 %collective-permute-start.1 = (bf16[768,768]{1,0:T(8,128)(2,1)S(1)}, bf16[768,768]{1,0:T(8,128)(2,1)}, u32[]{:S(2)}, u32[]{:S(2)}) collective-permute-start(bf16[768,768]{1,0:T(8,128)(2,1)S(1)} %pad_maximum_fusion.refs_1_), channel_id=1, source_target_pairs={{0,1},{1,0},{2,3},{3,2},{4,5},{5,4},{6,7},{7,6},{8,9},{9,8},{10,11... | collective-permute-start | bytes 3538952 | tf_op jit(solution)/shard_map/ppermute | solution.py:303
  6.6 19.9 %collective-permute-start.5 = (bf16[768,768]{1,0:T(8,128)(2,1)}, bf16[768,768]{1,0:T(8,128)(2,1)}, u32[]{:S(2)}, u32[]{:S(2)}) collective-permute-start(bf16[768,768]{1,0:T(8,128)(2,1)} %pad_maximum_fusion.1.refs_0_), channel_id=1, source_target_pairs={{0,1},{1,0},{2,3},{3,2},{4,5},{5,4},{6,7},{7,6},{8,9},{9,8},{10,11... | collective-permute-start | bytes 3538952 | tf_op jit(solution)/shard_map/ppermute | solution.py:303
  20.7 25.2 %collective-permute-start.4 = (bf16[768,768]{1,0:T(8,128)(2,1)}, bf16[768,768]{1,0:T(8,128)(2,1)}, u32[]{:S(2)}, u32[]{:S(2)}) collective-permute-start(bf16[768,768]{1,0:T(8,128)(2,1)} %collective-permute-done.3.refs_0_), channel_id=1, source_target_pairs={{0,1},{1,0},{2,3},{3,2},{4,5},{5,4},{6,7},{7,6},{8,9},{9,8},{10,11... | collective-permute-start | bytes 3538952 | tf_op jit(solution)/shard_map/ppermute | solution.py:303
  20.8 27.6 %collective-permute-start = (bf16[768,768]{1,0:T(8,128)(2,1)S(1)}, bf16[768,768]{1,0:T(8,128)(2,1)S(1)}, u32[]{:S(2)}, u32[]{:S(2)}) collective-permute-start(bf16[768,768]{1,0:T(8,128)(2,1)S(1)} %pad_maximum_fusion.refs_1_), channel_id=1, source_target_pairs={{1,2},{3,4},{5,6},{2,1},{4,3},{6,5},{9,10},{11,12},{13,14},{10,9},... | collective-permute-start | bytes 3538952 | tf_op jit(solution)/shard_map/ppermute | solution.py:307
  23.2 27.9 %collective-permute-start.2 = (bf16[768,768]{1,0:T(8,128)(2,1)}, bf16[768,768]{1,0:T(8,128)(2,1)}, u32[]{:S(2)}, u32[]{:S(2)}) collective-permute-start(bf16[768,768]{1,0:T(8,128)(2,1)} %collective-permute-done.1.refs_2_), channel_id=1, source_target_pairs={{1,2},{3,4},{5,6},{2,1},{4,3},{6,5},{9,10},{11,12},{13,14},{10,9},... | collective-permute-start | bytes 3538952 | tf_op jit(solution)/shard_map/ppermute | solution.py:307
  40.0 15.3 %slice-start = ((s8[4718592]{0:T(1024)(128)(4,1)}), s8[4194304]{0:T(1024)(128)(4,1)S(1)}, s32[]{:S(2)}) async-start(s8[4718592]{0:T(1024)(128)(4,1)} %bitcast.3), calls=%async_computation | async-start | bytes 8388608
  45.8 9.5 %slice-start.1 = ((s8[4718592]{0:T(1024)(128)(4,1)}), s8[524288]{0:T(1024)(128)(4,1)S(1)}, s32[]{:S(2)}) async-start(s8[4718592]{0:T(1024)(128)(4,1)} %bitcast.3), calls=%async_computation.1 | async-start | bytes 1048576
  56.0 16.3 %collective-permute-start.6 = (bf16[192,1536]{1,0:T(8,128)(2,1)S(1)}, bf16[192,1536]{1,0:T(8,128)(2,1)S(1)}, u32[]{:S(2)}, u32[]{:S(2)}) collective-permute-start(bf16[192,1536]{1,0:T(8,128)(2,1)S(1)} %shard_map.59), channel_id=1, source_target_pairs={{0,8},{8,0},{16,24},{24,16},{1,9},{9,1},{17,25},{25,17},{2,10},{10... | collective-permute-start | bytes 1769480 | tf_op jit(solution)/shard_map/ppermute | solution.py:322
  59.8 24.5 %collective-permute-start.10 = (bf16[192,1536]{1,0:T(8,128)(2,1)S(1)}, bf16[192,1536]{1,0:T(8,128)(2,1)S(1)}, u32[]{:S(2)}, u32[]{:S(2)}) collective-permute-start(bf16[192,1536]{1,0:T(8,128)(2,1)S(1)} %shard_map.64), channel_id=1, source_target_pairs={{0,8},{8,0},{16,24},{24,16},{1,9},{9,1},{17,25},{25,17},{2,10},{10... | collective-permute-start | bytes 1769480 | tf_op jit(solution)/shard_map/ppermute | solution.py:322
  61.5 23.3 %collective-permute-start.12 = (bf16[192,1536]{1,0:T(8,128)(2,1)S(1)}, bf16[192,1536]{1,0:T(8,128)(2,1)S(1)}, u32[]{:S(2)}, u32[]{:S(2)}) collective-permute-start(bf16[192,1536]{1,0:T(8,128)(2,1)S(1)} %shard_map.66), channel_id=1, source_target_pairs={{0,16},{8,24},{16,0},{24,8},{1,17},{9,25},{17,1},{25,9},{2,18},{10... | collective-permute-start | bytes 1769480 | tf_op jit(solution)/shard_map/ppermute | solution.py:322
  62.3 28.1 %collective-permute-start.8 = (bf16[192,1536]{1,0:T(8,128)(2,1)S(1)}, bf16[192,1536]{1,0:T(8,128)(2,1)S(1)}, u32[]{:S(2)}, u32[]{:S(2)}) collective-permute-start(bf16[192,1536]{1,0:T(8,128)(2,1)S(1)} %shard_map.61), channel_id=1, source_target_pairs={{0,16},{8,24},{16,0},{24,8},{1,17},{9,25},{17,1},{25,9},{2,18},{10... | collective-permute-start | bytes 1769480 | tf_op jit(solution)/shard_map/ppermute | solution.py:322
  72.7 30.7 %collective-permute-start.7 = (bf16[192,768]{1,0:T(8,128)(2,1)S(1)}, bf16[192,768]{1,0:T(8,128)(2,1)S(1)}, u32[]{:S(2)}, u32[]{:S(2)}) collective-permute-start(bf16[192,768]{1,0:T(8,128)(2,1)S(1)} %shard_map.60), channel_id=1, source_target_pairs={{0,16},{8,24},{16,0},{24,8},{1,17},{9,25},{17,1},{25,9},{2,18},{10... | collective-permute-start | bytes 884744 | tf_op jit(solution)/shard_map/ppermute | solution.py:322
  84.8 17.2 %collective-permute-start.11 = (bf16[192,768]{1,0:T(8,128)(2,1)S(1)}, bf16[192,768]{1,0:T(8,128)(2,1)S(1)}, u32[]{:S(2)}, u32[]{:S(2)}) collective-permute-start(bf16[192,768]{1,0:T(8,128)(2,1)S(1)} %shard_map.65), channel_id=1, source_target_pairs={{0,16},{8,24},{16,0},{24,8},{1,17},{9,25},{17,1},{25,9},{2,18},{10... | collective-permute-start | bytes 884744 | tf_op jit(solution)/shard_map/ppermute | solution.py:322
  85.3 16.7 %collective-permute-start.13 = (bf16[192,768]{1,0:T(8,128)(2,1)S(1)}, bf16[192,768]{1,0:T(8,128)(2,1)S(1)}, u32[]{:S(2)}, u32[]{:S(2)}) collective-permute-start(bf16[192,768]{1,0:T(8,128)(2,1)S(1)} %shard_map.67), channel_id=1, source_target_pairs={{0,8},{8,0},{16,24},{24,16},{1,9},{9,1},{17,25},{25,17},{2,10},{10... | collective-permute-start | bytes 884744 | tf_op jit(solution)/shard_map/ppermute | solution.py:322
  90.9 12.5 %collective-permute-start.9 = (bf16[192,768]{1,0:T(8,128)(2,1)S(1)}, bf16[192,768]{1,0:T(8,128)(2,1)S(1)}, u32[]{:S(2)}, u32[]{:S(2)}) collective-permute-start(bf16[192,768]{1,0:T(8,128)(2,1)S(1)} %shard_map.62), channel_id=1, source_target_pairs={{0,8},{8,0},{16,24},{24,16},{1,9},{9,1},{17,25},{25,17},{2,10},{10... | collective-permute-start | bytes 884744 | tf_op jit(solution)/shard_map/ppermute | solution.py:322

commit v4 on v3

--- a/solution.py
+++ b/solution.py
@@ -27,16 +27,15 @@
 def pack_frames(key_tok, value_tok):
     parity = lax.axis_index("frame") % 2
 
-    def packed(frame):
+    def packed(key, value, frame):
         return jnp.concatenate(
-            [
-                lax.dynamic_slice_in_dim(array, frame * FRAME_TOK, FRAME_TOK, 0)
-                for array in (key_tok, value_tok)
-            ],
+            [lax.dynamic_slice_in_dim(array, frame * FRAME_TOK, FRAME_TOK, 0) for array in (key, value)],
             axis=0,
         )
 
-    return packed(parity), packed(1 - parity)
+    edge = packed(key_tok, value_tok, parity)
+    edge, key_tok, value_tok = lax.optimization_barrier((edge, key_tok, value_tok))
+    return edge, packed(key_tok, value_tok, 1 - parity)
 
 
 def attend_step(table, query_tok, sources, states, cases, first=False, closed=None):
@@ -236,26 +235,47 @@
     )(attended, out_weight, *(array for array, _ in received))
 
 
-def finish(attended, parts, out_weight, received, is_edge, frames_here, into):
+def sum_own(attended, parts, out_weight, received):
     groups = lax.axis_size("head")
     width = out_weight.shape[1] // groups
     rows = FRAME_TOK // parts
     flat = [(array, spots[0], part) for part in range(parts) for array, spots in received[part]]
 
     def kernel(left, right, *rest):
+        out = rest[-1]
+        group = lax.axis_index("head")
+        column = pl.ds(pl.multiple_of(group * width, width), width)
+        sums = jnp.dot(left[...], right[:, column], preferred_element_type=F32)
+        for part in range(parts):
+            terms = sums[part * rows : (part + 1) * rows]
+            for ref, (_, spot, owner) in zip(rest, flat):
+                if owner == part:
+                    terms = terms + ref[:, spot * width : (spot + 1) * width].astype(F32)
+            out[part * rows : (part + 1) * rows, :] = terms
+
+    operands = [attended, out_weight, *(array for array, _, _ in flat)]
+    return pl.pallas_call(
+        kernel,
+        out_shape=jax.ShapeDtypeStruct((FRAME_TOK, width), F32),
+        in_specs=[VMEM] * len(operands),
+        out_specs=VMEM,
+        compiler_params=params(),
+    )(*operands)
+
+
+def finish(own, received, is_edge, frames_here, into):
+    parts = len(received)
+    rows = FRAME_TOK // parts
+    width = own.shape[1]
+
+    def kernel(terms, *rest):
         out, buffer, sems = rest[-3:]
-        group = lax.axis_index("head")
         parity = lax.axis_index("frame") % 2
         frame = parity if is_edge else 1 - parity
-        column = pl.ds(pl.multiple_of(group * width, width), width)
         copies = []
         for part in range(parts):
             span = slice(part * rows, (part + 1) * rows)
-            sums = jnp.dot(left[span, :], right[:, column], preferred_element_type=F32)
-            for ref, (_, spot, owner) in zip(rest, flat):
-                if owner == part:
-                    sums = sums + ref[:, spot * width : (spot + 1) * width].astype(F32)
-            buffer[span, :] = sums.astype(BF16)
+            buffer[span, :] = (terms[span, :] + rest[part][...].astype(F32)).astype(BF16)
             copies.append(
                 pltpu.make_async_copy(
                     buffer.at[pl.ds(part * rows, rows)],
@@ -267,7 +287,7 @@
         for copy in copies:
             copy.wait()
 
-    operands = [attended, out_weight, *(array for array, _, _ in flat)]
+    operands = [own, *received]
     in_specs = [VMEM] * len(operands)
     aliases = {}
     if into is not None:
@@ -344,15 +364,9 @@
             halve("I", stage + 1)
     result = None
     for role in "IE":
-        result = finish(
-            attended[role],
-            bits,
-            out_weight,
-            [gathered(role, part, [0]) for part in range(bits)],
-            role == "E",
-            local_frames,
-            result,
-        )
+        terms = [gathered(role, part, [0]) for part in range(bits)]
+        own = sum_own(attended[role], bits, out_weight, [t[:-1] for t in terms])
+        result = finish(own, [t[-1][0] for t in terms], role == "E", local_frames, result)
     return result
 
 

time: 105 us -> 104 us (level)
  waiting for transfers between devices: 49.6 us -> 48.1 us
    ppermute x8, waiting for transfers between devices: 33 us -> 31.6 us  [exchange(): lax.ppermute(value, 'head', [(i, i ^ 1 << bit) for i in range(groups)])]
    pallas_call x0 -> x2, Pallas kernels: none -> 1.33 us  [sum_own(): pl.pallas_call(kernel, out_shape=jax.ShapeDtypeStruct((FRAME_TOK, width),...]
    pallas_call x2, Pallas kernels: 2.91 us -> 1.76 us  [finish(): pl.pallas_call(kernel, out_shape=jax.ShapeDtypeStruct((frames_here * FRAM...]
  transfers between devices with their start and end apart: 14 -> 14, of which waited for: 6 -> 6; matrix products, arithmetic and copies ran while one was open for 0% -> 0% of each run, Pallas kernels for 27% -> 28%
where the time goes in v4:
time: 104 us
  waiting for transfers between devices  48.1 us (46%)
  Pallas kernels  35 us (34%)
  starting transfers between devices  17.3 us (17%)
  local copies, waits for them, and re-layouts  1.45 us (1%)
  other arithmetic  1.25 us (1%)
    ppermute x8, waiting for transfers between devices, exchange(): lax.ppermute(value, 'head', [(i, i ^ 1 << bit) for i in range(groups)])  31.6 us
    pallas_call x5, Pallas kernels, attend_step(): pl.pallas_call(kernel, out_shape=tuple(shapes), in_specs=[SMEM] + [VMEM]...  27.6 us
    ppermute x3, waiting for transfers between devices, across(): return lax.ppermute(value, 'frame', pairs + [(b, a) for a, b in pairs])  16.4 us
    ppermute x8, starting transfers between devices, exchange(): lax.ppermute(value, 'head', [(i, i ^ 1 << bit) for i in range(groups)])  7.78 us
    ppermute x3, starting transfers between devices, across(): return lax.ppermute(value, 'frame', pairs + [(b, a) for a, b in pairs])  7.59 us
    pallas_call x8, Pallas kernels, project(): pl.pallas_call(kernel, out_shape=jax.ShapeDtypeStruct((rows, len(slots) *...  4.35 us
  transfers between devices with their start and end apart: 14, of which 6 were waited for; matrix products, arithmetic and copies ran while one was open for 0% of the time, Pallas kernels for 28%

profile of v4, /device:TPU:20, one launch (start us, length us, event | category | flops | bytes accessed | tf_op | source)
XLA Modules:
  0.0 103.6 jit_solution(7340631061523848229)
XLA Ops:
  0.0 1.3 %constant_dynamic-slice_fusion.2 = (bf16[384,768]{1,0:T(8,128)(2,1)S(1)}, bf16[384,768]{1,0:T(8,128)(2,1)S(1)}) fusion(bf16[768,768]{1,0:T(8,128)(2,1)} %param.7, s32[]{:T(128)S(6)} %select_n.27, bf16[768,768]{1,0:T(8,128)(2,1)} %param.6), kind=kLoop, calls=%fused_computation.4 | loop fusion | bytes 2359300 | tf_op jit(solution)/shard_map/dynamic_slice | solution.py:32
  1.3 0.0 copy-start.1
  1.3 1.1 %pad_maximum_fusion.refs_0_ = bf16[768,768]{1,0:T(8,128)(2,1)} fusion(bf16[384,768]{1,0:T(8,128)(2,1)S(1)} %get-tuple-element.51, bf16[384,768]{1,0:T(8,128)(2,1)S(1)} %get-tuple-element.52), kind=kLoop, calls=%fused_computation | loop fusion | flops 2359296 | bytes 2359296 | tf_op jit(solution)/shard_map/concatenate | solution.py:31
  2.4 2.0 %collective-permute-start.3 = (bf16[768,768]{1,0:T(8,128)(2,1)}, bf16[768,768]{1,0:T(8,128)(2,1)}, u32[]{:S(2)}, u32[]{:S(2)}) collective-permute-start(bf16[768,768]{1,0:T(8,128)(2,1)} %pad_maximum_fusion.refs_0_), channel_id=1, source_target_pairs={{1,2},{3,4},{5,6},{2,1},{4,3},{6,5},{9,10},{11,12},{13,14},{10,9},... | collective-permute-start | bytes 3538952 | tf_op jit(solution)/shard_map/ppermute | solution.py:327
  4.6 0.0 copy-start.3
  4.6 0.0 copy-start
  4.6 0.1 pad_maximum_fusion.1.refs_1_
  4.7 1.7 %collective-permute-start.1 = (bf16[768,768]{1,0:T(8,128)(2,1)S(1)}, bf16[768,768]{1,0:T(8,128)(2,1)}, u32[]{:S(2)}, u32[]{:S(2)}) collective-permute-start(bf16[768,768]{1,0:T(8,128)(2,1)S(1)} %pad_maximum_fusion.1.refs_1_), channel_id=1, source_target_pairs={{0,1},{1,0},{2,3},{3,2},{4,5},{5,4},{6,7},{7,6},{8,9},{9,8},{10,11... | collective-permute-start | bytes 3538952 | tf_op jit(solution)/shard_map/ppermute | solution.py:323
  6.5 0.1 collective-permute-start.5
  6.6 13.8 %collective-permute-done.3.refs_0_ = bf16[768,768]{1,0:T(8,128)(2,1)} collective-permute-done((bf16[768,768]{1,0:T(8,128)(2,1)}, bf16[768,768]{1,0:T(8,128)(2,1)}, u32[]{:S(2)}, u32[]{:S(2)}) %collective-permute-start.3) | collective-permute-done | bytes 1179680 | tf_op jit(solution)/shard_map/ppermute | solution.py:327
  20.4 0.1 collective-permute-start.4
  20.5 2.3 %collective-permute-start = (bf16[768,768]{1,0:T(8,128)(2,1)S(1)}, bf16[768,768]{1,0:T(8,128)(2,1)S(1)}, u32[]{:S(2)}, u32[]{:S(2)}) collective-permute-start(bf16[768,768]{1,0:T(8,128)(2,1)S(1)} %pad_maximum_fusion.1.refs_1_), channel_id=1, source_target_pairs={{1,2},{3,4},{5,6},{2,1},{4,3},{6,5},{9,10},{11,12},{13,14},{10,9},... | collective-permute-start | bytes 3538952 | tf_op jit(solution)/shard_map/ppermute | solution.py:327
  22.9 3.2 %collective-permute-start.2 = (bf16[768,768]{1,0:T(8,128)(2,1)}, bf16[768,768]{1,0:T(8,128)(2,1)}, u32[]{:S(2)}, u32[]{:S(2)}) collective-permute-start(bf16[768,768]{1,0:T(8,128)(2,1)} %collective-permute-done.1.refs_2_), channel_id=1, source_target_pairs={{1,2},{3,4},{5,6},{2,1},{4,3},{6,5},{9,10},{11,12},{13,14},{10,9},... | collective-permute-start | bytes 3538952 | tf_op jit(solution)/shard_map/ppermute | solution.py:327
  26.1 0.1 pad_add_fusion.table_ref
  26.2 0.0 collective-permute-done.5.refs_3_
  26.2 13.6 %shard_map.55 = (f32[384,768]{1,0:T(8,128)S(1)}, f32[384,768]{1,0:T(8,128)S(1)}, f32[384,768]{1,0:T(8,128)S(1)}, f32[384,768]{1,0:T(8,128)S(1)}, f32[384,768]{1,0:T(8,128)S(1)}, /*index=5*/f32[384,768]{1,0:T(8,128)S(1)}) custom-call(s32[9]{0:T(128)S(1)} %pad_add_fusion.table_ref, bf16[768,768]{1,0:T(8,128)(2,1)S(1)} %copy-done, ...), custom_call_target="tpu_custom_call" | custom-call | tf_op jit(solution)/shard_map/pallas_call | solution.py:152
  39.8 0.0 slice-start
  39.8 5.8 %shard_map.56 = (f32[384,768]{1,0:T(8,128)S(1)}, f32[384,768]{1,0:T(8,128)S(1)}, f32[384,768]{1,0:T(8,128)S(1)}, f32[384,768]{1,0:T(8,128)S(1)}, f32[384,768]{1,0:T(8,128)S(1)}, /*index=5*/f32[384,768]{1,0:T(8,128)S(1)}) custom-call(s32[9]{0:T(128)S(1)} %pad_add_fusion.table_ref, ...), custom_call_target="tpu_custom_call", output_to_operand_aliasing={{0}: (3, {}), {1}: (4, {}), {2}: (5, {}), {3}: (6, {}), {4}... | custom-call | tf_op jit(solution)/shard_map/pallas_call | solution.py:152
  45.5 0.0 collective-permute-done.4.refs_0_
  45.6 0.0 slice-start.1
  45.6 2.6 %shard_map.57 = (f32[384,768]{1,0:T(8,128)S(1)}, f32[384,768]{1,0:T(8,128)S(1)}, f32[384,768]{1,0:T(8,128)S(1)}, f32[384,768]{1,0:T(8,128)S(1)}, f32[384,768]{1,...) custom-call(s32[9]{0:T(128)S(1)} %pad_add_fusion.table_ref, ...), custom_call_target="tpu_custom_call", output_to_operand_aliasing={{0}: (3, {}), {1}: (4, {}), {2}: (5, {}), {3}: (6, {}), {4}... | custom-call | tf_op jit(solution)/shard_map/pallas_call | solution.py:152
  48.2 2.6 %collective-permute-done.2.refs_1_ = bf16[768,768]{1,0:T(8,128)(2,1)} collective-permute-done((bf16[768,768]{1,0:T(8,128)(2,1)}, bf16[768,768]{1,0:T(8,128)(2,1)}, u32[]{:S(2)}, u32[]{:S(2)}) %collective-permute-start.2) | collective-permute-done | bytes 1179680 | tf_op jit(solution)/shard_map/ppermute | solution.py:327
  50.8 4.3 %shard_map.58.left = bf16[384,768]{1,0:T(8,128)(2,1)S(1)} custom-call(s32[9]{0:T(128)S(1)} %pad_add_fusion.table_ref, bf16[768,768]{1,0:T(8,128)(2,1)S(1)} %copy-done, bf16[768,768]{1,0:T(8,128)(2,1)S(1)} %collective-permute-done.refs_0_, bf16[768,768]{1,0:T(8,128)(2,1)} %collective-permute-done.2.refs_1_, ...), custom_call_target="tpu_custom_call", output_to_operand_aliasing={{}: (7, {})} | custom-call | tf_op jit(solution)/shard_map/pallas_call | solution.py:152
  55.1 0.7 shard_map.59
  55.7 1.7 %collective-permute-start.6 = (bf16[192,1536]{1,0:T(8,128)(2,1)S(1)}, bf16[192,1536]{1,0:T(8,128)(2,1)S(1)}, u32[]{:S(2)}, u32[]{:S(2)}) collective-permute-start(bf16[192,1536]{1,0:T(8,128)(2,1)S(1)} %shard_map.59), channel_id=1, source_target_pairs={{0,8},{8,0},{16,24},{24,16},{1,9},{9,1},{17,25},{25,17},{2,10},{10... | collective-permute-start | bytes 1769480 | tf_op jit(solution)/shard_map/ppermute | solution.py:342
  57.4 1.4 %shard_map.64.left = bf16[384,768]{1,0:T(8,128)(2,1)S(1)} custom-call(s32[9]{0:T(128)S(1)} %pad_add_fusion.table_ref, bf16[768,768]{1,0:T(8,128)(2,1)S(1)} %copy-done, bf16[768,768]{1,0:T(8,128)(2,1)S(1)} %collective-permute-done.refs_0_, f32[384,768]{1,0:T(8,128)S(1)} %get-tuple-element.47.refs_1_, ...), custom_call_target="tpu_custom_call", output_to_operand_aliasing={{}: (6, {})} | custom-call | tf_op jit(solution)/shard_map/pallas_call | solution.py:152
  58.8 0.7 shard_map.65
  59.5 1.1 %collective-permute-start.10 = (bf16[192,1536]{1,0:T(8,128)(2,1)S(1)}, bf16[192,1536]{1,0:T(8,128)(2,1)S(1)}, u32[]{:S(2)}, u32[]{:S(2)}) collective-permute-start(bf16[192,1536]{1,0:T(8,128)(2,1)S(1)} %shard_map.65), channel_id=1, source_target_pairs={{0,8},{8,0},{16,24},{24,16},{1,9},{9,1},{17,25},{25,17},{2,10},{10... | collective-permute-start | bytes 1769480 | tf_op jit(solution)/shard_map/ppermute | solution.py:342
  60.6 0.6 shard_map.66
  61.3 0.1 collective-permute-start.11
  61.3 0.7 shard_map.60
  62.0 2.0 %collective-permute-start.7 = (bf16[192,1536]{1,0:T(8,128)(2,1)S(1)}, bf16[192,1536]{1,0:T(8,128)(2,1)S(1)}, u32[]{:S(2)}, u32[]{:S(2)}) collective-permute-start(bf16[192,1536]{1,0:T(8,128)(2,1)S(1)} %shard_map.60), channel_id=1, source_target_pairs={{0,16},{8,24},{16,0},{24,8},{1,17},{9,25},{17,1},{25,9},{2,18},{10... | collective-permute-start | bytes 1769480 | tf_op jit(solution)/shard_map/ppermute | solution.py:342
  64.1 7.9 %collective-permute-done.6.rest_0_ = bf16[192,1536]{1,0:T(8,128)(2,1)S(1)} collective-permute-done((bf16[192,1536]{1,0:T(8,128)(2,1)S(1)}, bf16[192,1536]{1,0:T(8,128)(2,1)S(1)}, u32[]{:S(2)}, u32[]{:S(2)}) %collective-permute-start.6) | collective-permute-done | bytes 589856 | tf_op jit(solution)/shard_map/ppermute | solution.py:342
  72.0 0.4 shard_map.62
  72.4 0.1 collective-permute-start.8
  72.5 11.6 %collective-permute-done.10.rest_0_ = bf16[192,1536]{1,0:T(8,128)(2,1)S(1)} collective-permute-done((bf16[192,1536]{1,0:T(8,128)(2,1)S(1)}, bf16[192,1536]{1,0:T(8,128)(2,1)S(1)}, u32[]{:S(2)}, u32[]{:S(2)}) %collective-permute-start.10) | collective-permute-done | bytes 589856 | tf_op jit(solution)/shard_map/ppermute | solution.py:342
  84.1 0.4 shard_map.68
  84.5 0.1 collective-permute-start.12
  84.6 0.4 shard_map.69
  85.0 1.7 %collective-permute-start.13 = (bf16[192,768]{1,0:T(8,128)(2,1)S(1)}, bf16[192,768]{1,0:T(8,128)(2,1)S(1)}, u32[]{:S(2)}, u32[]{:S(2)}) collective-permute-start(bf16[192,768]{1,0:T(8,128)(2,1)S(1)} %shard_map.69), channel_id=1, source_target_pairs={{0,8},{8,0},{16,24},{24,16},{1,9},{9,1},{17,25},{25,17},{2,10},{10... | collective-permute-start | bytes 884744 | tf_op jit(solution)/shard_map/ppermute | solution.py:342
  86.7 3.5 %collective-permute-done.7.rest_1_.rest_0_ = bf16[192,1536]{1,0:T(8,128)(2,1)S(1)} collective-permute-done((bf16[192,1536]{1,0:T(8,128)(2,1)S(1)}, bf16[192,1536]{1,0:T(8,128)(2,1)S(1)}, u32[]{:S(2)}, u32[]{:S(2)}) %collective-permute-start.7) | collective-permute-done | bytes 589856 | tf_op jit(solution)/shard_map/ppermute | solution.py:342
  90.2 0.4 shard_map.63
  90.6 1.1 %collective-permute-start.9 = (bf16[192,768]{1,0:T(8,128)(2,1)S(1)}, bf16[192,768]{1,0:T(8,128)(2,1)S(1)}, u32[]{:S(2)}, u32[]{:S(2)}) collective-permute-start(bf16[192,768]{1,0:T(8,128)(2,1)S(1)} %shard_map.63), channel_id=1, source_target_pairs={{0,8},{8,0},{16,24},{24,16},{1,9},{9,1},{17,25},{25,17},{2,10},{10... | collective-permute-start | bytes 884744 | tf_op jit(solution)/shard_map/ppermute | solution.py:342
  91.7 0.7 shard_map.61.terms
  92.3 0.7 shard_map.67.terms
  93.0 8.6 %collective-permute-done.12.rest_0_ = bf16[192,768]{1,0:T(8,128)(2,1)S(1)} collective-permute-done((bf16[192,768]{1,0:T(8,128)(2,1)S(1)}, bf16[192,768]{1,0:T(8,128)(2,1)S(1)}, u32[]{:S(2)}, u32[]{:S(2)}) %collective-permute-start.12) | collective-permute-done | bytes 294944 | tf_op jit(solution)/shard_map/ppermute | solution.py:342
  101.7 0.9 shard_map.70.rest_2_
  102.6 0.9 shard_map.71
  (16 shorter events, 0.1 us)
Async XLA Ops:
  1.3 3.2 %copy-start.1 = (bf16[768,768]{1,0:T(8,128)(2,1)S(1)}, bf16[768,768]{1,0:T(8,128)(2,1)}, u32[]{:S(2)}) copy-start(bf16[768,768]{1,0:T(8,128)(2,1)} %param.6) | copy-start | bytes 3538948
  2.4 2.1 %copy-start.2 = (bf16[768,768]{1,0:T(8,128)(2,1)S(1)}, bf16[768,768]{1,0:T(8,128)(2,1)}, u32[]{:S(2)}) copy-start(bf16[768,768]{1,0:T(8,128)(2,1)} %param.7) | copy-start | bytes 3538948
  2.4 18.0 %collective-permute-start.3 = (bf16[768,768]{1,0:T(8,128)(2,1)}, bf16[768,768]{1,0:T(8,128)(2,1)}, u32[]{:S(2)}, u32[]{:S(2)}) collective-permute-start(bf16[768,768]{1,0:T(8,128)(2,1)} %pad_maximum_fusion.refs_0_), channel_id=1, source_target_pairs={{1,2},{3,4},{5,6},{2,1},{4,3},{6,5},{9,10},{11,12},{13,14},{10,9},... | collective-permute-start | bytes 3538952 | tf_op jit(solution)/shard_map/ppermute | solution.py:327
  4.6 21.5 %copy-start.3 = (s32[6]{0:T(128)S(1)}, s32[6]{0:T(128)}, u32[]{:S(2)}) copy-start(s32[6]{0:T(128)} %param.8) | copy-start | bytes 76
  4.6 21.6 %copy-start = (bf16[768,768]{1,0:T(8,128)(2,1)S(1)}, bf16[768,768]{1,0:T(8,128)(2,1)}, u32[]{:S(2)}) copy-start(bf16[768,768]{1,0:T(8,128)(2,1)} %query.9) | copy-start | bytes 3538948
  4.7 18.1 %collective-permute-start.1 = (bf16[768,768]{1,0:T(8,128)(2,1)S(1)}, bf16[768,768]{1,0:T(8,128)(2,1)}, u32[]{:S(2)}, u32[]{:S(2)}) collective-permute-start(bf16[768,768]{1,0:T(8,128)(2,1)S(1)} %pad_maximum_fusion.1.refs_1_), channel_id=1, source_target_pairs={{0,1},{1,0},{2,3},{3,2},{4,5},{5,4},{6,7},{7,6},{8,9},{9,8},{10,11... | collective-permute-start | bytes 3538952 | tf_op jit(solution)/shard_map/ppermute | solution.py:323
  6.5 19.7 %collective-permute-start.5 = (bf16[768,768]{1,0:T(8,128)(2,1)}, bf16[768,768]{1,0:T(8,128)(2,1)}, u32[]{:S(2)}, u32[]{:S(2)}) collective-permute-start(bf16[768,768]{1,0:T(8,128)(2,1)} %pad_maximum_fusion.refs_0_), channel_id=1, source_target_pairs={{0,1},{1,0},{2,3},{3,2},{4,5},{5,4},{6,7},{7,6},{8,9},{9,8},{10,11... | collective-permute-start | bytes 3538952 | tf_op jit(solution)/shard_map/ppermute | solution.py:323
  20.4 25.2 %collective-permute-start.4 = (bf16[768,768]{1,0:T(8,128)(2,1)}, bf16[768,768]{1,0:T(8,128)(2,1)}, u32[]{:S(2)}, u32[]{:S(2)}) collective-permute-start(bf16[768,768]{1,0:T(8,128)(2,1)} %collective-permute-done.3.refs_0_), channel_id=1, source_target_pairs={{0,1},{1,0},{2,3},{3,2},{4,5},{5,4},{6,7},{7,6},{8,9},{9,8},{10,11... | collective-permute-start | bytes 3538952 | tf_op jit(solution)/shard_map/ppermute | solution.py:323
  20.5 27.6 %collective-permute-start = (bf16[768,768]{1,0:T(8,128)(2,1)S(1)}, bf16[768,768]{1,0:T(8,128)(2,1)S(1)}, u32[]{:S(2)}, u32[]{:S(2)}) collective-permute-start(bf16[768,768]{1,0:T(8,128)(2,1)S(1)} %pad_maximum_fusion.1.refs_1_), channel_id=1, source_target_pairs={{1,2},{3,4},{5,6},{2,1},{4,3},{6,5},{9,10},{11,12},{13,14},{10,9},... | collective-permute-start | bytes 3538952 | tf_op jit(solution)/shard_map/ppermute | solution.py:327
  22.9 27.9 %collective-permute-start.2 = (bf16[768,768]{1,0:T(8,128)(2,1)}, bf16[768,768]{1,0:T(8,128)(2,1)}, u32[]{:S(2)}, u32[]{:S(2)}) collective-permute-start(bf16[768,768]{1,0:T(8,128)(2,1)} %collective-permute-done.1.refs_2_), channel_id=1, source_target_pairs={{1,2},{3,4},{5,6},{2,1},{4,3},{6,5},{9,10},{11,12},{13,14},{10,9},... | collective-permute-start | bytes 3538952 | tf_op jit(solution)/shard_map/ppermute | solution.py:327
  39.8 15.3 %slice-start = ((s8[4718592]{0:T(1024)(128)(4,1)}), s8[4194304]{0:T(1024)(128)(4,1)S(1)}, s32[]{:S(2)}) async-start(s8[4718592]{0:T(1024)(128)(4,1)} %bitcast.3), calls=%async_computation | async-start | bytes 8388608
  45.6 9.5 %slice-start.1 = ((s8[4718592]{0:T(1024)(128)(4,1)}), s8[524288]{0:T(1024)(128)(4,1)S(1)}, s32[]{:S(2)}) async-start(s8[4718592]{0:T(1024)(128)(4,1)} %bitcast.3), calls=%async_computation.1 | async-start | bytes 1048576
  55.7 16.3 %collective-permute-start.6 = (bf16[192,1536]{1,0:T(8,128)(2,1)S(1)}, bf16[192,1536]{1,0:T(8,128)(2,1)S(1)}, u32[]{:S(2)}, u32[]{:S(2)}) collective-permute-start(bf16[192,1536]{1,0:T(8,128)(2,1)S(1)} %shard_map.59), channel_id=1, source_target_pairs={{0,8},{8,0},{16,24},{24,16},{1,9},{9,1},{17,25},{25,17},{2,10},{10... | collective-permute-start | bytes 1769480 | tf_op jit(solution)/shard_map/ppermute | solution.py:342
  59.5 24.5 %collective-permute-start.10 = (bf16[192,1536]{1,0:T(8,128)(2,1)S(1)}, bf16[192,1536]{1,0:T(8,128)(2,1)S(1)}, u32[]{:S(2)}, u32[]{:S(2)}) collective-permute-start(bf16[192,1536]{1,0:T(8,128)(2,1)S(1)} %shard_map.65), channel_id=1, source_target_pairs={{0,8},{8,0},{16,24},{24,16},{1,9},{9,1},{17,25},{25,17},{2,10},{10... | collective-permute-start | bytes 1769480 | tf_op jit(solution)/shard_map/ppermute | solution.py:342
  61.3 23.3 %collective-permute-start.11 = (bf16[192,1536]{1,0:T(8,128)(2,1)S(1)}, bf16[192,1536]{1,0:T(8,128)(2,1)S(1)}, u32[]{:S(2)}, u32[]{:S(2)}) collective-permute-start(bf16[192,1536]{1,0:T(8,128)(2,1)S(1)} %shard_map.66), channel_id=1, source_target_pairs={{0,16},{8,24},{16,0},{24,8},{1,17},{9,25},{17,1},{25,9},{2,18},{10... | collective-permute-start | bytes 1769480 | tf_op jit(solution)/shard_map/ppermute | solution.py:342
  62.0 28.1 %collective-permute-start.7 = (bf16[192,1536]{1,0:T(8,128)(2,1)S(1)}, bf16[192,1536]{1,0:T(8,128)(2,1)S(1)}, u32[]{:S(2)}, u32[]{:S(2)}) collective-permute-start(bf16[192,1536]{1,0:T(8,128)(2,1)S(1)} %shard_map.60), channel_id=1, source_target_pairs={{0,16},{8,24},{16,0},{24,8},{1,17},{9,25},{17,1},{25,9},{2,18},{10... | collective-permute-start | bytes 1769480 | tf_op jit(solution)/shard_map/ppermute | solution.py:342
  72.4 30.1 %collective-permute-start.8 = (bf16[192,768]{1,0:T(8,128)(2,1)S(1)}, bf16[192,768]{1,0:T(8,128)(2,1)S(1)}, u32[]{:S(2)}, u32[]{:S(2)}) collective-permute-start(bf16[192,768]{1,0:T(8,128)(2,1)S(1)} %shard_map.62), channel_id=1, source_target_pairs={{0,16},{8,24},{16,0},{24,8},{1,17},{9,25},{17,1},{25,9},{2,18},{10... | collective-permute-start | bytes 884744 | tf_op jit(solution)/shard_map/ppermute | solution.py:342
  84.5 17.2 %collective-permute-start.12 = (bf16[192,768]{1,0:T(8,128)(2,1)S(1)}, bf16[192,768]{1,0:T(8,128)(2,1)S(1)}, u32[]{:S(2)}, u32[]{:S(2)}) collective-permute-start(bf16[192,768]{1,0:T(8,128)(2,1)S(1)} %shard_map.68), channel_id=1, source_target_pairs={{0,16},{8,24},{16,0},{24,8},{1,17},{9,25},{17,1},{25,9},{2,18},{10... | collective-permute-start | bytes 884744 | tf_op jit(solution)/shard_map/ppermute | solution.py:342
  85.0 16.7 %collective-permute-start.13 = (bf16[192,768]{1,0:T(8,128)(2,1)S(1)}, bf16[192,768]{1,0:T(8,128)(2,1)S(1)}, u32[]{:S(2)}, u32[]{:S(2)}) collective-permute-start(bf16[192,768]{1,0:T(8,128)(2,1)S(1)} %shard_map.69), channel_id=1, source_target_pairs={{0,8},{8,0},{16,24},{24,16},{1,9},{9,1},{17,25},{25,17},{2,10},{10... | collective-permute-start | bytes 884744 | tf_op jit(solution)/shard_map/ppermute | solution.py:342
  90.6 12.0 %collective-permute-start.9 = (bf16[192,768]{1,0:T(8,128)(2,1)S(1)}, bf16[192,768]{1,0:T(8,128)(2,1)S(1)}, u32[]{:S(2)}, u32[]{:S(2)}) collective-permute-start(bf16[192,768]{1,0:T(8,128)(2,1)S(1)} %shard_map.63), channel_id=1, source_target_pairs={{0,8},{8,0},{16,24},{24,16},{1,9},{9,1},{17,25},{25,17},{2,10},{10... | collective-permute-start | bytes 884744 | tf_op jit(solution)/shard_map/ppermute | solution.py:342

commit v5 on v4

--- a/solution.py
+++ b/solution.py
@@ -28,10 +28,8 @@
     parity = lax.axis_index("frame") % 2
 
     def packed(key, value, frame):
-        return jnp.concatenate(
-            [lax.dynamic_slice_in_dim(array, frame * FRAME_TOK, FRAME_TOK, 0) for array in (key, value)],
-            axis=0,
-        )
+        rows = [lax.dynamic_slice_in_dim(array, frame * FRAME_TOK, FRAME_TOK, 0) for array in (key, value)]
+        return jnp.concatenate(rows, axis=0)
 
     edge = packed(key_tok, value_tok, parity)
     edge, key_tok, value_tok = lax.optimization_barrier((edge, key_tok, value_tok))
@@ -201,12 +199,18 @@
     return attend_step(table, query_tok, [second], {"I": state}, cases, closed={"I": result})[1]["I"]
 
 
-def attend_edge(table, query_tok, state, second, third, result):
+def attend_edge(table, query_tok, state, second, result):
     cases = [
-        (lambda span, link, far_link: (span >= 3) & link, [("E", [0, 1])], "E"),
+        (lambda span, link, far_link: (span >= 3) & link, [("E", [0])], ""),
         (lambda span, link, far_link: (span == 2) & link, [("E", [0])], "E"),
     ]
-    return attend_step(table, query_tok, [second, third], {"E": state}, cases, closed={"E": result})[1]["E"]
+    state, result = attend_step(table, query_tok, [second], {"E": state}, cases, closed={"E": result})
+    return state["E"], result["E"]
+
+
+def attend_last(table, query_tok, state, third, result):
+    cases = [(lambda span, link, far_link: (span >= 3) & link, [("E", [0])], "E")]
+    return attend_step(table, query_tok, [third], {"E": state}, cases, closed={"E": result})[1]["E"]
 
 
 def project(attended, part, parts, out_weight, slots, received):
@@ -357,7 +361,8 @@
             held[role][part] = kept
 
     halve("I", 0)
-    attended["E"] = attend_edge(table, query_tok, state["E"], second, third, attended["E"])
+    state_e, attended["E"] = attend_edge(table, query_tok, state["E"], second, attended["E"])
+    attended["E"] = attend_last(table, query_tok, state_e, third, attended["E"])
     for stage in range(bits):
         halve("E", stage)
         if stage + 1 < bits:

time: 104 us -> 93.5 us (0.90)
  the two profiles are of different devices: /device:TPU:20 before, /device:TPU:22 now
where the time goes in v5:
time: 93.5 us; the launch traced here: 93.3 us
  waiting for transfers between devices  41.1 us (44%)
  Pallas kernels  34.4 us (37%)
  starting transfers between devices  14.5 us (16%)
  local copies, waits for them, and re-layouts  1.45 us (2%)
  other arithmetic  1.25 us (1%)
    ppermute x8, waiting for transfers between devices, exchange(): lax.ppermute(value, 'head', [(i, i ^ 1 << bit) for i in range(groups)])  27.3 us
    pallas_call x6, Pallas kernels, attend_step(): pl.pallas_call(kernel, out_shape=tuple(shapes), in_specs=[SMEM] + [VMEM]...  27 us
    ppermute x3, waiting for transfers between devices, across(): return lax.ppermute(value, 'frame', pairs + [(b, a) for a, b in pairs])  13.8 us
    ppermute x3, starting transfers between devices, across(): return lax.ppermute(value, 'frame', pairs + [(b, a) for a, b in pairs])  7.59 us
    ppermute x8, starting transfers between devices, exchange(): lax.ppermute(value, 'head', [(i, i ^ 1 << bit) for i in range(groups)])  4.98 us
    pallas_call x8, Pallas kernels, project(): pl.pallas_call(kernel, out_shape=jax.ShapeDtypeStruct((rows, len(slots) *...  4.33 us
    ppermute x3, starting transfers between devices, swap(): return lax.ppermute(value, 'frame', [(i, i ^ 1) for i in range(frames)])  1.94 us
  transfers between devices with their start and end apart: 14, of which 7 were waited for; matrix products, arithmetic and copies ran while one was open for 0% of the time, Pallas kernels for 36%

profile of v5, /device:TPU:22, one launch (start us, length us, event | category | flops | bytes accessed | tf_op | source)
XLA Modules:
  0.0 93.3 jit_solution(12513698668050086473)
XLA Ops:
  0.0 1.3 %constant_dynamic-slice_fusion.2 = (bf16[384,768]{1,0:T(8,128)(2,1)S(1)}, bf16[384,768]{1,0:T(8,128)(2,1)S(1)}) fusion(bf16[768,768]{1,0:T(8,128)(2,1)} %param.7, s32[]{:T(128)S(6)} %select_n.27, bf16[768,768]{1,0:T(8,128)(2,1)} %param.6), kind=kLoop, calls=%fused_computation.4 | loop fusion | bytes 2359300 | tf_op jit(solution)/shard_map/dynamic_slice | solution.py:31
  1.3 0.0 copy-start.1
  1.3 1.1 %pad_maximum_fusion.refs_0_ = bf16[768,768]{1,0:T(8,128)(2,1)} fusion(bf16[384,768]{1,0:T(8,128)(2,1)S(1)} %get-tuple-element.59, bf16[384,768]{1,0:T(8,128)(2,1)S(1)} %get-tuple-element.60), kind=kLoop, calls=%fused_computation | loop fusion | flops 2359296 | bytes 2359296 | tf_op jit(solution)/shard_map/concatenate | solution.py:32
  2.4 2.0 %collective-permute-start.3 = (bf16[768,768]{1,0:T(8,128)(2,1)}, bf16[768,768]{1,0:T(8,128)(2,1)}, u32[]{:S(2)}, u32[]{:S(2)}) collective-permute-start(bf16[768,768]{1,0:T(8,128)(2,1)} %pad_maximum_fusion.refs_0_), channel_id=1, source_target_pairs={{1,2},{3,4},{5,6},{2,1},{4,3},{6,5},{9,10},{11,12},{13,14},{10,9},... | collective-permute-start | bytes 3538952 | tf_op jit(solution)/shard_map/ppermute | solution.py:331
  4.6 0.0 copy-start.3
  4.6 0.0 copy-start
  4.6 0.1 pad_maximum_fusion.1.refs_1_
  4.7 1.7 %collective-permute-start = (bf16[768,768]{1,0:T(8,128)(2,1)S(1)}, bf16[768,768]{1,0:T(8,128)(2,1)}, u32[]{:S(2)}, u32[]{:S(2)}) collective-permute-start(bf16[768,768]{1,0:T(8,128)(2,1)S(1)} %pad_maximum_fusion.1.refs_1_), channel_id=1, source_target_pairs={{0,1},{1,0},{2,3},{3,2},{4,5},{5,4},{6,7},{7,6},{8,9},{9,8},{10,11... | collective-permute-start | bytes 3538952 | tf_op jit(solution)/shard_map/ppermute | solution.py:327
  6.5 0.1 collective-permute-start.5
  6.6 13.8 %collective-permute-done.3.refs_0_ = bf16[768,768]{1,0:T(8,128)(2,1)} collective-permute-done((bf16[768,768]{1,0:T(8,128)(2,1)}, bf16[768,768]{1,0:T(8,128)(2,1)}, u32[]{:S(2)}, u32[]{:S(2)}) %collective-permute-start.3) | collective-permute-done | bytes 1179680 | tf_op jit(solution)/shard_map/ppermute | solution.py:331
  20.4 0.1 collective-permute-start.4
  20.5 2.3 %collective-permute-start.2 = (bf16[768,768]{1,0:T(8,128)(2,1)S(1)}, bf16[768,768]{1,0:T(8,128)(2,1)S(1)}, u32[]{:S(2)}, u32[]{:S(2)}) collective-permute-start(bf16[768,768]{1,0:T(8,128)(2,1)S(1)} %pad_maximum_fusion.1.refs_1_), channel_id=1, source_target_pairs={{1,2},{3,4},{5,6},{2,1},{4,3},{6,5},{9,10},{11,12},{13,14},{10,9},... | collective-permute-start | bytes 3538952 | tf_op jit(solution)/shard_map/ppermute | solution.py:331
  22.9 0.0 collective-permute-done.refs_2_
  22.9 3.2 %collective-permute-start.1 = (bf16[768,768]{1,0:T(8,128)(2,1)}, bf16[768,768]{1,0:T(8,128)(2,1)}, u32[]{:S(2)}, u32[]{:S(2)}) collective-permute-start(bf16[768,768]{1,0:T(8,128)(2,1)} %collective-permute-done.refs_2_), channel_id=1, source_target_pairs={{1,2},{3,4},{5,6},{2,1},{4,3},{6,5},{9,10},{11,12},{13,14},{10,9},... | collective-permute-start | bytes 3538952 | tf_op jit(solution)/shard_map/ppermute | solution.py:331
  26.1 0.1 pad_add_fusion.table_ref
  26.2 11.7 %shard_map.55 = (f32[384,768]{1,0:T(8,128)S(1)}, f32[384,768]{1,0:T(8,128)S(1)}, f32[384,768]{1,0:T(8,128)S(1)}, f32[384,768]{1,0:T(8,128)S(1)}, f32[384,768]{1,0:T(8,128)S(1)}, /*index=5*/f32[384,768]{1,0:T(8,128)S(1)}) custom-call(s32[9]{0:T(128)S(1)} %pad_add_fusion.table_ref, bf16[768,768]{1,0:T(8,128)(2,1)S(1)} %copy-done, ...), custom_call_target="tpu_custom_call" | custom-call | tf_op jit(solution)/shard_map/pallas_call | solution.py:150
  37.9 0.0 slice-start
  37.9 4.4 %shard_map.56 = (f32[384,768]{1,0:T(8,128)S(1)}, f32[384,768]{1,0:T(8,128)S(1)}, f32[384,768]{1,0:T(8,128)S(1)}, f32[384,768]{1,0:T(8,128)S(1)}, f32[384,768]{1,0:T(8,128)S(1)}, /*index=5*/f32[384,768]{1,0:T(8,128)S(1)}) custom-call(s32[9]{0:T(128)S(1)} %pad_add_fusion.table_ref, ...), custom_call_target="tpu_custom_call", output_to_operand_aliasing={{0}: (3, {}), {1}: (4, {}), {2}: (5, {}), {3}: (6, {}), {4}... | custom-call | tf_op jit(solution)/shard_map/pallas_call | solution.py:150
  42.3 0.0 slice-start.1
  42.3 3.2 %shard_map.57 = (f32[384,768]{1,0:T(8,128)S(1)}, f32[384,768]{1,0:T(8,128)S(1)}, f32[384,768]{1,0:T(8,128)S(1)}, f32[384,768]{1,0:T(8,128)S(1)}, f32[384,768]{1,...) custom-call(s32[9]{0:T(128)S(1)} %pad_add_fusion.table_ref, ...), custom_call_target="tpu_custom_call", output_to_operand_aliasing={{0}: (3, {}), {1}: (4, {}), {2}: (5, {}), {3}: (6, {}), {4}... | custom-call | tf_op jit(solution)/shard_map/pallas_call | solution.py:150
  45.5 2.0 %shard_map.65.left = bf16[384,768]{1,0:T(8,128)(2,1)S(1)} custom-call(s32[9]{0:T(128)S(1)} %pad_add_fusion.table_ref, bf16[768,768]{1,0:T(8,128)(2,1)S(1)} %copy-done, bf16[768,768]{1,0:T(8,128)(2,1)S(1)} %collective-permute-done.2.refs_0_, f32[384,768]{1,0:T(8,128)S(1)} %get-tuple-element.55.refs_1_, ...), custom_call_target="tpu_custom_call", output_to_operand_aliasing={{}: (6, {})} | custom-call | tf_op jit(solution)/shard_map/pallas_call | solution.py:150
  47.5 0.6 shard_map.67
  48.2 0.7 shard_map.66
  48.9 2.7 %collective-permute-start.10 = (bf16[192,1536]{1,0:T(8,128)(2,1)S(1)}, bf16[192,1536]{1,0:T(8,128)(2,1)S(1)}, u32[]{:S(2)}, u32[]{:S(2)}) collective-permute-start(bf16[192,1536]{1,0:T(8,128)(2,1)S(1)} %shard_map.66), channel_id=1, source_target_pairs={{0,8},{8,0},{16,24},{24,16},{1,9},{9,1},{17,25},{25,17},{2,10},{10... | collective-permute-start | bytes 1769480 | tf_op jit(solution)/shard_map/ppermute | solution.py:346
  51.6 3.0 %shard_map.58 = (f32[384,768]{1,0:T(8,128)S(1)}, f32[384,768]{1,0:T(8,128)S(1)}, f32[384,768]{1,0:T(8,128)S(1)}, bf16[384,768]{1,0:T(8,128)(2,1)S(1)}) custom-call(s32[9]{0:T(128)S(1)} %pad_add_fusion.table_ref, bf16[768,768]{1,0:T(8,128)(2,1)S(1)} %copy-done, ...), custom_call_target="tpu_custom_call", output_to_operand_aliasing={{0}: (3, {}), {1}: (4, {}), {2}: (5, {}), {3}: (6, {})} | custom-call | tf_op jit(solution)/shard_map/pallas_call | solution.py:150
  54.5 2.8 %shard_map.59.left = bf16[384,768]{1,0:T(8,128)(2,1)S(1)} custom-call(s32[9]{0:T(128)S(1)} %pad_add_fusion.table_ref, bf16[768,768]{1,0:T(8,128)(2,1)S(1)} %copy-done, bf16[768,768]{1,0:T(8,128)(2,1)} %collective-permute-done.1.refs_0_, f32[384,768]{1,0:T(8,128)S(1)} %get-tuple-element.51.refs_1_, ...), custom_call_target="tpu_custom_call", output_to_operand_aliasing={{}: (6, {})} | custom-call | tf_op jit(solution)/shard_map/pallas_call | solution.py:150
  57.3 0.7 shard_map.60
  58.0 0.1 collective-permute-start.6
  58.1 0.6 shard_map.61
  58.7 0.9 collective-permute-start.7
  59.6 6.1 %collective-permute-done.10.rest_0_ = bf16[192,1536]{1,0:T(8,128)(2,1)S(1)} collective-permute-done((bf16[192,1536]{1,0:T(8,128)(2,1)S(1)}, bf16[192,1536]{1,0:T(8,128)(2,1)S(1)}, u32[]{:S(2)}, u32[]{:S(2)}) %collective-permute-start.10) | collective-permute-done | bytes 589856 | tf_op jit(solution)/shard_map/ppermute | solution.py:346
  65.7 0.4 shard_map.69
  66.2 0.1 collective-permute-start.12
  66.3 1.5 %collective-permute-done.11.rest_1_.rest_0_ = bf16[192,1536]{1,0:T(8,128)(2,1)S(1)} collective-permute-done((bf16[192,1536]{1,0:T(8,128)(2,1)S(1)}, bf16[192,1536]{1,0:T(8,128)(2,1)S(1)}, u32[]{:S(2)}, u32[]{:S(2)}) %collective-permute-start.11) | collective-permute-done | bytes 589856 | tf_op jit(solution)/shard_map/ppermute | solution.py:346
  67.8 0.4 shard_map.70
  68.2 0.6 collective-permute-start.13
  68.8 9.6 %collective-permute-done.6.rest_0_ = bf16[192,1536]{1,0:T(8,128)(2,1)S(1)} collective-permute-done((bf16[192,1536]{1,0:T(8,128)(2,1)S(1)}, bf16[192,1536]{1,0:T(8,128)(2,1)S(1)}, u32[]{:S(2)}, u32[]{:S(2)}) %collective-permute-start.6) | collective-permute-done | bytes 589856 | tf_op jit(solution)/shard_map/ppermute | solution.py:346
  78.4 0.4 shard_map.63
  78.8 0.1 collective-permute-start.8
  78.9 1.5 %collective-permute-done.7.rest_1_.rest_0_ = bf16[192,1536]{1,0:T(8,128)(2,1)S(1)} collective-permute-done((bf16[192,1536]{1,0:T(8,128)(2,1)S(1)}, bf16[192,1536]{1,0:T(8,128)(2,1)S(1)}, u32[]{:S(2)}, u32[]{:S(2)}) %collective-permute-start.7) | collective-permute-done | bytes 589856 | tf_op jit(solution)/shard_map/ppermute | solution.py:346
  80.4 0.4 shard_map.64
  80.8 0.6 collective-permute-start.9
  81.4 0.7 shard_map.68.terms
  82.1 0.7 shard_map.62.terms
  82.7 4.0 %collective-permute-done.12.rest_0_ = bf16[192,768]{1,0:T(8,128)(2,1)S(1)} collective-permute-done((bf16[192,768]{1,0:T(8,128)(2,1)S(1)}, bf16[192,768]{1,0:T(8,128)(2,1)S(1)}, u32[]{:S(2)}, u32[]{:S(2)}) %collective-permute-start.12) | collective-permute-done | bytes 294944 | tf_op jit(solution)/shard_map/ppermute | solution.py:346
  86.7 0.9 shard_map.71.rest_2_
  87.6 4.6 %collective-permute-done.8.rest_0_ = bf16[192,768]{1,0:T(8,128)(2,1)S(1)} collective-permute-done((bf16[192,768]{1,0:T(8,128)(2,1)S(1)}, bf16[192,768]{1,0:T(8,128)(2,1)S(1)}, u32[]{:S(2)}, u32[]{:S(2)}) %collective-permute-start.8) | collective-permute-done | bytes 294944 | tf_op jit(solution)/shard_map/ppermute | solution.py:346
  92.2 0.9 shard_map.72
  (17 shorter events, 0.1 us)
Async XLA Ops:
  1.3 3.2 %copy-start.1 = (bf16[768,768]{1,0:T(8,128)(2,1)S(1)}, bf16[768,768]{1,0:T(8,128)(2,1)}, u32[]{:S(2)}) copy-start(bf16[768,768]{1,0:T(8,128)(2,1)} %param.6) | copy-start | bytes 3538948
  2.4 2.1 %copy-start.2 = (bf16[768,768]{1,0:T(8,128)(2,1)S(1)}, bf16[768,768]{1,0:T(8,128)(2,1)}, u32[]{:S(2)}) copy-start(bf16[768,768]{1,0:T(8,128)(2,1)} %param.7) | copy-start | bytes 3538948
  2.4 18.0 %collective-permute-start.3 = (bf16[768,768]{1,0:T(8,128)(2,1)}, bf16[768,768]{1,0:T(8,128)(2,1)}, u32[]{:S(2)}, u32[]{:S(2)}) collective-permute-start(bf16[768,768]{1,0:T(8,128)(2,1)} %pad_maximum_fusion.refs_0_), channel_id=1, source_target_pairs={{1,2},{3,4},{5,6},{2,1},{4,3},{6,5},{9,10},{11,12},{13,14},{10,9},... | collective-permute-start | bytes 3538952 | tf_op jit(solution)/shard_map/ppermute | solution.py:331
  4.6 21.5 %copy-start.3 = (s32[6]{0:T(128)S(1)}, s32[6]{0:T(128)}, u32[]{:S(2)}) copy-start(s32[6]{0:T(128)} %param.8) | copy-start | bytes 76
  4.6 21.6 %copy-start = (bf16[768,768]{1,0:T(8,128)(2,1)S(1)}, bf16[768,768]{1,0:T(8,128)(2,1)}, u32[]{:S(2)}) copy-start(bf16[768,768]{1,0:T(8,128)(2,1)} %query.11) | copy-start | bytes 3538948
  4.7 18.1 %collective-permute-start = (bf16[768,768]{1,0:T(8,128)(2,1)S(1)}, bf16[768,768]{1,0:T(8,128)(2,1)}, u32[]{:S(2)}, u32[]{:S(2)}) collective-permute-start(bf16[768,768]{1,0:T(8,128)(2,1)S(1)} %pad_maximum_fusion.1.refs_1_), channel_id=1, source_target_pairs={{0,1},{1,0},{2,3},{3,2},{4,5},{5,4},{6,7},{7,6},{8,9},{9,8},{10,11... | collective-permute-start | bytes 3538952 | tf_op jit(solution)/shard_map/ppermute | solution.py:327
  6.5 19.7 %collective-permute-start.5 = (bf16[768,768]{1,0:T(8,128)(2,1)}, bf16[768,768]{1,0:T(8,128)(2,1)}, u32[]{:S(2)}, u32[]{:S(2)}) collective-permute-start(bf16[768,768]{1,0:T(8,128)(2,1)} %pad_maximum_fusion.refs_0_), channel_id=1, source_target_pairs={{0,1},{1,0},{2,3},{3,2},{4,5},{5,4},{6,7},{7,6},{8,9},{9,8},{10,11... | collective-permute-start | bytes 3538952 | tf_op jit(solution)/shard_map/ppermute | solution.py:327
  20.4 21.9 %collective-permute-start.4 = (bf16[768,768]{1,0:T(8,128)(2,1)}, bf16[768,768]{1,0:T(8,128)(2,1)}, u32[]{:S(2)}, u32[]{:S(2)}) collective-permute-start(bf16[768,768]{1,0:T(8,128)(2,1)} %collective-permute-done.3.refs_0_), channel_id=1, source_target_pairs={{0,1},{1,0},{2,3},{3,2},{4,5},{5,4},{6,7},{7,6},{8,9},{9,8},{10,11... | collective-permute-start | bytes 3538952 | tf_op jit(solution)/shard_map/ppermute | solution.py:327
  20.5 25.0 %collective-permute-start.2 = (bf16[768,768]{1,0:T(8,128)(2,1)S(1)}, bf16[768,768]{1,0:T(8,128)(2,1)S(1)}, u32[]{:S(2)}, u32[]{:S(2)}) collective-permute-start(bf16[768,768]{1,0:T(8,128)(2,1)S(1)} %pad_maximum_fusion.1.refs_1_), channel_id=1, source_target_pairs={{1,2},{3,4},{5,6},{2,1},{4,3},{6,5},{9,10},{11,12},{13,14},{10,9},... | collective-permute-start | bytes 3538952 | tf_op jit(solution)/shard_map/ppermute | solution.py:331
  22.9 31.7 %collective-permute-start.1 = (bf16[768,768]{1,0:T(8,128)(2,1)}, bf16[768,768]{1,0:T(8,128)(2,1)}, u32[]{:S(2)}, u32[]{:S(2)}) collective-permute-start(bf16[768,768]{1,0:T(8,128)(2,1)} %collective-permute-done.refs_2_), channel_id=1, source_target_pairs={{1,2},{3,4},{5,6},{2,1},{4,3},{6,5},{9,10},{11,12},{13,14},{10,9},... | collective-permute-start | bytes 3538952 | tf_op jit(solution)/shard_map/ppermute | solution.py:331
  37.9 9.6 %slice-start = ((s8[4718592]{0:T(1024)(128)(4,1)}), s8[4194304]{0:T(1024)(128)(4,1)S(1)}, s32[]{:S(2)}) async-start(s8[4718592]{0:T(1024)(128)(4,1)} %bitcast.3), calls=%async_computation | async-start | bytes 8388608
  42.3 5.2 %slice-start.1 = ((s8[4718592]{0:T(1024)(128)(4,1)}), s8[524288]{0:T(1024)(128)(4,1)S(1)}, s32[]{:S(2)}) async-start(s8[4718592]{0:T(1024)(128)(4,1)} %bitcast.3), calls=%async_computation.1 | async-start | bytes 1048576
  48.9 16.9 %collective-permute-start.10 = (bf16[192,1536]{1,0:T(8,128)(2,1)S(1)}, bf16[192,1536]{1,0:T(8,128)(2,1)S(1)}, u32[]{:S(2)}, u32[]{:S(2)}) collective-permute-start(bf16[192,1536]{1,0:T(8,128)(2,1)S(1)} %shard_map.66), channel_id=1, source_target_pairs={{0,8},{8,0},{16,24},{24,16},{1,9},{9,1},{17,25},{25,17},{2,10},{10... | collective-permute-start | bytes 1769480 | tf_op jit(solution)/shard_map/ppermute | solution.py:346
  51.6 16.2 %collective-permute-start.11 = (bf16[192,1536]{1,0:T(8,128)(2,1)S(1)}, bf16[192,1536]{1,0:T(8,128)(2,1)S(1)}, u32[]{:S(2)}, u32[]{:S(2)}) collective-permute-start(bf16[192,1536]{1,0:T(8,128)(2,1)S(1)} %shard_map.67), channel_id=1, source_target_pairs={{0,16},{8,24},{16,0},{24,8},{1,17},{9,25},{17,1},{25,9},{2,18},{10... | collective-permute-start | bytes 1769480 | tf_op jit(solution)/shard_map/ppermute | solution.py:346
  58.0 20.4 %collective-permute-start.6 = (bf16[192,1536]{1,0:T(8,128)(2,1)S(1)}, bf16[192,1536]{1,0:T(8,128)(2,1)S(1)}, u32[]{:S(2)}, u32[]{:S(2)}) collective-permute-start(bf16[192,1536]{1,0:T(8,128)(2,1)S(1)} %shard_map.60), channel_id=1, source_target_pairs={{0,8},{8,0},{16,24},{24,16},{1,9},{9,1},{17,25},{25,17},{2,10},{10... | collective-permute-start | bytes 1769480 | tf_op jit(solution)/shard_map/ppermute | solution.py:346
  58.7 21.7 %collective-permute-start.7 = (bf16[192,1536]{1,0:T(8,128)(2,1)S(1)}, bf16[192,1536]{1,0:T(8,128)(2,1)S(1)}, u32[]{:S(2)}, u32[]{:S(2)}) collective-permute-start(bf16[192,1536]{1,0:T(8,128)(2,1)S(1)} %shard_map.61), channel_id=1, source_target_pairs={{0,16},{8,24},{16,0},{24,8},{1,17},{9,25},{17,1},{25,9},{2,18},{10... | collective-permute-start | bytes 1769480 | tf_op jit(solution)/shard_map/ppermute | solution.py:346
  66.2 20.6 %collective-permute-start.12 = (bf16[192,768]{1,0:T(8,128)(2,1)S(1)}, bf16[192,768]{1,0:T(8,128)(2,1)S(1)}, u32[]{:S(2)}, u32[]{:S(2)}) collective-permute-start(bf16[192,768]{1,0:T(8,128)(2,1)S(1)} %shard_map.69), channel_id=1, source_target_pairs={{0,16},{8,24},{16,0},{24,8},{1,17},{9,25},{17,1},{25,9},{2,18},{10... | collective-permute-start | bytes 884744 | tf_op jit(solution)/shard_map/ppermute | solution.py:346
  68.2 18.5 %collective-permute-start.13 = (bf16[192,768]{1,0:T(8,128)(2,1)S(1)}, bf16[192,768]{1,0:T(8,128)(2,1)S(1)}, u32[]{:S(2)}, u32[]{:S(2)}) collective-permute-start(bf16[192,768]{1,0:T(8,128)(2,1)S(1)} %shard_map.70), channel_id=1, source_target_pairs={{0,8},{8,0},{16,24},{24,16},{1,9},{9,1},{17,25},{25,17},{2,10},{10... | collective-permute-start | bytes 884744 | tf_op jit(solution)/shard_map/ppermute | solution.py:346
  78.8 13.4 %collective-permute-start.8 = (bf16[192,768]{1,0:T(8,128)(2,1)S(1)}, bf16[192,768]{1,0:T(8,128)(2,1)S(1)}, u32[]{:S(2)}, u32[]{:S(2)}) collective-permute-start(bf16[192,768]{1,0:T(8,128)(2,1)S(1)} %shard_map.63), channel_id=1, source_target_pairs={{0,16},{8,24},{16,0},{24,8},{1,17},{9,25},{17,1},{25,9},{2,18},{10... | collective-permute-start | bytes 884744 | tf_op jit(solution)/shard_map/ppermute | solution.py:346
  80.8 11.4 %collective-permute-start.9 = (bf16[192,768]{1,0:T(8,128)(2,1)S(1)}, bf16[192,768]{1,0:T(8,128)(2,1)S(1)}, u32[]{:S(2)}, u32[]{:S(2)}) collective-permute-start(bf16[192,768]{1,0:T(8,128)(2,1)S(1)} %shard_map.64), channel_id=1, source_target_pairs={{0,8},{8,0},{16,24},{24,16},{1,9},{9,1},{17,25},{25,17},{2,10},{10... | collective-permute-start | bytes 884744 | tf_op jit(solution)/shard_map/ppermute | solution.py:346

commit v6 on v5

--- a/solution.py
+++ b/solution.py
@@ -36,14 +36,15 @@
     return edge, packed(key_tok, value_tok, 1 - parity)
 
 
-def attend_step(table, query_tok, sources, states, cases, first=False, closed=None):
+def attend_step(head_span, query_tok, sources, states, cases, first=False, closed=None):
     heads = query_tok.shape[1] // HD
+    frames = lax.axis_size("frame")
     names = list(states)
     closed = closed or {}
     scale = LOG2E / HD**0.5
     keep = first or any(items and not close for _, items, close in cases)
 
-    def kernel(table_ref, query, *refs):
+    def kernel(span_ref, query, *refs):
         refs = list(refs)
         chosen = refs.pop()
         loaded = [refs.pop(0) for _ in sources]
@@ -54,7 +55,10 @@
         outs = {role: [refs.pop(0) for _ in range(3)] for role in names} if keep else {}
         results = {role: refs.pop(0) for role in closed}
         reads = outs if keep and not first else olds
-        parity, link, far_link = table_ref[0], table_ref[1] > 0, table_ref[2] > 0
+        seat = lax.axis_index("frame")
+        parity = seat % 2
+        link = ((parity == 0) & (seat > 0)) | ((parity == 1) & (seat < frames - 1))
+        far_link = ((parity == 0) & (seat < frames - 2)) | ((parity == 1) & (seat > 1))
         starts = {"E": parity * FRAME_TOK, "I": (1 - parity) * FRAME_TOK}
 
         def wide(tops, times):
@@ -107,7 +111,7 @@
         def collect(condition):
             def add(head, count):
                 chosen[count] = head
-                return count + condition(table_ref[3 + head], link, far_link).astype(jnp.int32)
+                return count + condition(span_ref[head], link, far_link).astype(jnp.int32)
 
             return lax.fori_loop(0, heads, add, jnp.int32(0))
 
@@ -131,7 +135,7 @@
 
                 lax.fori_loop(0, count, plain, 0)
 
-    operands = [table, query_tok, *sources]
+    operands = [head_span, query_tok, *sources]
     shapes = []
     aliases = {}
     if not first:
@@ -161,7 +165,7 @@
     return new_states, {role: out.pop(0) for role in closed}
 
 
-def attend_chip(table, query_tok, edge, inner, partner_inner, partner_edge):
+def attend_chip(head_span, query_tok, edge, inner, partner_inner, partner_edge):
     order = {"E": [0, 1, 2, 3], "I": [1, 0, 2, 3]}
     reach = {"E": [1, 2, 3, 4], "I": [1, 3, 4, 4]}
     cases = [
@@ -173,44 +177,44 @@
         for limit in range(4)
     ]
     return attend_step(
-        table, query_tok, [edge, inner, partner_inner, partner_edge], {"E": None, "I": None}, cases, first=True
+        head_span, query_tok, [edge, inner, partner_inner, partner_edge], {"E": None, "I": None}, cases, first=True
     )[0]
 
 
-def attend_near(table, query_tok, state, near):
+def attend_near(head_span, query_tok, state, near):
     cases = [
         (lambda span, link, far_link: (span >= 2) & link, [("E", [0]), ("I", [0])], ""),
         (lambda span, link, far_link: (span == 1) & link, [("E", [0])], ""),
     ]
-    return attend_step(table, query_tok, [near], state, cases)[0]
-
-
-def attend_beyond(table, query_tok, state, beyond):
+    return attend_step(head_span, query_tok, [near], state, cases)[0]
+
+
+def attend_beyond(head_span, query_tok, state, beyond):
     cases = [
         (lambda span, link, far_link: (span >= 3) & far_link, [("I", [0])], ""),
         (lambda span, link, far_link: (span < 3) | jnp.logical_not(link), [], "I"),
         (lambda span, link, far_link: (span < 2) | jnp.logical_not(link), [], "E"),
     ]
-    return attend_step(table, query_tok, [beyond], state, cases, closed={"I": None, "E": None})
-
-
-def attend_inner(table, query_tok, state, second, result):
+    return attend_step(head_span, query_tok, [beyond], state, cases, closed={"I": None, "E": None})
+
+
+def attend_inner(head_span, query_tok, state, second, result):
     cases = [(lambda span, link, far_link: (span >= 3) & link, [("I", [0])], "I")]
-    return attend_step(table, query_tok, [second], {"I": state}, cases, closed={"I": result})[1]["I"]
-
-
-def attend_edge(table, query_tok, state, second, result):
+    return attend_step(head_span, query_tok, [second], {"I": state}, cases, closed={"I": result})[1]["I"]
+
+
+def attend_edge(head_span, query_tok, state, second, result):
     cases = [
         (lambda span, link, far_link: (span >= 3) & link, [("E", [0])], ""),
         (lambda span, link, far_link: (span == 2) & link, [("E", [0])], "E"),
     ]
-    state, result = attend_step(table, query_tok, [second], {"E": state}, cases, closed={"E": result})
+    state, result = attend_step(head_span, query_tok, [second], {"E": state}, cases, closed={"E": result})
     return state["E"], result["E"]
 
 
-def attend_last(table, query_tok, state, third, result):
+def attend_last(head_span, query_tok, state, third, result):
     cases = [(lambda span, link, far_link: (span >= 3) & link, [("E", [0])], "E")]
-    return attend_step(table, query_tok, [third], {"E": state}, cases, closed={"E": result})[1]["E"]
+    return attend_step(head_span, query_tok, [third], {"E": state}, cases, closed={"E": result})[1]["E"]
 
 
 def project(attended, part, parts, out_weight, slots, received):
@@ -315,13 +319,6 @@
     local_frames = key_tok.shape[0] // FRAME_TOK
     bits = groups.bit_length() - 1
     assert local_frames == 2 and frames % 2 == 0 and groups == 1 << bits and FRAME_TOK % bits == 0
-    seat = lax.axis_index("frame")
-    parity = seat % 2
-    link = jnp.where(parity == 0, seat > 0, seat < frames - 1)
-    far_link = jnp.where(parity == 0, seat < frames - 2, seat > 1)
-    table = jnp.concatenate(
-        [jnp.stack([parity, link, far_link]).astype(jnp.int32), head_span.astype(jnp.int32)]
-    )
 
     def swap(value):
         return lax.ppermute(value, "frame", [(i, i ^ 1) for i in range(frames)])
@@ -336,11 +333,11 @@
     partner_edge = swap(edge)
     second = across(inner)
     third = across(partner_inner)
-    state = attend_chip(table, query_tok, edge, inner, partner_inner, partner_edge)
+    state = attend_chip(head_span, query_tok, edge, inner, partner_inner, partner_edge)
     beyond = swap(near)
-    state = attend_near(table, query_tok, state, near)
-    state, attended = attend_beyond(table, query_tok, state, beyond)
-    attended["I"] = attend_inner(table, query_tok, state["I"], second, attended["I"])
+    state = attend_near(head_span, query_tok, state, near)
+    state, attended = attend_beyond(head_span, query_tok, state, beyond)
+    attended["I"] = attend_inner(head_span, query_tok, state["I"], second, attended["I"])
 
     def exchange(value, bit):
         return lax.ppermute(value, "head", [(i, i ^ (1 << bit)) for i in range(groups)])
@@ -361,8 +358,8 @@
             held[role][part] = kept
 
     halve("I", 0)
-    state_e, attended["E"] = attend_edge(table, query_tok, state["E"], second, attended["E"])
-    attended["E"] = attend_last(table, query_tok, state_e, third, attended["E"])
+    state_e, attended["E"] = attend_edge(head_span, query_tok, state["E"], second, attended["E"])
+    attended["E"] = attend_last(head_span, query_tok, state_e, third, attended["E"])
     for stage in range(bits):
         halve("E", stage)
         if stage + 1 < bits:

time: 93.5 us -> 89 us (0.952)
  Pallas kernels: 34.4 us -> 30.5 us
  local copies, waits for them, and re-layouts: 1.45 us -> 2.65 us
  other arithmetic: 1.25 us -> 0.16 us
    pallas_call x6, Pallas kernels: 27 us -> 23.1 us  [attend_step(): pl.pallas_call(kernel, out_shape=tuple(shapes), in_specs=[SMEM] + [VMEM]...]
    ppermute x3, waiting for transfers between devices: 13.8 us -> 12.3 us  [across(): return lax.ppermute(value, 'frame', pairs + [(b, a) for a, b in pairs])]
    unnamed x12, local copies, waits for them, and re-layouts: 0.04 us -> 1.25 us
    concatenate x2, other arithmetic: 1.17 us -> 0.16 us  [packed(): return jnp.concatenate(rows, axis=0)]
  transfers between devices with their start and end apart: 14 -> 14, of which waited for: 7 -> 7; matrix products, arithmetic and copies ran while one was open for 0% -> 0% of each run, Pallas kernels for 36% -> 33%
where the time goes in v6:
time: 89 us; the launch traced here: 88.8 us
  waiting for transfers between devices  40.4 us (45%)
  Pallas kernels  30.5 us (34%)
  starting transfers between devices  14.6 us (16%)
  local copies, waits for them, and re-layouts  2.65 us (3%)
    ppermute x8, waiting for transfers between devices, exchange(): lax.ppermute(value, 'head', [(i, i ^ 1 << bit) for i in range(groups)])  28 us
    pallas_call x6, Pallas kernels, attend_step(): pl.pallas_call(kernel, out_shape=tuple(shapes), in_specs=[SMEM] + [VMEM]...  23.1 us
    ppermute x3, waiting for transfers between devices, across(): return lax.ppermute(value, 'frame', pairs + [(b, a) for a, b in pairs])  12.3 us
    ppermute x3, starting transfers between devices, across(): return lax.ppermute(value, 'frame', pairs + [(b, a) for a, b in pairs])  7.6 us
    ppermute x8, starting transfers between devices, exchange(): lax.ppermute(value, 'head', [(i, i ^ 1 << bit) for i in range(groups)])  5.01 us
    pallas_call x8, Pallas kernels, project(): pl.pallas_call(kernel, out_shape=jax.ShapeDtypeStruct((rows, len(slots) *...  4.32 us
    ppermute x3, starting transfers between devices, swap(): return lax.ppermute(value, 'frame', [(i, i ^ 1) for i in range(frames)])  1.94 us
  transfers between devices with their start and end apart: 14, of which 7 were waited for; matrix products, arithmetic and copies ran while one was open for 0% of the time, Pallas kernels for 33%

profile of v6, /device:TPU:22, one launch (start us, length us, event | category | flops | bytes accessed | tf_op | source)
XLA Modules:
  0.0 88.8 jit_solution(13417397298811703754)
XLA Ops:
  0.0 1.3 %constant_dynamic-slice_fusion.2 = (bf16[384,768]{1,0:T(8,128)(2,1)S(1)}, bf16[384,768]{1,0:T(8,128)(2,1)S(1)}) fusion(bf16[768,768]{1,0:T(8,128)(2,1)} %param.7, s32[]{:T(128)S(6)} %select_n.16, bf16[768,768]{1,0:T(8,128)(2,1)} %param.6), kind=kLoop, calls=%fused_computation.4 | loop fusion | bytes 2359300 | tf_op jit(solution)/shard_map/dynamic_slice | solution.py:31
  1.3 0.0 copy-start.2
  1.3 0.1 pad_maximum_fusion.refs_0_
  1.4 2.1 %collective-permute-start.3 = (bf16[768,768]{1,0:T(8,128)(2,1)S(1)}, bf16[768,768]{1,0:T(8,128)(2,1)S(1)}, u32[]{:S(2)}, u32[]{:S(2)}) collective-permute-start(bf16[768,768]{1,0:T(8,128)(2,1)S(1)} %pad_maximum_fusion.refs_0_), channel_id=1, source_target_pairs={{1,2},{3,4},{5,6},{2,1},{4,3},{6,5},{9,10},{11,12},{13,14},{10,9},... | collective-permute-start | bytes 3538952 | tf_op jit(solution)/shard_map/ppermute | solution.py:328
  3.5 0.0 copy-start.3
  3.6 1.2 %copy-done.3 = bf16[768,768]{1,0:T(8,128)(2,1)S(1)} copy-done((bf16[768,768]{1,0:T(8,128)(2,1)S(1)}, bf16[768,768]{1,0:T(8,128)(2,1)}, u32[]{:S(2)}) %copy-start.3) | copy-done | bytes 1179672
  4.8 0.0 copy-start
  4.8 0.0 copy-start.1
  4.8 0.1 pad_maximum_fusion.1.refs_1_
  4.9 1.7 %collective-permute-start = (bf16[768,768]{1,0:T(8,128)(2,1)S(1)}, bf16[768,768]{1,0:T(8,128)(2,1)S(1)}, u32[]{:S(2)}, u32[]{:S(2)}) collective-permute-start(bf16[768,768]{1,0:T(8,128)(2,1)S(1)} %pad_maximum_fusion.1.refs_1_), channel_id=1, source_target_pairs={{0,1},{1,0},{2,3},{3,2},{4,5},{5,4},{6,7},{7,6},{8,9},{9,8},{10,11... | collective-permute-start | bytes 3538952 | tf_op jit(solution)/shard_map/ppermute | solution.py:324
  6.7 0.1 collective-permute-start.5
  6.8 12.3 %collective-permute-done.3.refs_0_ = bf16[768,768]{1,0:T(8,128)(2,1)S(1)} collective-permute-done((bf16[768,768]{1,0:T(8,128)(2,1)S(1)}, bf16[768,768]{1,0:T(8,128)(2,1)S(1)}, u32[]{:S(2)}, u32[]{:S(2)}) %collective-permute-start.3) | collective-permute-done | bytes 1179680 | tf_op jit(solution)/shard_map/ppermute | solution.py:328
  19.1 0.1 collective-permute-start.4
  19.2 2.3 %collective-permute-start.2 = (bf16[768,768]{1,0:T(8,128)(2,1)S(1)}, bf16[768,768]{1,0:T(8,128)(2,1)S(1)}, u32[]{:S(2)}, u32[]{:S(2)}) collective-permute-start(bf16[768,768]{1,0:T(8,128)(2,1)S(1)} %pad_maximum_fusion.1.refs_1_), channel_id=1, source_target_pairs={{1,2},{3,4},{5,6},{2,1},{4,3},{6,5},{9,10},{11,12},{13,14},{10,9},... | collective-permute-start | bytes 3538952 | tf_op jit(solution)/shard_map/ppermute | solution.py:328
  21.6 3.2 %collective-permute-start.1 = (bf16[768,768]{1,0:T(8,128)(2,1)S(1)}, bf16[768,768]{1,0:T(8,128)(2,1)S(1)}, u32[]{:S(2)}, u32[]{:S(2)}) collective-permute-start(bf16[768,768]{1,0:T(8,128)(2,1)S(1)} %collective-permute-done.refs_2_), channel_id=1, source_target_pairs={{1,2},{3,4},{5,6},{2,1},{4,3},{6,5},{9,10},{11,12},{13,14},{10,9},... | collective-permute-start | bytes 3538952 | tf_op jit(solution)/shard_map/ppermute | solution.py:328
  24.8 10.3 %shard_map.55 = (f32[384,768]{1,0:T(8,128)S(1)}, f32[384,768]{1,0:T(8,128)S(1)}, f32[384,768]{1,0:T(8,128)S(1)}, f32[384,768]{1,0:T(8,128)S(1)}, f32[384,768]{1,0:T(8,128)S(1)}, /*index=5*/f32[384,768]{1,0:T(8,128)S(1)}) custom-call(s32[6]{0:T(128)S(1)} %copy-done.1, bf16[768,768]{1,0:T(8,128)(2,1)S(1)} %copy-done, ...), custom_call_target="tpu_custom_call" | custom-call | tf_op jit(solution)/shard_map/pallas_call | solution.py:154
  35.1 0.0 slice-start
  35.1 3.5 %shard_map.56 = (f32[384,768]{1,0:T(8,128)S(1)}, f32[384,768]{1,0:T(8,128)S(1)}, f32[384,768]{1,0:T(8,128)S(1)}, f32[384,768]{1,0:T(8,128)S(1)}, f32[384,768]{1,0:T(8,128)S(1)}, /*index=5*/f32[384,768]{1,0:T(8,128)S(1)}) custom-call(s32[6]{0:T(128)S(1)} %copy-done.1, ...), custom_call_target="tpu_custom_call", output_to_operand_aliasing={{0}: (3, {}), {1}: (4, {}), {2}: (5, {}), {3}: (6, {}), {4}... | custom-call | tf_op jit(solution)/shard_map/pallas_call | solution.py:154
  38.6 0.0 slice-start.1
  38.6 2.4 %shard_map.57 = (f32[384,768]{1,0:T(8,128)S(1)}, f32[384,768]{1,0:T(8,128)S(1)}, f32[384,768]{1,0:T(8,128)S(1)}, f32[384,768]{1,0:T(8,128)S(1)}, f32[384,768]{1,...) custom-call(s32[6]{0:T(128)S(1)} %copy-done.1, ...), custom_call_target="tpu_custom_call", output_to_operand_aliasing={{0}: (3, {}), {1}: (4, {}), {2}: (5, {}), {3}: (6, {}), {4}... | custom-call | tf_op jit(solution)/shard_map/pallas_call | solution.py:154
  41.0 2.0 %shard_map.65.left = bf16[384,768]{1,0:T(8,128)(2,1)S(1)} custom-call(s32[6]{0:T(128)S(1)} %copy-done.1, bf16[768,768]{1,0:T(8,128)(2,1)S(1)} %copy-done, bf16[768,768]{1,0:T(8,128)(2,1)S(1)} %collective-permute-done.2.refs_0_, f32[384,768]{1,0:T(8,128)S(1)} %get-tuple-element.55.refs_1_, ...), custom_call_target="tpu_custom_call", output_to_operand_aliasing={{}: (6, {})} | custom-call | tf_op jit(solution)/shard_map/pallas_call | solution.py:154
  43.1 0.7 shard_map.67
  43.7 0.7 shard_map.66
  44.4 2.7 %collective-permute-start.10 = (bf16[192,1536]{1,0:T(8,128)(2,1)S(1)}, bf16[192,1536]{1,0:T(8,128)(2,1)S(1)}, u32[]{:S(2)}, u32[]{:S(2)}) collective-permute-start(bf16[192,1536]{1,0:T(8,128)(2,1)S(1)} %shard_map.66), channel_id=1, source_target_pairs={{0,8},{8,0},{16,24},{24,16},{1,9},{9,1},{17,25},{25,17},{2,10},{10... | collective-permute-start | bytes 1769480 | tf_op jit(solution)/shard_map/ppermute | solution.py:343
  47.1 2.9 %shard_map.58 = (f32[384,768]{1,0:T(8,128)S(1)}, f32[384,768]{1,0:T(8,128)S(1)}, f32[384,768]{1,0:T(8,128)S(1)}, bf16[384,768]{1,0:T(8,128)(2,1)S(1)}) custom-call(s32[6]{0:T(128)S(1)} %copy-done.1, bf16[768,768]{1,0:T(8,128)(2,1)S(1)} %copy-done, ...), custom_call_target="tpu_custom_call", output_to_operand_aliasing={{0}: (3, {}), {1}: (4, {}), {2}: (5, {}), {3}: (6, {})} | custom-call | tf_op jit(solution)/shard_map/pallas_call | solution.py:154
  50.1 2.0 %shard_map.59.left = bf16[384,768]{1,0:T(8,128)(2,1)S(1)} custom-call(s32[6]{0:T(128)S(1)} %copy-done.1, bf16[768,768]{1,0:T(8,128)(2,1)S(1)} %copy-done, bf16[768,768]{1,0:T(8,128)(2,1)S(1)} %collective-permute-done.1.refs_0_, f32[384,768]{1,0:T(8,128)S(1)} %get-tuple-element.51.refs_1_, ...), custom_call_target="tpu_custom_call", output_to_operand_aliasing={{}: (6, {})} | custom-call | tf_op jit(solution)/shard_map/pallas_call | solution.py:154
  52.1 0.7 shard_map.60
  52.8 0.1 collective-permute-start.6
  52.8 0.6 shard_map.61
  53.5 1.0 %collective-permute-start.7 = (bf16[192,1536]{1,0:T(8,128)(2,1)S(1)}, bf16[192,1536]{1,0:T(8,128)(2,1)S(1)}, u32[]{:S(2)}, u32[]{:S(2)}) collective-permute-start(bf16[192,1536]{1,0:T(8,128)(2,1)S(1)} %shard_map.61), channel_id=1, source_target_pairs={{0,16},{8,24},{16,0},{24,8},{1,17},{9,25},{17,1},{25,9},{2,18},{10... | collective-permute-start | bytes 1769480 | tf_op jit(solution)/shard_map/ppermute | solution.py:343
  54.4 6.8 %collective-permute-done.10.rest_0_ = bf16[192,1536]{1,0:T(8,128)(2,1)S(1)} collective-permute-done((bf16[192,1536]{1,0:T(8,128)(2,1)S(1)}, bf16[192,1536]{1,0:T(8,128)(2,1)S(1)}, u32[]{:S(2)}, u32[]{:S(2)}) %collective-permute-start.10) | collective-permute-done | bytes 589856 | tf_op jit(solution)/shard_map/ppermute | solution.py:343
  61.3 0.4 shard_map.69
  61.7 0.1 collective-permute-start.12
  61.8 1.5 %collective-permute-done.11.rest_1_.rest_0_ = bf16[192,1536]{1,0:T(8,128)(2,1)S(1)} collective-permute-done((bf16[192,1536]{1,0:T(8,128)(2,1)S(1)}, bf16[192,1536]{1,0:T(8,128)(2,1)S(1)}, u32[]{:S(2)}, u32[]{:S(2)}) %collective-permute-start.11) | collective-permute-done | bytes 589856 | tf_op jit(solution)/shard_map/ppermute | solution.py:343
  63.3 0.4 shard_map.70
  63.7 0.6 collective-permute-start.13
  64.3 9.6 %collective-permute-done.6.rest_0_ = bf16[192,1536]{1,0:T(8,128)(2,1)S(1)} collective-permute-done((bf16[192,1536]{1,0:T(8,128)(2,1)S(1)}, bf16[192,1536]{1,0:T(8,128)(2,1)S(1)}, u32[]{:S(2)}, u32[]{:S(2)}) %collective-permute-start.6) | collective-permute-done | bytes 589856 | tf_op jit(solution)/shard_map/ppermute | solution.py:343
  73.9 0.4 shard_map.63
  74.3 0.1 collective-permute-start.8
  74.4 1.5 %collective-permute-done.7.rest_1_.rest_0_ = bf16[192,1536]{1,0:T(8,128)(2,1)S(1)} collective-permute-done((bf16[192,1536]{1,0:T(8,128)(2,1)S(1)}, bf16[192,1536]{1,0:T(8,128)(2,1)S(1)}, u32[]{:S(2)}, u32[]{:S(2)}) %collective-permute-start.7) | collective-permute-done | bytes 589856 | tf_op jit(solution)/shard_map/ppermute | solution.py:343
  75.9 0.4 shard_map.64
  76.4 0.6 collective-permute-start.9
  76.9 0.7 shard_map.68.terms
  77.6 0.7 shard_map.62.terms
  78.3 4.0 %collective-permute-done.12.rest_0_ = bf16[192,768]{1,0:T(8,128)(2,1)S(1)} collective-permute-done((bf16[192,768]{1,0:T(8,128)(2,1)S(1)}, bf16[192,768]{1,0:T(8,128)(2,1)S(1)}, u32[]{:S(2)}, u32[]{:S(2)}) %collective-permute-start.12) | collective-permute-done | bytes 294944 | tf_op jit(solution)/shard_map/ppermute | solution.py:343
  82.2 0.9 shard_map.71.rest_2_
  83.1 4.6 %collective-permute-done.8.rest_0_ = bf16[192,768]{1,0:T(8,128)(2,1)S(1)} collective-permute-done((bf16[192,768]{1,0:T(8,128)(2,1)S(1)}, bf16[192,768]{1,0:T(8,128)(2,1)S(1)}, u32[]{:S(2)}, u32[]{:S(2)}) %collective-permute-start.8) | collective-permute-done | bytes 294944 | tf_op jit(solution)/shard_map/ppermute | solution.py:343
  87.7 0.9 shard_map.72
  (16 shorter events, 0.1 us)
Async XLA Ops:
  1.3 2.2 %copy-start.2 = (bf16[768,768]{1,0:T(8,128)(2,1)S(1)}, bf16[768,768]{1,0:T(8,128)(2,1)}, u32[]{:S(2)}) copy-start(bf16[768,768]{1,0:T(8,128)(2,1)} %param.6) | copy-start | bytes 3538948
  1.4 17.7 %collective-permute-start.3 = (bf16[768,768]{1,0:T(8,128)(2,1)S(1)}, bf16[768,768]{1,0:T(8,128)(2,1)S(1)}, u32[]{:S(2)}, u32[]{:S(2)}) collective-permute-start(bf16[768,768]{1,0:T(8,128)(2,1)S(1)} %pad_maximum_fusion.refs_0_), channel_id=1, source_target_pairs={{1,2},{3,4},{5,6},{2,1},{4,3},{6,5},{9,10},{11,12},{13,14},{10,9},... | collective-permute-start | bytes 3538952 | tf_op jit(solution)/shard_map/ppermute | solution.py:328
  3.5 1.3 %copy-start.3 = (bf16[768,768]{1,0:T(8,128)(2,1)S(1)}, bf16[768,768]{1,0:T(8,128)(2,1)}, u32[]{:S(2)}) copy-start(bf16[768,768]{1,0:T(8,128)(2,1)} %param.7) | copy-start | bytes 3538948
  4.8 20.0 %copy-start = (bf16[768,768]{1,0:T(8,128)(2,1)S(1)}, bf16[768,768]{1,0:T(8,128)(2,1)}, u32[]{:S(2)}) copy-start(bf16[768,768]{1,0:T(8,128)(2,1)} %query.11) | copy-start | bytes 3538948
  4.8 20.0 %copy-start.1 = (s32[6]{0:T(128)S(1)}, s32[6]{0:T(128)}, u32[]{:S(2)}) copy-start(s32[6]{0:T(128)} %span_ref.11) | copy-start | bytes 76
  4.9 16.6 %collective-permute-start = (bf16[768,768]{1,0:T(8,128)(2,1)S(1)}, bf16[768,768]{1,0:T(8,128)(2,1)S(1)}, u32[]{:S(2)}, u32[]{:S(2)}) collective-permute-start(bf16[768,768]{1,0:T(8,128)(2,1)S(1)} %pad_maximum_fusion.1.refs_1_), channel_id=1, source_target_pairs={{0,1},{1,0},{2,3},{3,2},{4,5},{5,4},{6,7},{7,6},{8,9},{9,8},{10,11... | collective-permute-start | bytes 3538952 | tf_op jit(solution)/shard_map/ppermute | solution.py:324
  6.7 18.1 %collective-permute-start.5 = (bf16[768,768]{1,0:T(8,128)(2,1)S(1)}, bf16[768,768]{1,0:T(8,128)(2,1)S(1)}, u32[]{:S(2)}, u32[]{:S(2)}) collective-permute-start(bf16[768,768]{1,0:T(8,128)(2,1)S(1)} %pad_maximum_fusion.refs_0_), channel_id=1, source_target_pairs={{0,1},{1,0},{2,3},{3,2},{4,5},{5,4},{6,7},{7,6},{8,9},{9,8},{10,11... | collective-permute-start | bytes 3538952 | tf_op jit(solution)/shard_map/ppermute | solution.py:324
  19.1 19.5 %collective-permute-start.4 = (bf16[768,768]{1,0:T(8,128)(2,1)S(1)}, bf16[768,768]{1,0:T(8,128)(2,1)S(1)}, u32[]{:S(2)}, u32[]{:S(2)}) collective-permute-start(bf16[768,768]{1,0:T(8,128)(2,1)S(1)} %collective-permute-done.3.refs_0_), channel_id=1, source_target_pairs={{0,1},{1,0},{2,3},{3,2},{4,5},{5,4},{6,7},{7,6},{8,9},{9,8},{10,11... | collective-permute-start | bytes 3538952 | tf_op jit(solution)/shard_map/ppermute | solution.py:324
  19.2 21.8 %collective-permute-start.2 = (bf16[768,768]{1,0:T(8,128)(2,1)S(1)}, bf16[768,768]{1,0:T(8,128)(2,1)S(1)}, u32[]{:S(2)}, u32[]{:S(2)}) collective-permute-start(bf16[768,768]{1,0:T(8,128)(2,1)S(1)} %pad_maximum_fusion.1.refs_1_), channel_id=1, source_target_pairs={{1,2},{3,4},{5,6},{2,1},{4,3},{6,5},{9,10},{11,12},{13,14},{10,9},... | collective-permute-start | bytes 3538952 | tf_op jit(solution)/shard_map/ppermute | solution.py:328
  21.6 28.5 %collective-permute-start.1 = (bf16[768,768]{1,0:T(8,128)(2,1)S(1)}, bf16[768,768]{1,0:T(8,128)(2,1)S(1)}, u32[]{:S(2)}, u32[]{:S(2)}) collective-permute-start(bf16[768,768]{1,0:T(8,128)(2,1)S(1)} %collective-permute-done.refs_2_), channel_id=1, source_target_pairs={{1,2},{3,4},{5,6},{2,1},{4,3},{6,5},{9,10},{11,12},{13,14},{10,9},... | collective-permute-start | bytes 3538952 | tf_op jit(solution)/shard_map/ppermute | solution.py:328
  35.1 8.0 %slice-start = ((s8[4718592]{0:T(1024)(128)(4,1)}), s8[4194304]{0:T(1024)(128)(4,1)S(1)}, s32[]{:S(2)}) async-start(s8[4718592]{0:T(1024)(128)(4,1)} %bitcast), calls=%async_computation | async-start | bytes 8388608
  38.6 4.4 %slice-start.1 = ((s8[4718592]{0:T(1024)(128)(4,1)}), s8[524288]{0:T(1024)(128)(4,1)S(1)}, s32[]{:S(2)}) async-start(s8[4718592]{0:T(1024)(128)(4,1)} %bitcast), calls=%async_computation.1 | async-start | bytes 1048576
  44.4 16.9 %collective-permute-start.10 = (bf16[192,1536]{1,0:T(8,128)(2,1)S(1)}, bf16[192,1536]{1,0:T(8,128)(2,1)S(1)}, u32[]{:S(2)}, u32[]{:S(2)}) collective-permute-start(bf16[192,1536]{1,0:T(8,128)(2,1)S(1)} %shard_map.66), channel_id=1, source_target_pairs={{0,8},{8,0},{16,24},{24,16},{1,9},{9,1},{17,25},{25,17},{2,10},{10... | collective-permute-start | bytes 1769480 | tf_op jit(solution)/shard_map/ppermute | solution.py:343
  47.1 16.2 %collective-permute-start.11 = (bf16[192,1536]{1,0:T(8,128)(2,1)S(1)}, bf16[192,1536]{1,0:T(8,128)(2,1)S(1)}, u32[]{:S(2)}, u32[]{:S(2)}) collective-permute-start(bf16[192,1536]{1,0:T(8,128)(2,1)S(1)} %shard_map.67), channel_id=1, source_target_pairs={{0,16},{8,24},{16,0},{24,8},{1,17},{9,25},{17,1},{25,9},{2,18},{10... | collective-permute-start | bytes 1769480 | tf_op jit(solution)/shard_map/ppermute | solution.py:343
  52.8 21.1 %collective-permute-start.6 = (bf16[192,1536]{1,0:T(8,128)(2,1)S(1)}, bf16[192,1536]{1,0:T(8,128)(2,1)S(1)}, u32[]{:S(2)}, u32[]{:S(2)}) collective-permute-start(bf16[192,1536]{1,0:T(8,128)(2,1)S(1)} %shard_map.60), channel_id=1, source_target_pairs={{0,8},{8,0},{16,24},{24,16},{1,9},{9,1},{17,25},{25,17},{2,10},{10... | collective-permute-start | bytes 1769480 | tf_op jit(solution)/shard_map/ppermute | solution.py:343
  53.5 22.4 %collective-permute-start.7 = (bf16[192,1536]{1,0:T(8,128)(2,1)S(1)}, bf16[192,1536]{1,0:T(8,128)(2,1)S(1)}, u32[]{:S(2)}, u32[]{:S(2)}) collective-permute-start(bf16[192,1536]{1,0:T(8,128)(2,1)S(1)} %shard_map.61), channel_id=1, source_target_pairs={{0,16},{8,24},{16,0},{24,8},{1,17},{9,25},{17,1},{25,9},{2,18},{10... | collective-permute-start | bytes 1769480 | tf_op jit(solution)/shard_map/ppermute | solution.py:343
  61.7 20.6 %collective-permute-start.12 = (bf16[192,768]{1,0:T(8,128)(2,1)S(1)}, bf16[192,768]{1,0:T(8,128)(2,1)S(1)}, u32[]{:S(2)}, u32[]{:S(2)}) collective-permute-start(bf16[192,768]{1,0:T(8,128)(2,1)S(1)} %shard_map.69), channel_id=1, source_target_pairs={{0,16},{8,24},{16,0},{24,8},{1,17},{9,25},{17,1},{25,9},{2,18},{10... | collective-permute-start | bytes 884744 | tf_op jit(solution)/shard_map/ppermute | solution.py:343
  63.7 18.5 %collective-permute-start.13 = (bf16[192,768]{1,0:T(8,128)(2,1)S(1)}, bf16[192,768]{1,0:T(8,128)(2,1)S(1)}, u32[]{:S(2)}, u32[]{:S(2)}) collective-permute-start(bf16[192,768]{1,0:T(8,128)(2,1)S(1)} %shard_map.70), channel_id=1, source_target_pairs={{0,8},{8,0},{16,24},{24,16},{1,9},{9,1},{17,25},{25,17},{2,10},{10... | collective-permute-start | bytes 884744 | tf_op jit(solution)/shard_map/ppermute | solution.py:343
  74.3 13.4 %collective-permute-start.8 = (bf16[192,768]{1,0:T(8,128)(2,1)S(1)}, bf16[192,768]{1,0:T(8,128)(2,1)S(1)}, u32[]{:S(2)}, u32[]{:S(2)}) collective-permute-start(bf16[192,768]{1,0:T(8,128)(2,1)S(1)} %shard_map.63), channel_id=1, source_target_pairs={{0,16},{8,24},{16,0},{24,8},{1,17},{9,25},{17,1},{25,9},{2,18},{10... | collective-permute-start | bytes 884744 | tf_op jit(solution)/shard_map/ppermute | solution.py:343
  76.4 11.4 %collective-permute-start.9 = (bf16[192,768]{1,0:T(8,128)(2,1)S(1)}, bf16[192,768]{1,0:T(8,128)(2,1)S(1)}, u32[]{:S(2)}, u32[]{:S(2)}) collective-permute-start(bf16[192,768]{1,0:T(8,128)(2,1)S(1)} %shard_map.64), channel_id=1, source_target_pairs={{0,8},{8,0},{16,24},{24,16},{1,9},{9,1},{17,25},{25,17},{2,10},{10... | collective-permute-start | bytes 884744 | tf_op jit(solution)/shard_map/ppermute | solution.py:343

commit v7 on v6

--- a/solution.py
+++ b/solution.py
@@ -13,6 +13,7 @@
 BF16 = jnp.bfloat16
 VMEM_LIMIT = 16 << 20
 CHUNK = 384
+LEAN = 16
 
 
 def params():
@@ -217,10 +218,15 @@
     return attend_step(head_span, query_tok, [third], {"E": state}, cases, closed={"E": result})[1]["E"]
 
 
+def row_edges(parts):
+    return [0] + [part * FRAME_TOK // parts + LEAN for part in range(1, parts)] + [FRAME_TOK]
+
+
 def project(attended, part, parts, out_weight, slots, received):
     groups = lax.axis_size("head")
     width = out_weight.shape[1] // groups
-    rows = attended.shape[0] // parts
+    start, stop = row_edges(parts)[part : part + 2]
+    rows = stop - start
 
     def kernel(left, right, *rest):
         out = rest[-1]
@@ -228,7 +234,7 @@
         for index, slot in enumerate(slots):
             column = pl.ds(pl.multiple_of((group ^ slot) * width, width), width)
             sums = jnp.dot(
-                left[part * rows : (part + 1) * rows, :], right[:, column], preferred_element_type=F32
+                left[start:stop, :], right[:, column], preferred_element_type=F32
             )
             for ref, (_, spots) in zip(rest, received):
                 sums = sums + ref[:, spots[index] * width : (spots[index] + 1) * width].astype(F32)
@@ -246,7 +252,7 @@
 def sum_own(attended, parts, out_weight, received):
     groups = lax.axis_size("head")
     width = out_weight.shape[1] // groups
-    rows = FRAME_TOK // parts
+    edges = row_edges(parts)
     flat = [(array, spots[0], part) for part in range(parts) for array, spots in received[part]]
 
     def kernel(left, right, *rest):
@@ -255,11 +261,11 @@
         column = pl.ds(pl.multiple_of(group * width, width), width)
         sums = jnp.dot(left[...], right[:, column], preferred_element_type=F32)
         for part in range(parts):
-            terms = sums[part * rows : (part + 1) * rows]
+            terms = sums[edges[part] : edges[part + 1]]
             for ref, (_, spot, owner) in zip(rest, flat):
                 if owner == part:
                     terms = terms + ref[:, spot * width : (spot + 1) * width].astype(F32)
-            out[part * rows : (part + 1) * rows, :] = terms
+            out[edges[part] : edges[part + 1], :] = terms
 
     operands = [attended, out_weight, *(array for array, _, _ in flat)]
     return pl.pallas_call(
@@ -273,7 +279,7 @@
 
 def finish(own, received, is_edge, frames_here, into):
     parts = len(received)
-    rows = FRAME_TOK // parts
+    edges = row_edges(parts)
     width = own.shape[1]
 
     def kernel(terms, *rest):
@@ -282,12 +288,13 @@
         frame = parity if is_edge else 1 - parity
         copies = []
         for part in range(parts):
-            span = slice(part * rows, (part + 1) * rows)
+            start, rows = edges[part], edges[part + 1] - edges[part]
+            span = slice(start, start + rows)
             buffer[span, :] = (terms[span, :] + rest[part][...].astype(F32)).astype(BF16)
             copies.append(
                 pltpu.make_async_copy(
-                    buffer.at[pl.ds(part * rows, rows)],
-                    out.at[pl.ds(pl.multiple_of(frame * FRAME_TOK + part * rows, rows), rows)],
+                    buffer.at[pl.ds(start, rows)],
+                    out.at[pl.ds(pl.multiple_of(frame * FRAME_TOK + start, 16), rows)],
                     sems.at[part],
                 )
             )

time: 89 us -> 95.5 us (1.073)
  the two profiles are of different devices: /device:TPU:22 before, /device:TPU:20 now
where the time goes in v7:
time: 95.5 us; the launch traced here: 95.3 us
  waiting for transfers between devices  45.1 us (47%)
  Pallas kernels  32.3 us (34%)
  starting transfers between devices  14.6 us (15%)
  local copies, waits for them, and re-layouts  2.65 us (3%)
    ppermute x8, waiting for transfers between devices, exchange(): lax.ppermute(value, 'head', [(i, i ^ 1 << bit) for i in range(groups)])  32.5 us
    pallas_call x6, Pallas kernels, attend_step(): pl.pallas_call(kernel, out_shape=tuple(shapes), in_specs=[SMEM] + [VMEM]...  24.8 us
    ppermute x3, waiting for transfers between devices, across(): return lax.ppermute(value, 'frame', pairs + [(b, a) for a, b in pairs])  12.6 us
    ppermute x3, starting transfers between devices, across(): return lax.ppermute(value, 'frame', pairs + [(b, a) for a, b in pairs])  7.6 us
    ppermute x8, starting transfers between devices, exchange(): lax.ppermute(value, 'head', [(i, i ^ 1 << bit) for i in range(groups)])  5.05 us
    pallas_call x8, Pallas kernels, project(): pl.pallas_call(kernel, out_shape=jax.ShapeDtypeStruct((rows, len(slots) *...  4.33 us
    ppermute x3, starting transfers between devices, swap(): return lax.ppermute(value, 'frame', [(i, i ^ 1) for i in range(frames)])  1.94 us
  transfers between devices with their start and end apart: 14, of which 9 were waited for; matrix products, arithmetic and copies ran while one was open for 0% of the time, Pallas kernels for 33%

profile of v7, /device:TPU:20, one launch (start us, length us, event | category | flops | bytes accessed | tf_op | source)
XLA Modules:
  0.0 95.3 jit_solution(15016939279445858581)
XLA Ops:
  0.0 1.3 %constant_dynamic-slice_fusion.2 = (bf16[384,768]{1,0:T(8,128)(2,1)S(1)}, bf16[384,768]{1,0:T(8,128)(2,1)S(1)}) fusion(bf16[768,768]{1,0:T(8,128)(2,1)} %param.7, s32[]{:T(128)S(6)} %select_n.16, bf16[768,768]{1,0:T(8,128)(2,1)} %param.6), kind=kLoop, calls=%fused_computation.4 | loop fusion | bytes 2359300 | tf_op jit(solution)/shard_map/dynamic_slice | solution.py:32
  1.3 0.0 copy-start.2
  1.3 0.1 pad_maximum_fusion.refs_0_
  1.4 2.1 %collective-permute-start.3 = (bf16[768,768]{1,0:T(8,128)(2,1)S(1)}, bf16[768,768]{1,0:T(8,128)(2,1)S(1)}, u32[]{:S(2)}, u32[]{:S(2)}) collective-permute-start(bf16[768,768]{1,0:T(8,128)(2,1)S(1)} %pad_maximum_fusion.refs_0_), channel_id=1, source_target_pairs={{1,2},{3,4},{5,6},{2,1},{4,3},{6,5},{9,10},{11,12},{13,14},{10,9},... | collective-permute-start | bytes 3538952 | tf_op jit(solution)/shard_map/ppermute | solution.py:335
  3.6 1.2 %copy-done.3 = bf16[768,768]{1,0:T(8,128)(2,1)S(1)} copy-done((bf16[768,768]{1,0:T(8,128)(2,1)S(1)}, bf16[768,768]{1,0:T(8,128)(2,1)}, u32[]{:S(2)}) %copy-start.3) | copy-done | bytes 1179672
  4.8 0.1 pad_maximum_fusion.1.refs_1_
  4.9 1.7 %collective-permute-start = (bf16[768,768]{1,0:T(8,128)(2,1)S(1)}, bf16[768,768]{1,0:T(8,128)(2,1)S(1)}, u32[]{:S(2)}, u32[]{:S(2)}) collective-permute-start(bf16[768,768]{1,0:T(8,128)(2,1)S(1)} %pad_maximum_fusion.1.refs_1_), channel_id=1, source_target_pairs={{0,1},{1,0},{2,3},{3,2},{4,5},{5,4},{6,7},{7,6},{8,9},{9,8},{10,11... | collective-permute-start | bytes 3538952 | tf_op jit(solution)/shard_map/ppermute | solution.py:331
  6.7 0.1 collective-permute-start.5
  6.8 12.3 %collective-permute-done.3.refs_0_ = bf16[768,768]{1,0:T(8,128)(2,1)S(1)} collective-permute-done((bf16[768,768]{1,0:T(8,128)(2,1)S(1)}, bf16[768,768]{1,0:T(8,128)(2,1)S(1)}, u32[]{:S(2)}, u32[]{:S(2)}) %collective-permute-start.3) | collective-permute-done | bytes 1179680 | tf_op jit(solution)/shard_map/ppermute | solution.py:335
  19.1 0.1 collective-permute-start.4
  19.2 2.3 %collective-permute-start.2 = (bf16[768,768]{1,0:T(8,128)(2,1)S(1)}, bf16[768,768]{1,0:T(8,128)(2,1)S(1)}, u32[]{:S(2)}, u32[]{:S(2)}) collective-permute-start(bf16[768,768]{1,0:T(8,128)(2,1)S(1)} %pad_maximum_fusion.1.refs_1_), channel_id=1, source_target_pairs={{1,2},{3,4},{5,6},{2,1},{4,3},{6,5},{9,10},{11,12},{13,14},{10,9},... | collective-permute-start | bytes 3538952 | tf_op jit(solution)/shard_map/ppermute | solution.py:335
  21.6 3.2 %collective-permute-start.1 = (bf16[768,768]{1,0:T(8,128)(2,1)S(1)}, bf16[768,768]{1,0:T(8,128)(2,1)S(1)}, u32[]{:S(2)}, u32[]{:S(2)}) collective-permute-start(bf16[768,768]{1,0:T(8,128)(2,1)S(1)} %collective-permute-done.refs_2_), channel_id=1, source_target_pairs={{1,2},{3,4},{5,6},{2,1},{4,3},{6,5},{9,10},{11,12},{13,14},{10,9},... | collective-permute-start | bytes 3538952 | tf_op jit(solution)/shard_map/ppermute | solution.py:335
  24.8 12.2 %shard_map.55 = (f32[384,768]{1,0:T(8,128)S(1)}, f32[384,768]{1,0:T(8,128)S(1)}, f32[384,768]{1,0:T(8,128)S(1)}, f32[384,768]{1,0:T(8,128)S(1)}, f32[384,768]{1,0:T(8,128)S(1)}, /*index=5*/f32[384,768]{1,0:T(8,128)S(1)}) custom-call(s32[6]{0:T(128)S(1)} %copy-done.1, bf16[768,768]{1,0:T(8,128)(2,1)S(1)} %copy-done, ...), custom_call_target="tpu_custom_call" | custom-call | tf_op jit(solution)/shard_map/pallas_call | solution.py:155
  37.0 0.0 slice-start
  37.0 4.9 %shard_map.56 = (f32[384,768]{1,0:T(8,128)S(1)}, f32[384,768]{1,0:T(8,128)S(1)}, f32[384,768]{1,0:T(8,128)S(1)}, f32[384,768]{1,0:T(8,128)S(1)}, f32[384,768]{1,0:T(8,128)S(1)}, /*index=5*/f32[384,768]{1,0:T(8,128)S(1)}) custom-call(s32[6]{0:T(128)S(1)} %copy-done.1, ...), custom_call_target="tpu_custom_call", output_to_operand_aliasing={{0}: (3, {}), {1}: (4, {}), {2}: (5, {}), {3}: (6, {}), {4}... | custom-call | tf_op jit(solution)/shard_map/pallas_call | solution.py:155
  41.9 0.0 slice-start.1
  41.9 1.8 %shard_map.57 = (f32[384,768]{1,0:T(8,128)S(1)}, f32[384,768]{1,0:T(8,128)S(1)}, f32[384,768]{1,0:T(8,128)S(1)}, f32[384,768]{1,0:T(8,128)S(1)}, f32[384,768]{1,...) custom-call(s32[6]{0:T(128)S(1)} %copy-done.1, ...), custom_call_target="tpu_custom_call", output_to_operand_aliasing={{0}: (3, {}), {1}: (4, {}), {2}: (5, {}), {3}: (6, {}), {4}... | custom-call | tf_op jit(solution)/shard_map/pallas_call | solution.py:155
  43.7 1.4 %shard_map.65.left = bf16[384,768]{1,0:T(8,128)(2,1)S(1)} custom-call(s32[6]{0:T(128)S(1)} %copy-done.1, bf16[768,768]{1,0:T(8,128)(2,1)S(1)} %copy-done, bf16[768,768]{1,0:T(8,128)(2,1)S(1)} %collective-permute-done.2.refs_0_, f32[384,768]{1,0:T(8,128)S(1)} %get-tuple-element.55.refs_1_, ...), custom_call_target="tpu_custom_call", output_to_operand_aliasing={{}: (6, {})} | custom-call | tf_op jit(solution)/shard_map/pallas_call | solution.py:155
  45.1 0.7 shard_map.66
  45.9 0.1 collective-permute-start.10
  45.9 3.1 %shard_map.58 = (f32[384,768]{1,0:T(8,128)S(1)}, f32[384,768]{1,0:T(8,128)S(1)}, f32[384,768]{1,0:T(8,128)S(1)}, bf16[384,768]{1,0:T(8,128)(2,1)S(1)}) custom-call(s32[6]{0:T(128)S(1)} %copy-done.1, bf16[768,768]{1,0:T(8,128)(2,1)S(1)} %copy-done, ...), custom_call_target="tpu_custom_call", output_to_operand_aliasing={{0}: (3, {}), {1}: (4, {}), {2}: (5, {}), {3}: (6, {})} | custom-call | tf_op jit(solution)/shard_map/pallas_call | solution.py:155
  49.1 0.3 collective-permute-done.1.refs_0_
  49.3 1.4 %shard_map.59.left = bf16[384,768]{1,0:T(8,128)(2,1)S(1)} custom-call(s32[6]{0:T(128)S(1)} %copy-done.1, bf16[768,768]{1,0:T(8,128)(2,1)S(1)} %copy-done, bf16[768,768]{1,0:T(8,128)(2,1)S(1)} %collective-permute-done.1.refs_0_, f32[384,768]{1,0:T(8,128)S(1)} %get-tuple-element.51.refs_1_, ...), custom_call_target="tpu_custom_call", output_to_operand_aliasing={{}: (6, {})} | custom-call | tf_op jit(solution)/shard_map/pallas_call | solution.py:155
  50.8 0.7 shard_map.60
  51.5 2.2 %collective-permute-start.6 = (bf16[208,1536]{1,0:T(8,128)(2,1)S(1)}, bf16[208,1536]{1,0:T(8,128)(2,1)S(1)}, u32[]{:S(2)}, u32[]{:S(2)}) collective-permute-start(bf16[208,1536]{1,0:T(8,128)(2,1)S(1)} %shard_map.60), channel_id=1, source_target_pairs={{0,8},{8,0},{16,24},{24,16},{1,9},{9,1},{17,25},{25,17},{2,10},{10... | collective-permute-start | bytes 1916936 | tf_op jit(solution)/shard_map/ppermute | solution.py:350
  53.7 0.6 shard_map.67
  54.3 0.1 collective-permute-start.11
  54.4 0.6 shard_map.61
  55.1 2.1 %collective-permute-start.7 = (bf16[176,1536]{1,0:T(8,128)(2,1)S(1)}, bf16[176,1536]{1,0:T(8,128)(2,1)S(1)}, u32[]{:S(2)}, u32[]{:S(2)}) collective-permute-start(bf16[176,1536]{1,0:T(8,128)(2,1)S(1)} %shard_map.61), channel_id=1, source_target_pairs={{0,16},{8,24},{16,0},{24,8},{1,17},{9,25},{17,1},{25,9},{2,18},{10... | collective-permute-start | bytes 1622024 | tf_op jit(solution)/shard_map/ppermute | solution.py:350
  57.1 6.0 %collective-permute-done.10.rest_0_ = bf16[208,1536]{1,0:T(8,128)(2,1)S(1)} collective-permute-done((bf16[208,1536]{1,0:T(8,128)(2,1)S(1)}, bf16[208,1536]{1,0:T(8,128)(2,1)S(1)}, u32[]{:S(2)}, u32[]{:S(2)}) %collective-permute-start.10) | collective-permute-done | bytes 639008 | tf_op jit(solution)/shard_map/ppermute | solution.py:350
  63.2 0.4 shard_map.69
  63.6 0.1 collective-permute-start.12
  63.7 12.6 %collective-permute-done.6.rest_0_ = bf16[208,1536]{1,0:T(8,128)(2,1)S(1)} collective-permute-done((bf16[208,1536]{1,0:T(8,128)(2,1)S(1)}, bf16[208,1536]{1,0:T(8,128)(2,1)S(1)}, u32[]{:S(2)}, u32[]{:S(2)}) %collective-permute-start.6) | collective-permute-done | bytes 639008 | tf_op jit(solution)/shard_map/ppermute | solution.py:350
  76.3 0.4 shard_map.63
  76.7 0.1 collective-permute-start.8
  76.8 0.4 shard_map.70
  77.2 0.4 collective-permute-start.13
  77.6 3.5 %collective-permute-done.7.rest_1_.rest_0_ = bf16[176,1536]{1,0:T(8,128)(2,1)S(1)} collective-permute-done((bf16[176,1536]{1,0:T(8,128)(2,1)S(1)}, bf16[176,1536]{1,0:T(8,128)(2,1)S(1)}, u32[]{:S(2)}, u32[]{:S(2)}) %collective-permute-start.7) | collective-permute-done | bytes 540704 | tf_op jit(solution)/shard_map/ppermute | solution.py:350
  81.1 0.4 shard_map.64
  81.5 0.1 collective-permute-start.9
  81.6 0.7 shard_map.68.terms
  82.3 0.7 shard_map.62.terms
  83.0 3.7 %collective-permute-done.13.rest_1_ = bf16[176,768]{1,0:T(8,128)(2,1)S(1)} collective-permute-done((bf16[176,768]{1,0:T(8,128)(2,1)S(1)}, bf16[176,768]{1,0:T(8,128)(2,1)S(1)}, u32[]{:S(2)}, u32[]{:S(2)}) %collective-permute-start.13) | collective-permute-done | bytes 270368 | tf_op jit(solution)/shard_map/ppermute | solution.py:350
  86.7 1.3 %collective-permute-done.12.rest_0_ = bf16[208,768]{1,0:T(8,128)(2,1)S(1)} collective-permute-done((bf16[208,768]{1,0:T(8,128)(2,1)S(1)}, bf16[208,768]{1,0:T(8,128)(2,1)S(1)}, u32[]{:S(2)}, u32[]{:S(2)}) %collective-permute-start.12) | collective-permute-done | bytes 319520 | tf_op jit(solution)/shard_map/ppermute | solution.py:350
  88.0 0.9 shard_map.71.rest_2_
  88.9 2.1 %collective-permute-done.9.rest_1_ = bf16[176,768]{1,0:T(8,128)(2,1)S(1)} collective-permute-done((bf16[176,768]{1,0:T(8,128)(2,1)S(1)}, bf16[176,768]{1,0:T(8,128)(2,1)S(1)}, u32[]{:S(2)}, u32[]{:S(2)}) %collective-permute-start.9) | collective-permute-done | bytes 270368 | tf_op jit(solution)/shard_map/ppermute | solution.py:350
  91.0 3.2 %collective-permute-done.8.rest_0_ = bf16[208,768]{1,0:T(8,128)(2,1)S(1)} collective-permute-done((bf16[208,768]{1,0:T(8,128)(2,1)S(1)}, bf16[208,768]{1,0:T(8,128)(2,1)S(1)}, u32[]{:S(2)}, u32[]{:S(2)}) %collective-permute-start.8) | collective-permute-done | bytes 319520 | tf_op jit(solution)/shard_map/ppermute | solution.py:350
  94.2 0.9 shard_map.72
  (16 shorter events, 0.1 us)
Async XLA Ops:
  1.3 2.2 %copy-start.2 = (bf16[768,768]{1,0:T(8,128)(2,1)S(1)}, bf16[768,768]{1,0:T(8,128)(2,1)}, u32[]{:S(2)}) copy-start(bf16[768,768]{1,0:T(8,128)(2,1)} %param.6) | copy-start | bytes 3538948
  1.4 17.7 %collective-permute-start.3 = (bf16[768,768]{1,0:T(8,128)(2,1)S(1)}, bf16[768,768]{1,0:T(8,128)(2,1)S(1)}, u32[]{:S(2)}, u32[]{:S(2)}) collective-permute-start(bf16[768,768]{1,0:T(8,128)(2,1)S(1)} %pad_maximum_fusion.refs_0_), channel_id=1, source_target_pairs={{1,2},{3,4},{5,6},{2,1},{4,3},{6,5},{9,10},{11,12},{13,14},{10,9},... | collective-permute-start | bytes 3538952 | tf_op jit(solution)/shard_map/ppermute | solution.py:335
  3.5 1.3 %copy-start.3 = (bf16[768,768]{1,0:T(8,128)(2,1)S(1)}, bf16[768,768]{1,0:T(8,128)(2,1)}, u32[]{:S(2)}) copy-start(bf16[768,768]{1,0:T(8,128)(2,1)} %param.7) | copy-start | bytes 3538948
  4.8 20.0 %copy-start = (bf16[768,768]{1,0:T(8,128)(2,1)S(1)}, bf16[768,768]{1,0:T(8,128)(2,1)}, u32[]{:S(2)}) copy-start(bf16[768,768]{1,0:T(8,128)(2,1)} %query.11) | copy-start | bytes 3538948
  4.8 20.0 %copy-start.1 = (s32[6]{0:T(128)S(1)}, s32[6]{0:T(128)}, u32[]{:S(2)}) copy-start(s32[6]{0:T(128)} %span_ref.11) | copy-start | bytes 76
  4.9 16.6 %collective-permute-start = (bf16[768,768]{1,0:T(8,128)(2,1)S(1)}, bf16[768,768]{1,0:T(8,128)(2,1)S(1)}, u32[]{:S(2)}, u32[]{:S(2)}) collective-permute-start(bf16[768,768]{1,0:T(8,128)(2,1)S(1)} %pad_maximum_fusion.1.refs_1_), channel_id=1, source_target_pairs={{0,1},{1,0},{2,3},{3,2},{4,5},{5,4},{6,7},{7,6},{8,9},{9,8},{10,11... | collective-permute-start | bytes 3538952 | tf_op jit(solution)/shard_map/ppermute | solution.py:331
  6.7 18.1 %collective-permute-start.5 = (bf16[768,768]{1,0:T(8,128)(2,1)S(1)}, bf16[768,768]{1,0:T(8,128)(2,1)S(1)}, u32[]{:S(2)}, u32[]{:S(2)}) collective-permute-start(bf16[768,768]{1,0:T(8,128)(2,1)S(1)} %pad_maximum_fusion.refs_0_), channel_id=1, source_target_pairs={{0,1},{1,0},{2,3},{3,2},{4,5},{5,4},{6,7},{7,6},{8,9},{9,8},{10,11... | collective-permute-start | bytes 3538952 | tf_op jit(solution)/shard_map/ppermute | solution.py:331
  19.1 22.8 %collective-permute-start.4 = (bf16[768,768]{1,0:T(8,128)(2,1)S(1)}, bf16[768,768]{1,0:T(8,128)(2,1)S(1)}, u32[]{:S(2)}, u32[]{:S(2)}) collective-permute-start(bf16[768,768]{1,0:T(8,128)(2,1)S(1)} %collective-permute-done.3.refs_0_), channel_id=1, source_target_pairs={{0,1},{1,0},{2,3},{3,2},{4,5},{5,4},{6,7},{7,6},{8,9},{9,8},{10,11... | collective-permute-start | bytes 3538952 | tf_op jit(solution)/shard_map/ppermute | solution.py:331
  19.2 24.5 %collective-permute-start.2 = (bf16[768,768]{1,0:T(8,128)(2,1)S(1)}, bf16[768,768]{1,0:T(8,128)(2,1)S(1)}, u32[]{:S(2)}, u32[]{:S(2)}) collective-permute-start(bf16[768,768]{1,0:T(8,128)(2,1)S(1)} %pad_maximum_fusion.1.refs_1_), channel_id=1, source_target_pairs={{1,2},{3,4},{5,6},{2,1},{4,3},{6,5},{9,10},{11,12},{13,14},{10,9},... | collective-permute-start | bytes 3538952 | tf_op jit(solution)/shard_map/ppermute | solution.py:335
  21.6 27.8 %collective-permute-start.1 = (bf16[768,768]{1,0:T(8,128)(2,1)S(1)}, bf16[768,768]{1,0:T(8,128)(2,1)S(1)}, u32[]{:S(2)}, u32[]{:S(2)}) collective-permute-start(bf16[768,768]{1,0:T(8,128)(2,1)S(1)} %collective-permute-done.refs_2_), channel_id=1, source_target_pairs={{1,2},{3,4},{5,6},{2,1},{4,3},{6,5},{9,10},{11,12},{13,14},{10,9},... | collective-permute-start | bytes 3538952 | tf_op jit(solution)/shard_map/ppermute | solution.py:335
  37.0 8.1 %slice-start = ((s8[4718592]{0:T(1024)(128)(4,1)}), s8[4194304]{0:T(1024)(128)(4,1)S(1)}, s32[]{:S(2)}) async-start(s8[4718592]{0:T(1024)(128)(4,1)} %bitcast), calls=%async_computation | async-start | bytes 8388608
  41.9 3.2 %slice-start.1 = ((s8[4718592]{0:T(1024)(128)(4,1)}), s8[524288]{0:T(1024)(128)(4,1)S(1)}, s32[]{:S(2)}) async-start(s8[4718592]{0:T(1024)(128)(4,1)} %bitcast), calls=%async_computation.1 | async-start | bytes 1048576
  45.9 17.3 %collective-permute-start.10 = (bf16[208,1536]{1,0:T(8,128)(2,1)S(1)}, bf16[208,1536]{1,0:T(8,128)(2,1)S(1)}, u32[]{:S(2)}, u32[]{:S(2)}) collective-permute-start(bf16[208,1536]{1,0:T(8,128)(2,1)S(1)} %shard_map.66), channel_id=1, source_target_pairs={{0,8},{8,0},{16,24},{24,16},{1,9},{9,1},{17,25},{25,17},{2,10},{10... | collective-permute-start | bytes 1916936 | tf_op jit(solution)/shard_map/ppermute | solution.py:350
  51.5 24.8 %collective-permute-start.6 = (bf16[208,1536]{1,0:T(8,128)(2,1)S(1)}, bf16[208,1536]{1,0:T(8,128)(2,1)S(1)}, u32[]{:S(2)}, u32[]{:S(2)}) collective-permute-start(bf16[208,1536]{1,0:T(8,128)(2,1)S(1)} %shard_map.60), channel_id=1, source_target_pairs={{0,8},{8,0},{16,24},{24,16},{1,9},{9,1},{17,25},{25,17},{2,10},{10... | collective-permute-start | bytes 1916936 | tf_op jit(solution)/shard_map/ppermute | solution.py:350
  54.3 22.5 %collective-permute-start.11 = (bf16[176,1536]{1,0:T(8,128)(2,1)S(1)}, bf16[176,1536]{1,0:T(8,128)(2,1)S(1)}, u32[]{:S(2)}, u32[]{:S(2)}) collective-permute-start(bf16[176,1536]{1,0:T(8,128)(2,1)S(1)} %shard_map.67), channel_id=1, source_target_pairs={{0,16},{8,24},{16,0},{24,8},{1,17},{9,25},{17,1},{25,9},{2,18},{10... | collective-permute-start | bytes 1622024 | tf_op jit(solution)/shard_map/ppermute | solution.py:350
  55.1 26.1 %collective-permute-start.7 = (bf16[176,1536]{1,0:T(8,128)(2,1)S(1)}, bf16[176,1536]{1,0:T(8,128)(2,1)S(1)}, u32[]{:S(2)}, u32[]{:S(2)}) collective-permute-start(bf16[176,1536]{1,0:T(8,128)(2,1)S(1)} %shard_map.61), channel_id=1, source_target_pairs={{0,16},{8,24},{16,0},{24,8},{1,17},{9,25},{17,1},{25,9},{2,18},{10... | collective-permute-start | bytes 1622024 | tf_op jit(solution)/shard_map/ppermute | solution.py:350
  63.6 24.4 %collective-permute-start.12 = (bf16[208,768]{1,0:T(8,128)(2,1)S(1)}, bf16[208,768]{1,0:T(8,128)(2,1)S(1)}, u32[]{:S(2)}, u32[]{:S(2)}) collective-permute-start(bf16[208,768]{1,0:T(8,128)(2,1)S(1)} %shard_map.69), channel_id=1, source_target_pairs={{0,16},{8,24},{16,0},{24,8},{1,17},{9,25},{17,1},{25,9},{2,18},{10... | collective-permute-start | bytes 958472 | tf_op jit(solution)/shard_map/ppermute | solution.py:350
  76.7 17.5 %collective-permute-start.8 = (bf16[208,768]{1,0:T(8,128)(2,1)S(1)}, bf16[208,768]{1,0:T(8,128)(2,1)S(1)}, u32[]{:S(2)}, u32[]{:S(2)}) collective-permute-start(bf16[208,768]{1,0:T(8,128)(2,1)S(1)} %shard_map.63), channel_id=1, source_target_pairs={{0,16},{8,24},{16,0},{24,8},{1,17},{9,25},{17,1},{25,9},{2,18},{10... | collective-permute-start | bytes 958472 | tf_op jit(solution)/shard_map/ppermute | solution.py:350
  77.2 9.4 %collective-permute-start.13 = (bf16[176,768]{1,0:T(8,128)(2,1)S(1)}, bf16[176,768]{1,0:T(8,128)(2,1)S(1)}, u32[]{:S(2)}, u32[]{:S(2)}) collective-permute-start(bf16[176,768]{1,0:T(8,128)(2,1)S(1)} %shard_map.70), channel_id=1, source_target_pairs={{0,8},{8,0},{16,24},{24,16},{1,9},{9,1},{17,25},{25,17},{2,10},{10... | collective-permute-start | bytes 811016 | tf_op jit(solution)/shard_map/ppermute | solution.py:350
  81.5 9.5 %collective-permute-start.9 = (bf16[176,768]{1,0:T(8,128)(2,1)S(1)}, bf16[176,768]{1,0:T(8,128)(2,1)S(1)}, u32[]{:S(2)}, u32[]{:S(2)}) collective-permute-start(bf16[176,768]{1,0:T(8,128)(2,1)S(1)} %shard_map.64), channel_id=1, source_target_pairs={{0,8},{8,0},{16,24},{24,16},{1,9},{9,1},{17,25},{25,17},{2,10},{10... | collective-permute-start | bytes 811016 | tf_op jit(solution)/shard_map/ppermute | solution.py:350

commit v8 on v7

--- a/solution.py
+++ b/solution.py
@@ -13,7 +13,7 @@
 BF16 = jnp.bfloat16
 VMEM_LIMIT = 16 << 20
 CHUNK = 384
-LEAN = 16
+LEAN = 32
 
 
 def params():
@@ -218,14 +218,15 @@
     return attend_step(head_span, query_tok, [third], {"E": state}, cases, closed={"E": result})[1]["E"]
 
 
-def row_edges(parts):
-    return [0] + [part * FRAME_TOK // parts + LEAN for part in range(1, parts)] + [FRAME_TOK]
-
-
-def project(attended, part, parts, out_weight, slots, received):
+def row_edges(role, parts):
+    lean = LEAN if role == "E" else 0
+    return [0] + [part * FRAME_TOK // parts + lean for part in range(1, parts)] + [FRAME_TOK]
+
+
+def project(role, attended, part, parts, out_weight, slots, received):
     groups = lax.axis_size("head")
     width = out_weight.shape[1] // groups
-    start, stop = row_edges(parts)[part : part + 2]
+    start, stop = row_edges(role, parts)[part : part + 2]
     rows = stop - start
 
     def kernel(left, right, *rest):
@@ -249,10 +250,10 @@
     )(attended, out_weight, *(array for array, _ in received))
 
 
-def sum_own(attended, parts, out_weight, received):
+def sum_own(role, attended, parts, out_weight, received):
     groups = lax.axis_size("head")
     width = out_weight.shape[1] // groups
-    edges = row_edges(parts)
+    edges = row_edges(role, parts)
     flat = [(array, spots[0], part) for part in range(parts) for array, spots in received[part]]
 
     def kernel(left, right, *rest):
@@ -277,15 +278,15 @@
     )(*operands)
 
 
-def finish(own, received, is_edge, frames_here, into):
+def finish(role, own, received, frames_here, into):
     parts = len(received)
-    edges = row_edges(parts)
+    edges = row_edges(role, parts)
     width = own.shape[1]
 
     def kernel(terms, *rest):
         out, buffer, sems = rest[-3:]
         parity = lax.axis_index("frame") % 2
-        frame = parity if is_edge else 1 - parity
+        frame = parity if role == "E" else 1 - parity
         copies = []
         for part in range(parts):
             start, rows = edges[part], edges[part + 1] - edges[part]
@@ -360,7 +361,7 @@
             bit = (part + stage) % bits
             sent = [s for s in held[role][part] if s >> bit & 1]
             kept = [s for s in held[role][part] if not s >> bit & 1]
-            terms = project(attended[role], part, bits, out_weight, sent, gathered(role, part, sent))
+            terms = project(role, attended[role], part, bits, out_weight, sent, gathered(role, part, sent))
             received[role][part].append((exchange(terms, bit), kept))
             held[role][part] = kept
 
@@ -374,8 +375,8 @@
     result = None
     for role in "IE":
         terms = [gathered(role, part, [0]) for part in range(bits)]
-        own = sum_own(attended[role], bits, out_weight, [t[:-1] for t in terms])
-        result = finish(own, [t[-1][0] for t in terms], role == "E", local_frames, result)
+        own = sum_own(role, attended[role], bits, out_weight, [t[:-1] for t in terms])
+        result = finish(role, own, [t[-1][0] for t in terms], local_frames, result)
     return result
 
 

time: 95.5 us -> 100 us (1.047)
  the two profiles are of different devices: /device:TPU:20 before, /device:TPU:16 now
where the time goes in v8:
time: 100 us; the launch traced here: 99.8 us
  waiting for transfers between devices  51.2 us (51%)
  Pallas kernels  25.5 us (26%)
  starting transfers between devices  19.7 us (20%)
  local copies, waits for them, and re-layouts  2.65 us (3%)
    ppermute x8, waiting for transfers between devices, exchange(): lax.ppermute(value, 'head', [(i, i ^ 1 << bit) for i in range(groups)])  29.5 us
    ppermute x3, waiting for transfers between devices, across(): return lax.ppermute(value, 'frame', pairs + [(b, a) for a, b in pairs])  21.7 us
    pallas_call x6, Pallas kernels, attend_step(): pl.pallas_call(kernel, out_shape=tuple(shapes), in_specs=[SMEM] + [VMEM]...  18.2 us
    ppermute x8, starting transfers between devices, exchange(): lax.ppermute(value, 'head', [(i, i ^ 1 << bit) for i in range(groups)])  10.2 us
    ppermute x3, starting transfers between devices, across(): return lax.ppermute(value, 'frame', pairs + [(b, a) for a, b in pairs])  7.6 us
    pallas_call x8, Pallas kernels, project(): pl.pallas_call(kernel, out_shape=jax.ShapeDtypeStruct((rows, len(slots) *...  4.35 us
  transfers between devices with their start and end apart: 14, of which 6 were waited for; matrix products, arithmetic and copies ran while one was open for 0% of the time, Pallas kernels for 22%

profile of v8, /device:TPU:16, one launch (start us, length us, event | category | flops | bytes accessed | tf_op | source)
XLA Modules:
  0.0 99.8 jit_solution(1037583041322154181)
XLA Ops:
  0.0 1.3 %constant_dynamic-slice_fusion.2 = (bf16[384,768]{1,0:T(8,128)(2,1)S(1)}, bf16[384,768]{1,0:T(8,128)(2,1)S(1)}) fusion(bf16[768,768]{1,0:T(8,128)(2,1)} %param.7, s32[]{:T(128)S(6)} %select_n.16, bf16[768,768]{1,0:T(8,128)(2,1)} %param.6), kind=kLoop, calls=%fused_computation.4 | loop fusion | bytes 2359300 | tf_op jit(solution)/shard_map/dynamic_slice | solution.py:32
  1.3 0.0 copy-start.2
  1.3 0.1 pad_maximum_fusion.refs_0_
  1.4 2.1 %collective-permute-start.3 = (bf16[768,768]{1,0:T(8,128)(2,1)S(1)}, bf16[768,768]{1,0:T(8,128)(2,1)S(1)}, u32[]{:S(2)}, u32[]{:S(2)}) collective-permute-start(bf16[768,768]{1,0:T(8,128)(2,1)S(1)} %pad_maximum_fusion.refs_0_), channel_id=1, source_target_pairs={{1,2},{3,4},{5,6},{2,1},{4,3},{6,5},{9,10},{11,12},{13,14},{10,9},... | collective-permute-start | bytes 3538952 | tf_op jit(solution)/shard_map/ppermute | solution.py:336
  3.5 0.0 copy-start.3
  3.6 1.2 %copy-done.3 = bf16[768,768]{1,0:T(8,128)(2,1)S(1)} copy-done((bf16[768,768]{1,0:T(8,128)(2,1)S(1)}, bf16[768,768]{1,0:T(8,128)(2,1)}, u32[]{:S(2)}) %copy-start.3) | copy-done | bytes 1179672
  4.8 0.0 copy-start
  4.8 0.0 copy-start.1
  4.8 0.1 pad_maximum_fusion.1.refs_1_
  4.9 1.7 %collective-permute-start = (bf16[768,768]{1,0:T(8,128)(2,1)S(1)}, bf16[768,768]{1,0:T(8,128)(2,1)S(1)}, u32[]{:S(2)}, u32[]{:S(2)}) collective-permute-start(bf16[768,768]{1,0:T(8,128)(2,1)S(1)} %pad_maximum_fusion.1.refs_1_), channel_id=1, source_target_pairs={{0,1},{1,0},{2,3},{3,2},{4,5},{5,4},{6,7},{7,6},{8,9},{9,8},{10,11... | collective-permute-start | bytes 3538952 | tf_op jit(solution)/shard_map/ppermute | solution.py:332
  6.7 0.1 collective-permute-start.5
  6.8 12.3 %collective-permute-done.3.refs_0_ = bf16[768,768]{1,0:T(8,128)(2,1)S(1)} collective-permute-done((bf16[768,768]{1,0:T(8,128)(2,1)S(1)}, bf16[768,768]{1,0:T(8,128)(2,1)S(1)}, u32[]{:S(2)}, u32[]{:S(2)}) %collective-permute-start.3) | collective-permute-done | bytes 1179680 | tf_op jit(solution)/shard_map/ppermute | solution.py:336
  19.1 0.1 collective-permute-start.4
  19.2 2.3 %collective-permute-start.2 = (bf16[768,768]{1,0:T(8,128)(2,1)S(1)}, bf16[768,768]{1,0:T(8,128)(2,1)S(1)}, u32[]{:S(2)}, u32[]{:S(2)}) collective-permute-start(bf16[768,768]{1,0:T(8,128)(2,1)S(1)} %pad_maximum_fusion.1.refs_1_), channel_id=1, source_target_pairs={{1,2},{3,4},{5,6},{2,1},{4,3},{6,5},{9,10},{11,12},{13,14},{10,9},... | collective-permute-start | bytes 3538952 | tf_op jit(solution)/shard_map/ppermute | solution.py:336
  21.6 3.2 %collective-permute-start.1 = (bf16[768,768]{1,0:T(8,128)(2,1)S(1)}, bf16[768,768]{1,0:T(8,128)(2,1)S(1)}, u32[]{:S(2)}, u32[]{:S(2)}) collective-permute-start(bf16[768,768]{1,0:T(8,128)(2,1)S(1)} %collective-permute-done.refs_2_), channel_id=1, source_target_pairs={{1,2},{3,4},{5,6},{2,1},{4,3},{6,5},{9,10},{11,12},{13,14},{10,9},... | collective-permute-start | bytes 3538952 | tf_op jit(solution)/shard_map/ppermute | solution.py:336
  24.8 8.8 %shard_map.55 = (f32[384,768]{1,0:T(8,128)S(1)}, f32[384,768]{1,0:T(8,128)S(1)}, f32[384,768]{1,0:T(8,128)S(1)}, f32[384,768]{1,0:T(8,128)S(1)}, f32[384,768]{1,0:T(8,128)S(1)}, /*index=5*/f32[384,768]{1,0:T(8,128)S(1)}) custom-call(s32[6]{0:T(128)S(1)} %copy-done.1, bf16[768,768]{1,0:T(8,128)(2,1)S(1)} %copy-done, ...), custom_call_target="tpu_custom_call" | custom-call | tf_op jit(solution)/shard_map/pallas_call | solution.py:155
  33.6 2.9 %shard_map.56 = (f32[384,768]{1,0:T(8,128)S(1)}, f32[384,768]{1,0:T(8,128)S(1)}, f32[384,768]{1,0:T(8,128)S(1)}, f32[384,768]{1,0:T(8,128)S(1)}, f32[384,768]{1,0:T(8,128)S(1)}, /*index=5*/f32[384,768]{1,0:T(8,128)S(1)}) custom-call(s32[6]{0:T(128)S(1)} %copy-done.1, ...), custom_call_target="tpu_custom_call", output_to_operand_aliasing={{0}: (3, {}), {1}: (4, {}), {2}: (5, {}), {3}: (6, {}), {4}... | custom-call | tf_op jit(solution)/shard_map/pallas_call | solution.py:155
  36.5 0.0 slice-start
  36.5 1.9 %shard_map.57 = (f32[384,768]{1,0:T(8,128)S(1)}, f32[384,768]{1,0:T(8,128)S(1)}, f32[384,768]{1,0:T(8,128)S(1)}, f32[384,768]{1,0:T(8,128)S(1)}, f32[384,768]{1,...) custom-call(s32[6]{0:T(128)S(1)} %copy-done.1, ...), custom_call_target="tpu_custom_call", output_to_operand_aliasing={{0}: (3, {}), {1}: (4, {}), {2}: (5, {}), {3}: (6, {}), {4}... | custom-call | tf_op jit(solution)/shard_map/pallas_call | solution.py:155
  38.4 0.0 slice-start.1
  38.5 1.5 %shard_map.58 = (f32[384,768]{1,0:T(8,128)S(1)}, f32[384,768]{1,0:T(8,128)S(1)}, f32[384,768]{1,0:T(8,128)S(1)}, bf16[384,768]{1,0:T(8,128)(2,1)S(1)}) custom-call(s32[6]{0:T(128)S(1)} %copy-done.1, bf16[768,768]{1,0:T(8,128)(2,1)S(1)} %copy-done, ...), custom_call_target="tpu_custom_call", output_to_operand_aliasing={{0}: (3, {}), {1}: (4, {}), {2}: (5, {}), {3}: (6, {})} | custom-call | tf_op jit(solution)/shard_map/pallas_call | solution.py:155
  40.0 9.3 %collective-permute-done.1.refs_0_ = bf16[768,768]{1,0:T(8,128)(2,1)S(1)} collective-permute-done((bf16[768,768]{1,0:T(8,128)(2,1)S(1)}, bf16[768,768]{1,0:T(8,128)(2,1)S(1)}, u32[]{:S(2)}, u32[]{:S(2)}) %collective-permute-start.1) | collective-permute-done | bytes 1179680 | tf_op jit(solution)/shard_map/ppermute | solution.py:336
  49.3 1.6 %shard_map.59.left = bf16[384,768]{1,0:T(8,128)(2,1)S(1)} custom-call(s32[6]{0:T(128)S(1)} %copy-done.1, bf16[768,768]{1,0:T(8,128)(2,1)S(1)} %copy-done, bf16[768,768]{1,0:T(8,128)(2,1)S(1)} %collective-permute-done.1.refs_0_, f32[384,768]{1,0:T(8,128)S(1)} %get-tuple-element.51.refs_1_, ...), custom_call_target="tpu_custom_call", output_to_operand_aliasing={{}: (6, {})} | custom-call | tf_op jit(solution)/shard_map/pallas_call | solution.py:155
  51.0 0.7 shard_map.60
  51.8 1.5 %collective-permute-start.6 = (bf16[224,1536]{1,0:T(8,128)(2,1)S(1)}, bf16[224,1536]{1,0:T(8,128)(2,1)S(1)}, u32[]{:S(2)}, u32[]{:S(2)}) collective-permute-start(bf16[224,1536]{1,0:T(8,128)(2,1)S(1)} %shard_map.60), channel_id=1, source_target_pairs={{0,8},{8,0},{16,24},{24,16},{1,9},{9,1},{17,25},{25,17},{2,10},{10... | collective-permute-start | bytes 2064392 | tf_op jit(solution)/shard_map/ppermute | solution.py:351
  53.3 1.4 %shard_map.65.left = bf16[384,768]{1,0:T(8,128)(2,1)S(1)} custom-call(s32[6]{0:T(128)S(1)} %copy-done.1, bf16[768,768]{1,0:T(8,128)(2,1)S(1)} %copy-done, bf16[768,768]{1,0:T(8,128)(2,1)S(1)} %collective-permute-done.2.refs_0_, f32[384,768]{1,0:T(8,128)S(1)} %get-tuple-element.55.refs_1_, ...), custom_call_target="tpu_custom_call", output_to_operand_aliasing={{}: (6, {})} | custom-call | tf_op jit(solution)/shard_map/pallas_call | solution.py:155
  54.7 0.7 shard_map.66
  55.4 0.6 collective-permute-start.10
  56.0 0.7 shard_map.67
  56.7 2.3 %collective-permute-start.11 = (bf16[192,1536]{1,0:T(8,128)(2,1)S(1)}, bf16[192,1536]{1,0:T(8,128)(2,1)S(1)}, u32[]{:S(2)}, u32[]{:S(2)}) collective-permute-start(bf16[192,1536]{1,0:T(8,128)(2,1)S(1)} %shard_map.67), channel_id=1, source_target_pairs={{0,16},{8,24},{16,0},{24,8},{1,17},{9,25},{17,1},{25,9},{2,18},{10... | collective-permute-start | bytes 1769480 | tf_op jit(solution)/shard_map/ppermute | solution.py:351
  59.0 0.6 shard_map.61
  59.5 0.1 collective-permute-start.7
  59.6 10.5 %collective-permute-done.6.rest_0_ = bf16[224,1536]{1,0:T(8,128)(2,1)S(1)} collective-permute-done((bf16[224,1536]{1,0:T(8,128)(2,1)S(1)}, bf16[224,1536]{1,0:T(8,128)(2,1)S(1)}, u32[]{:S(2)}, u32[]{:S(2)}) %collective-permute-start.6) | collective-permute-done | bytes 688160 | tf_op jit(solution)/shard_map/ppermute | solution.py:351
  70.1 0.5 shard_map.63
  70.6 1.7 %collective-permute-start.8 = (bf16[224,768]{1,0:T(8,128)(2,1)S(1)}, bf16[224,768]{1,0:T(8,128)(2,1)S(1)}, u32[]{:S(2)}, u32[]{:S(2)}) collective-permute-start(bf16[224,768]{1,0:T(8,128)(2,1)S(1)} %shard_map.63), channel_id=1, source_target_pairs={{0,16},{8,24},{16,0},{24,8},{1,17},{9,25},{17,1},{25,9},{2,18},{10... | collective-permute-start | bytes 1032200 | tf_op jit(solution)/shard_map/ppermute | solution.py:351
  72.3 9.9 %collective-permute-done.10.rest_0_ = bf16[192,1536]{1,0:T(8,128)(2,1)S(1)} collective-permute-done((bf16[192,1536]{1,0:T(8,128)(2,1)S(1)}, bf16[192,1536]{1,0:T(8,128)(2,1)S(1)}, u32[]{:S(2)}, u32[]{:S(2)}) %collective-permute-start.10) | collective-permute-done | bytes 589856 | tf_op jit(solution)/shard_map/ppermute | solution.py:351
  82.2 0.4 shard_map.69
  82.6 1.9 %collective-permute-start.12 = (bf16[192,768]{1,0:T(8,128)(2,1)S(1)}, bf16[192,768]{1,0:T(8,128)(2,1)S(1)}, u32[]{:S(2)}, u32[]{:S(2)}) collective-permute-start(bf16[192,768]{1,0:T(8,128)(2,1)S(1)} %shard_map.69), channel_id=1, source_target_pairs={{0,16},{8,24},{16,0},{24,8},{1,17},{9,25},{17,1},{25,9},{2,18},{10... | collective-permute-start | bytes 884744 | tf_op jit(solution)/shard_map/ppermute | solution.py:351
  84.6 0.4 shard_map.70
  85.0 1.8 %collective-permute-start.13 = (bf16[192,768]{1,0:T(8,128)(2,1)S(1)}, bf16[192,768]{1,0:T(8,128)(2,1)S(1)}, u32[]{:S(2)}, u32[]{:S(2)}) collective-permute-start(bf16[192,768]{1,0:T(8,128)(2,1)S(1)} %shard_map.70), channel_id=1, source_target_pairs={{0,8},{8,0},{16,24},{24,16},{1,9},{9,1},{17,25},{25,17},{2,10},{10... | collective-permute-start | bytes 884744 | tf_op jit(solution)/shard_map/ppermute | solution.py:351
  86.8 0.4 shard_map.64
  87.2 0.3 collective-permute-start.9
  87.5 0.6 shard_map.68.terms
  88.2 0.6 shard_map.62.terms
  88.8 8.0 %collective-permute-done.12.rest_0_ = bf16[192,768]{1,0:T(8,128)(2,1)S(1)} collective-permute-done((bf16[192,768]{1,0:T(8,128)(2,1)S(1)}, bf16[192,768]{1,0:T(8,128)(2,1)S(1)}, u32[]{:S(2)}, u32[]{:S(2)}) %collective-permute-start.12) | collective-permute-done | bytes 294944 | tf_op jit(solution)/shard_map/ppermute | solution.py:351
  96.8 0.9 shard_map.71.rest_2_
  97.7 1.1 %collective-permute-done.9.rest_1_ = bf16[160,768]{1,0:T(8,128)(2,1)S(1)} collective-permute-done((bf16[160,768]{1,0:T(8,128)(2,1)S(1)}, bf16[160,768]{1,0:T(8,128)(2,1)S(1)}, u32[]{:S(2)}, u32[]{:S(2)}) %collective-permute-start.9) | collective-permute-done | bytes 245792 | tf_op jit(solution)/shard_map/ppermute | solution.py:351
  98.8 0.9 shard_map.72
  (16 shorter events, 0.1 us)
Async XLA Ops:
  1.3 2.2 %copy-start.2 = (bf16[768,768]{1,0:T(8,128)(2,1)S(1)}, bf16[768,768]{1,0:T(8,128)(2,1)}, u32[]{:S(2)}) copy-start(bf16[768,768]{1,0:T(8,128)(2,1)} %param.6) | copy-start | bytes 3538948
  1.4 17.7 %collective-permute-start.3 = (bf16[768,768]{1,0:T(8,128)(2,1)S(1)}, bf16[768,768]{1,0:T(8,128)(2,1)S(1)}, u32[]{:S(2)}, u32[]{:S(2)}) collective-permute-start(bf16[768,768]{1,0:T(8,128)(2,1)S(1)} %pad_maximum_fusion.refs_0_), channel_id=1, source_target_pairs={{1,2},{3,4},{5,6},{2,1},{4,3},{6,5},{9,10},{11,12},{13,14},{10,9},... | collective-permute-start | bytes 3538952 | tf_op jit(solution)/shard_map/ppermute | solution.py:336
  3.5 1.3 %copy-start.3 = (bf16[768,768]{1,0:T(8,128)(2,1)S(1)}, bf16[768,768]{1,0:T(8,128)(2,1)}, u32[]{:S(2)}) copy-start(bf16[768,768]{1,0:T(8,128)(2,1)} %param.7) | copy-start | bytes 3538948
  4.8 20.0 %copy-start = (bf16[768,768]{1,0:T(8,128)(2,1)S(1)}, bf16[768,768]{1,0:T(8,128)(2,1)}, u32[]{:S(2)}) copy-start(bf16[768,768]{1,0:T(8,128)(2,1)} %query.11) | copy-start | bytes 3538948
  4.8 20.0 %copy-start.1 = (s32[6]{0:T(128)S(1)}, s32[6]{0:T(128)}, u32[]{:S(2)}) copy-start(s32[6]{0:T(128)} %span_ref.11) | copy-start | bytes 76
  4.9 16.6 %collective-permute-start = (bf16[768,768]{1,0:T(8,128)(2,1)S(1)}, bf16[768,768]{1,0:T(8,128)(2,1)S(1)}, u32[]{:S(2)}, u32[]{:S(2)}) collective-permute-start(bf16[768,768]{1,0:T(8,128)(2,1)S(1)} %pad_maximum_fusion.1.refs_1_), channel_id=1, source_target_pairs={{0,1},{1,0},{2,3},{3,2},{4,5},{5,4},{6,7},{7,6},{8,9},{9,8},{10,11... | collective-permute-start | bytes 3538952 | tf_op jit(solution)/shard_map/ppermute | solution.py:332
  6.7 18.1 %collective-permute-start.5 = (bf16[768,768]{1,0:T(8,128)(2,1)S(1)}, bf16[768,768]{1,0:T(8,128)(2,1)S(1)}, u32[]{:S(2)}, u32[]{:S(2)}) collective-permute-start(bf16[768,768]{1,0:T(8,128)(2,1)S(1)} %pad_maximum_fusion.refs_0_), channel_id=1, source_target_pairs={{0,1},{1,0},{2,3},{3,2},{4,5},{5,4},{6,7},{7,6},{8,9},{9,8},{10,11... | collective-permute-start | bytes 3538952 | tf_op jit(solution)/shard_map/ppermute | solution.py:332
  19.1 17.4 %collective-permute-start.4 = (bf16[768,768]{1,0:T(8,128)(2,1)S(1)}, bf16[768,768]{1,0:T(8,128)(2,1)S(1)}, u32[]{:S(2)}, u32[]{:S(2)}) collective-permute-start(bf16[768,768]{1,0:T(8,128)(2,1)S(1)} %collective-permute-done.3.refs_0_), channel_id=1, source_target_pairs={{0,1},{1,0},{2,3},{3,2},{4,5},{5,4},{6,7},{7,6},{8,9},{9,8},{10,11... | collective-permute-start | bytes 3538952 | tf_op jit(solution)/shard_map/ppermute | solution.py:332
  19.2 19.2 %collective-permute-start.2 = (bf16[768,768]{1,0:T(8,128)(2,1)S(1)}, bf16[768,768]{1,0:T(8,128)(2,1)S(1)}, u32[]{:S(2)}, u32[]{:S(2)}) collective-permute-start(bf16[768,768]{1,0:T(8,128)(2,1)S(1)} %pad_maximum_fusion.1.refs_1_), channel_id=1, source_target_pairs={{1,2},{3,4},{5,6},{2,1},{4,3},{6,5},{9,10},{11,12},{13,14},{10,9},... | collective-permute-start | bytes 3538952 | tf_op jit(solution)/shard_map/ppermute | solution.py:336
  21.6 27.8 %collective-permute-start.1 = (bf16[768,768]{1,0:T(8,128)(2,1)S(1)}, bf16[768,768]{1,0:T(8,128)(2,1)S(1)}, u32[]{:S(2)}, u32[]{:S(2)}) collective-permute-start(bf16[768,768]{1,0:T(8,128)(2,1)S(1)} %collective-permute-done.refs_2_), channel_id=1, source_target_pairs={{1,2},{3,4},{5,6},{2,1},{4,3},{6,5},{9,10},{11,12},{13,14},{10,9},... | collective-permute-start | bytes 3538952 | tf_op jit(solution)/shard_map/ppermute | solution.py:336
  36.5 14.5 %slice-start = ((s8[4718592]{0:T(1024)(128)(4,1)}), s8[524288]{0:T(1024)(128)(4,1)S(1)}, s32[]{:S(2)}) async-start(s8[4718592]{0:T(1024)(128)(4,1)} %bitcast), calls=%async_computation | async-start | bytes 1048576
  38.4 12.6 %slice-start.1 = ((s8[4718592]{0:T(1024)(128)(4,1)}), s8[4194304]{0:T(1024)(128)(4,1)S(1)}, s32[]{:S(2)}) async-start(s8[4718592]{0:T(1024)(128)(4,1)} %bitcast), calls=%async_computation.1 | async-start | bytes 8388608
  51.8 18.4 %collective-permute-start.6 = (bf16[224,1536]{1,0:T(8,128)(2,1)S(1)}, bf16[224,1536]{1,0:T(8,128)(2,1)S(1)}, u32[]{:S(2)}, u32[]{:S(2)}) collective-permute-start(bf16[224,1536]{1,0:T(8,128)(2,1)S(1)} %shard_map.60), channel_id=1, source_target_pairs={{0,8},{8,0},{16,24},{24,16},{1,9},{9,1},{17,25},{25,17},{2,10},{10... | collective-permute-start | bytes 2064392 | tf_op jit(solution)/shard_map/ppermute | solution.py:351
  55.4 26.8 %collective-permute-start.10 = (bf16[192,1536]{1,0:T(8,128)(2,1)S(1)}, bf16[192,1536]{1,0:T(8,128)(2,1)S(1)}, u32[]{:S(2)}, u32[]{:S(2)}) collective-permute-start(bf16[192,1536]{1,0:T(8,128)(2,1)S(1)} %shard_map.66), channel_id=1, source_target_pairs={{0,8},{8,0},{16,24},{24,16},{1,9},{9,1},{17,25},{25,17},{2,10},{10... | collective-permute-start | bytes 1769480 | tf_op jit(solution)/shard_map/ppermute | solution.py:351
  56.7 27.8 %collective-permute-start.11 = (bf16[192,1536]{1,0:T(8,128)(2,1)S(1)}, bf16[192,1536]{1,0:T(8,128)(2,1)S(1)}, u32[]{:S(2)}, u32[]{:S(2)}) collective-permute-start(bf16[192,1536]{1,0:T(8,128)(2,1)S(1)} %shard_map.67), channel_id=1, source_target_pairs={{0,16},{8,24},{16,0},{24,8},{1,17},{9,25},{17,1},{25,9},{2,18},{10... | collective-permute-start | bytes 1769480 | tf_op jit(solution)/shard_map/ppermute | solution.py:351
  59.5 27.2 %collective-permute-start.7 = (bf16[160,1536]{1,0:T(8,128)(2,1)S(1)}, bf16[160,1536]{1,0:T(8,128)(2,1)S(1)}, u32[]{:S(2)}, u32[]{:S(2)}) collective-permute-start(bf16[160,1536]{1,0:T(8,128)(2,1)S(1)} %shard_map.61), channel_id=1, source_target_pairs={{0,16},{8,24},{16,0},{24,8},{1,17},{9,25},{17,1},{25,9},{2,18},{10... | collective-permute-start | bytes 1474568 | tf_op jit(solution)/shard_map/ppermute | solution.py:351
  70.6 28.2 %collective-permute-start.8 = (bf16[224,768]{1,0:T(8,128)(2,1)S(1)}, bf16[224,768]{1,0:T(8,128)(2,1)S(1)}, u32[]{:S(2)}, u32[]{:S(2)}) collective-permute-start(bf16[224,768]{1,0:T(8,128)(2,1)S(1)} %shard_map.63), channel_id=1, source_target_pairs={{0,16},{8,24},{16,0},{24,8},{1,17},{9,25},{17,1},{25,9},{2,18},{10... | collective-permute-start | bytes 1032200 | tf_op jit(solution)/shard_map/ppermute | solution.py:351
  82.6 14.2 %collective-permute-start.12 = (bf16[192,768]{1,0:T(8,128)(2,1)S(1)}, bf16[192,768]{1,0:T(8,128)(2,1)S(1)}, u32[]{:S(2)}, u32[]{:S(2)}) collective-permute-start(bf16[192,768]{1,0:T(8,128)(2,1)S(1)} %shard_map.69), channel_id=1, source_target_pairs={{0,16},{8,24},{16,0},{24,8},{1,17},{9,25},{17,1},{25,9},{2,18},{10... | collective-permute-start | bytes 884744 | tf_op jit(solution)/shard_map/ppermute | solution.py:351
  85.0 11.8 %collective-permute-start.13 = (bf16[192,768]{1,0:T(8,128)(2,1)S(1)}, bf16[192,768]{1,0:T(8,128)(2,1)S(1)}, u32[]{:S(2)}, u32[]{:S(2)}) collective-permute-start(bf16[192,768]{1,0:T(8,128)(2,1)S(1)} %shard_map.70), channel_id=1, source_target_pairs={{0,8},{8,0},{16,24},{24,16},{1,9},{9,1},{17,25},{25,17},{2,10},{10... | collective-permute-start | bytes 884744 | tf_op jit(solution)/shard_map/ppermute | solution.py:351
  87.2 11.6 %collective-permute-start.9 = (bf16[160,768]{1,0:T(8,128)(2,1)S(1)}, bf16[160,768]{1,0:T(8,128)(2,1)S(1)}, u32[]{:S(2)}, u32[]{:S(2)}) collective-permute-start(bf16[160,768]{1,0:T(8,128)(2,1)S(1)} %shard_map.64), channel_id=1, source_target_pairs={{0,8},{8,0},{16,24},{24,16},{1,9},{9,1},{17,25},{25,17},{2,10},{10... | collective-permute-start | bytes 737288 | tf_op jit(solution)/shard_map/ppermute | solution.py:351

commit v9 on v8

--- a/solution.py
+++ b/solution.py
@@ -25,16 +25,31 @@
 HBM = pl.BlockSpec(memory_space=pltpu.HBM)
 
 
-def pack_frames(key_tok, value_tok):
-    parity = lax.axis_index("frame") % 2
-
-    def packed(key, value, frame):
-        rows = [lax.dynamic_slice_in_dim(array, frame * FRAME_TOK, FRAME_TOK, 0) for array in (key, value)]
-        return jnp.concatenate(rows, axis=0)
-
-    edge = packed(key_tok, value_tok, parity)
-    edge, key_tok, value_tok = lax.optimization_barrier((edge, key_tok, value_tok))
-    return edge, packed(key_tok, value_tok, 1 - parity)
+def pack_frame(key_tok, value_tok, is_edge):
+    def kernel(key, value, out, sems):
+        parity = lax.axis_index("frame") % 2
+        frame = parity if is_edge else 1 - parity
+        copies = [
+            pltpu.make_async_copy(
+                source.at[pl.ds(pl.multiple_of(frame * FRAME_TOK, FRAME_TOK), FRAME_TOK)],
+                out.at[pl.ds(place * FRAME_TOK, FRAME_TOK)],
+                sems.at[place],
+            )
+            for place, source in enumerate((key, value))
+        ]
+        for copy in copies:
+            copy.start()
+        for copy in copies:
+            copy.wait()
+
+    return pl.pallas_call(
+        kernel,
+        out_shape=jax.ShapeDtypeStruct((2 * FRAME_TOK, key_tok.shape[1]), BF16),
+        in_specs=[HBM, HBM],
+        out_specs=VMEM,
+        scratch_shapes=[pltpu.SemaphoreType.DMA((2,))],
+        compiler_params=params(),
+    )(pltpu.with_memory_space_constraint(key_tok, pltpu.HBM), pltpu.with_memory_space_constraint(value_tok, pltpu.HBM))
 
 
 def attend_step(head_span, query_tok, sources, states, cases, first=False, closed=None):
@@ -278,32 +293,23 @@
     )(*operands)
 
 
-def finish(role, own, received, frames_here, into):
-    parts = len(received)
-    edges = row_edges(role, parts)
+def finish(role, own, received, part, parts, frames_here, into):
+    start, stop = row_edges(role, parts)[part : part + 2]
+    rows = stop - start
     width = own.shape[1]
 
-    def kernel(terms, *rest):
-        out, buffer, sems = rest[-3:]
+    def kernel(terms, last, *rest):
+        out, buffer, sem = rest[-3:]
         parity = lax.axis_index("frame") % 2
         frame = parity if role == "E" else 1 - parity
-        copies = []
-        for part in range(parts):
-            start, rows = edges[part], edges[part + 1] - edges[part]
-            span = slice(start, start + rows)
-            buffer[span, :] = (terms[span, :] + rest[part][...].astype(F32)).astype(BF16)
-            copies.append(
-                pltpu.make_async_copy(
-                    buffer.at[pl.ds(start, rows)],
-                    out.at[pl.ds(pl.multiple_of(frame * FRAME_TOK + start, 16), rows)],
-                    sems.at[part],
-                )
-            )
-            copies[-1].start()
-        for copy in copies:
-            copy.wait()
-
-    operands = [own, *received]
+        buffer[...] = (terms[start:stop, :] + last[...].astype(F32)).astype(BF16)
+        copy = pltpu.make_async_copy(
+            buffer, out.at[pl.ds(pl.multiple_of(frame * FRAME_TOK + start, 16), rows)], sem
+        )
+        copy.start()
+        copy.wait()
+
+    operands = [own, received]
     in_specs = [VMEM] * len(operands)
     aliases = {}
     if into is not None:
@@ -315,7 +321,7 @@
         out_shape=jax.ShapeDtypeStruct((frames_here * FRAME_TOK, width), BF16),
         in_specs=in_specs,
         out_specs=HBM,
-        scratch_shapes=[pltpu.VMEM((FRAME_TOK, width), BF16), pltpu.SemaphoreType.DMA((parts,))],
+        scratch_shapes=[pltpu.VMEM((rows, width), BF16), pltpu.SemaphoreType.DMA(())],
         input_output_aliases=aliases,
         compiler_params=params(),
     )(*operands)
@@ -335,7 +341,8 @@
         pairs = [(i, i + 1) for i in range(1, frames - 1, 2)]
         return lax.ppermute(value, "frame", pairs + [(b, a) for a, b in pairs])
 
-    edge, inner = pack_frames(key_tok, value_tok)
+    edge = pack_frame(key_tok, value_tok, True)
+    inner = pack_frame(key_tok, value_tok, False)
     near = across(edge)
     partner_inner = swap(inner)
     partner_edge = swap(edge)
@@ -376,7 +383,8 @@
     for role in "IE":
         terms = [gathered(role, part, [0]) for part in range(bits)]
         own = sum_own(role, attended[role], bits, out_weight, [t[:-1] for t in terms])
-        result = finish(role, own, [t[-1][0] for t in terms], local_frames, result)
+        for part in reversed(range(bits)):
+            result = finish(role, own, terms[part][-1][0], part, bits, local_frames, result)
     return result
 
 

time: 100 us -> 98.3 us (0.983)
  the two profiles are of different devices: /device:TPU:16 before, /device:TPU:20 now
where the time goes in v9:
time: 98.3 us; the launch traced here: 98.1 us
  waiting for transfers between devices  43.6 us (44%)
  Pallas kernels  36 us (37%)
  starting transfers between devices  17.9 us (18%)
    ppermute x8, waiting for transfers between devices, exchange(): lax.ppermute(value, 'head', [(i, i ^ 1 << bit) for i in range(groups)])  28.4 us
    pallas_call x6, Pallas kernels, attend_step(): pl.pallas_call(kernel, out_shape=tuple(shapes), in_specs=[SMEM] + [VMEM]...  24.8 us
    ppermute x3, waiting for transfers between devices, across(): return lax.ppermute(value, 'frame', pairs + [(b, a) for a, b in pairs])  15.2 us
    ppermute x8, starting transfers between devices, exchange(): lax.ppermute(value, 'head', [(i, i ^ 1 << bit) for i in range(groups)])  8.35 us
    ppermute x3, starting transfers between devices, across(): return lax.ppermute(value, 'frame', pairs + [(b, a) for a, b in pairs])  7.6 us
    pallas_call x8, Pallas kernels, project(): pl.pallas_call(kernel, out_shape=jax.ShapeDtypeStruct((rows, len(slots) *...  4.28 us
    pallas_call x4, Pallas kernels, finish(): pl.pallas_call(kernel, out_shape=jax.ShapeDtypeStruct((frames_here * FRAM...  3.09 us
    pallas_call x2, Pallas kernels, pack_frame(): pl.pallas_call(kernel, out_shape=jax.ShapeDtypeStruct((2 * FRAME_TOK, key...  2.53 us
  transfers between devices with their start and end apart: 14, of which 7 were waited for; matrix products, arithmetic and copies ran while one was open for 0% of the time, Pallas kernels for 32%

profile of v9, /device:TPU:20, one launch (start us, length us, event | category | flops | bytes accessed | tf_op | source)
XLA Modules:
  0.0 98.1 jit_solution(15927178305126373542)
XLA Ops:
  0.0 1.3 %shard_map.56.refs_0_ = bf16[768,768]{1,0:T(8,128)(2,1)S(1)} custom-call(bf16[768,768]{1,0:T(8,128)(2,1)} %key.3, bf16[768,768]{1,0:T(8,128)(2,1)} %value.3), custom_call_target="tpu_custom_call" | custom-call | tf_op jit(solution)/shard_map/pallas_call | solution.py:45
  1.3 0.0 copy-start
  1.3 0.0 copy-start.1
  1.3 2.1 %collective-permute-start.3 = (bf16[768,768]{1,0:T(8,128)(2,1)S(1)}, bf16[768,768]{1,0:T(8,128)(2,1)S(1)}, u32[]{:S(2)}, u32[]{:S(2)}) collective-permute-start(bf16[768,768]{1,0:T(8,128)(2,1)S(1)} %shard_map.56.refs_0_), channel_id=1, source_target_pairs={{1,2},{3,4},{5,6},{2,1},{4,3},{6,5},{9,10},{11,12},{13,14},{10,9},... | collective-permute-start | bytes 3538952 | tf_op jit(solution)/shard_map/ppermute | solution.py:342
  3.4 1.3 %shard_map.55.refs_1_ = bf16[768,768]{1,0:T(8,128)(2,1)S(1)} custom-call(bf16[768,768]{1,0:T(8,128)(2,1)} %key.3, bf16[768,768]{1,0:T(8,128)(2,1)} %value.3), custom_call_target="tpu_custom_call" | custom-call | tf_op jit(solution)/shard_map/pallas_call | solution.py:45
  4.6 1.7 %collective-permute-start = (bf16[768,768]{1,0:T(8,128)(2,1)S(1)}, bf16[768,768]{1,0:T(8,128)(2,1)S(1)}, u32[]{:S(2)}, u32[]{:S(2)}) collective-permute-start(bf16[768,768]{1,0:T(8,128)(2,1)S(1)} %shard_map.55.refs_1_), channel_id=1, source_target_pairs={{0,1},{1,0},{2,3},{3,2},{4,5},{5,4},{6,7},{7,6},{8,9},{9,8},{10,11... | collective-permute-start | bytes 3538952 | tf_op jit(solution)/shard_map/ppermute | solution.py:338
  6.4 0.1 collective-permute-start.5
  6.5 12.5 %collective-permute-done.3.refs_0_ = bf16[768,768]{1,0:T(8,128)(2,1)S(1)} collective-permute-done((bf16[768,768]{1,0:T(8,128)(2,1)S(1)}, bf16[768,768]{1,0:T(8,128)(2,1)S(1)}, u32[]{:S(2)}, u32[]{:S(2)}) %collective-permute-start.3) | collective-permute-done | bytes 1179680 | tf_op jit(solution)/shard_map/ppermute | solution.py:342
  18.9 0.1 collective-permute-start.4
  19.1 2.3 %collective-permute-start.2 = (bf16[768,768]{1,0:T(8,128)(2,1)S(1)}, bf16[768,768]{1,0:T(8,128)(2,1)S(1)}, u32[]{:S(2)}, u32[]{:S(2)}) collective-permute-start(bf16[768,768]{1,0:T(8,128)(2,1)S(1)} %shard_map.55.refs_1_), channel_id=1, source_target_pairs={{1,2},{3,4},{5,6},{2,1},{4,3},{6,5},{9,10},{11,12},{13,14},{10,9},... | collective-permute-start | bytes 3538952 | tf_op jit(solution)/shard_map/ppermute | solution.py:342
  21.4 0.0 collective-permute-done.refs_2_
  21.4 3.2 %collective-permute-start.1 = (bf16[768,768]{1,0:T(8,128)(2,1)S(1)}, bf16[768,768]{1,0:T(8,128)(2,1)S(1)}, u32[]{:S(2)}, u32[]{:S(2)}) collective-permute-start(bf16[768,768]{1,0:T(8,128)(2,1)S(1)} %collective-permute-done.refs_2_), channel_id=1, source_target_pairs={{1,2},{3,4},{5,6},{2,1},{4,3},{6,5},{9,10},{11,12},{13,14},{10,9},... | collective-permute-start | bytes 3538952 | tf_op jit(solution)/shard_map/ppermute | solution.py:342
  24.7 12.2 %shard_map.57 = (f32[384,768]{1,0:T(8,128)S(1)}, f32[384,768]{1,0:T(8,128)S(1)}, f32[384,768]{1,0:T(8,128)S(1)}, f32[384,768]{1,0:T(8,128)S(1)}, f32[384,768]{1,0:T(8,128)S(1)}, /*index=5*/f32[384,768]{1,0:T(8,128)S(1)}) custom-call(s32[6]{0:T(128)S(1)} %copy-done.1, bf16[768,768]{1,0:T(8,128)(2,1)S(1)} %copy-done, bf16[768,768]{1,0:T(8,128)(2,1)S(1)} %shard_map.56.refs_0_, ...), custom_call_target="tpu_custom_call" | custom-call | tf_op jit(solution)/shard_map/pallas_call | solution.py:170
  36.8 4.9 %shard_map.58 = (f32[384,768]{1,0:T(8,128)S(1)}, f32[384,768]{1,0:T(8,128)S(1)}, f32[384,768]{1,0:T(8,128)S(1)}, f32[384,768]{1,0:T(8,128)S(1)}, f32[384,768]{1,0:T(8,128)S(1)}, /*index=5*/f32[384,768]{1,0:T(8,128)S(1)}) custom-call(s32[6]{0:T(128)S(1)} %copy-done.1, ...), custom_call_target="tpu_custom_call", output_to_operand_aliasing={{0}: (3, {}), {1}: (4, {}), {2}: (5, {}), {3}: (6, {}), {4}... | custom-call | tf_op jit(solution)/shard_map/pallas_call | solution.py:170
  41.7 0.0 slice-start
  41.7 1.8 %shard_map.59 = (f32[384,768]{1,0:T(8,128)S(1)}, f32[384,768]{1,0:T(8,128)S(1)}, f32[384,768]{1,0:T(8,128)S(1)}, f32[384,768]{1,0:T(8,128)S(1)}, f32[384,768]{1,...) custom-call(s32[6]{0:T(128)S(1)} %copy-done.1, ...), custom_call_target="tpu_custom_call", output_to_operand_aliasing={{0}: (3, {}), {1}: (4, {}), {2}: (5, {}), {3}: (6, {}), {4}... | custom-call | tf_op jit(solution)/shard_map/pallas_call | solution.py:170
  43.5 0.0 slice-start.1
  43.5 2.9 %shard_map.60 = (f32[384,768]{1,0:T(8,128)S(1)}, f32[384,768]{1,0:T(8,128)S(1)}, f32[384,768]{1,0:T(8,128)S(1)}, bf16[384,768]{1,0:T(8,128)(2,1)S(1)}) custom-call(s32[6]{0:T(128)S(1)} %copy-done.1, bf16[768,768]{1,0:T(8,128)(2,1)S(1)} %copy-done, ...), custom_call_target="tpu_custom_call", output_to_operand_aliasing={{0}: (3, {}), {1}: (4, {}), {2}: (5, {}), {3}: (6, {})} | custom-call | tf_op jit(solution)/shard_map/pallas_call | solution.py:170
  46.5 2.7 %collective-permute-done.1.refs_0_ = bf16[768,768]{1,0:T(8,128)(2,1)S(1)} collective-permute-done((bf16[768,768]{1,0:T(8,128)(2,1)S(1)}, bf16[768,768]{1,0:T(8,128)(2,1)S(1)}, u32[]{:S(2)}, u32[]{:S(2)}) %collective-permute-start.1) | collective-permute-done | bytes 1179680 | tf_op jit(solution)/shard_map/ppermute | solution.py:342
  49.2 1.6 %shard_map.61.left = bf16[384,768]{1,0:T(8,128)(2,1)S(1)} custom-call(s32[6]{0:T(128)S(1)} %copy-done.1, bf16[768,768]{1,0:T(8,128)(2,1)S(1)} %copy-done, bf16[768,768]{1,0:T(8,128)(2,1)S(1)} %collective-permute-done.1.refs_0_, f32[384,768]{1,0:T(8,128)S(1)} %get-tuple-element.45.refs_1_, ...), custom_call_target="tpu_custom_call", output_to_operand_aliasing={{}: (6, {})} | custom-call | tf_op jit(solution)/shard_map/pallas_call | solution.py:170
  50.9 0.7 shard_map.62
  51.7 2.2 %collective-permute-start.6 = (bf16[224,1536]{1,0:T(8,128)(2,1)S(1)}, bf16[224,1536]{1,0:T(8,128)(2,1)S(1)}, u32[]{:S(2)}, u32[]{:S(2)}) collective-permute-start(bf16[224,1536]{1,0:T(8,128)(2,1)S(1)} %shard_map.62), channel_id=1, source_target_pairs={{0,8},{8,0},{16,24},{24,16},{1,9},{9,1},{17,25},{25,17},{2,10},{10... | collective-permute-start | bytes 2064392 | tf_op jit(solution)/shard_map/ppermute | solution.py:358
  53.8 1.4 %shard_map.67.left = bf16[384,768]{1,0:T(8,128)(2,1)S(1)} custom-call(s32[6]{0:T(128)S(1)} %copy-done.1, bf16[768,768]{1,0:T(8,128)(2,1)S(1)} %copy-done, bf16[768,768]{1,0:T(8,128)(2,1)S(1)} %collective-permute-done.2.refs_0_, f32[384,768]{1,0:T(8,128)S(1)} %get-tuple-element.49.refs_1_, ...), custom_call_target="tpu_custom_call", output_to_operand_aliasing={{}: (6, {})} | custom-call | tf_op jit(solution)/shard_map/pallas_call | solution.py:170
  55.2 0.7 shard_map.69
  55.9 0.1 collective-permute-start.11
  56.0 0.7 shard_map.68
  56.7 0.7 collective-permute-start.10
  57.3 0.6 shard_map.63
  57.9 2.1 %collective-permute-start.7 = (bf16[160,1536]{1,0:T(8,128)(2,1)S(1)}, bf16[160,1536]{1,0:T(8,128)(2,1)S(1)}, u32[]{:S(2)}, u32[]{:S(2)}) collective-permute-start(bf16[160,1536]{1,0:T(8,128)(2,1)S(1)} %shard_map.63), channel_id=1, source_target_pairs={{0,16},{8,24},{16,0},{24,8},{1,17},{9,25},{17,1},{25,9},{2,18},{10... | collective-permute-start | bytes 1474568 | tf_op jit(solution)/shard_map/ppermute | solution.py:358
  60.0 10.1 %collective-permute-done.6.rest_0_ = bf16[224,1536]{1,0:T(8,128)(2,1)S(1)} collective-permute-done((bf16[224,1536]{1,0:T(8,128)(2,1)S(1)}, bf16[224,1536]{1,0:T(8,128)(2,1)S(1)}, u32[]{:S(2)}, u32[]{:S(2)}) %collective-permute-start.6) | collective-permute-done | bytes 688160 | tf_op jit(solution)/shard_map/ppermute | solution.py:358
  70.1 0.4 shard_map.65
  70.5 0.5 collective-permute-start.8
  71.0 1.1 %collective-permute-done.11.rest_1_.rest_0_ = bf16[192,1536]{1,0:T(8,128)(2,1)S(1)} collective-permute-done((bf16[192,1536]{1,0:T(8,128)(2,1)S(1)}, bf16[192,1536]{1,0:T(8,128)(2,1)S(1)}, u32[]{:S(2)}, u32[]{:S(2)}) %collective-permute-start.11) | collective-permute-done | bytes 589856 | tf_op jit(solution)/shard_map/ppermute | solution.py:358
  72.2 0.4 shard_map.72
  72.6 0.7 collective-permute-start.13
  73.3 9.5 %collective-permute-done.10.rest_0_ = bf16[192,1536]{1,0:T(8,128)(2,1)S(1)} collective-permute-done((bf16[192,1536]{1,0:T(8,128)(2,1)S(1)}, bf16[192,1536]{1,0:T(8,128)(2,1)S(1)}, u32[]{:S(2)}, u32[]{:S(2)}) %collective-permute-start.10) | collective-permute-done | bytes 589856 | tf_op jit(solution)/shard_map/ppermute | solution.py:358
  82.7 0.4 shard_map.71
  83.1 0.5 collective-permute-start.12
  83.7 0.4 shard_map.66
  84.0 1.7 %collective-permute-start.9 = (bf16[160,768]{1,0:T(8,128)(2,1)S(1)}, bf16[160,768]{1,0:T(8,128)(2,1)S(1)}, u32[]{:S(2)}, u32[]{:S(2)}) collective-permute-start(bf16[160,768]{1,0:T(8,128)(2,1)S(1)} %shard_map.66), channel_id=1, source_target_pairs={{0,8},{8,0},{16,24},{24,16},{1,9},{9,1},{17,25},{25,17},{2,10},{10... | collective-permute-start | bytes 737288 | tf_op jit(solution)/shard_map/ppermute | solution.py:358
  85.7 0.7 shard_map.70.terms
  86.4 0.7 shard_map.64.terms
  87.1 2.0 %collective-permute-done.13.last = bf16[192,768]{1,0:T(8,128)(2,1)S(1)} collective-permute-done((bf16[192,768]{1,0:T(8,128)(2,1)S(1)}, bf16[192,768]{1,0:T(8,128)(2,1)S(1)}, u32[]{:S(2)}, u32[]{:S(2)}) %collective-permute-start.13) | collective-permute-done | bytes 294944 | tf_op jit(solution)/shard_map/ppermute | solution.py:358
  89.1 0.8 shard_map.73.rest_0_
  89.8 5.7 %collective-permute-done.12.last = bf16[192,768]{1,0:T(8,128)(2,1)S(1)} collective-permute-done((bf16[192,768]{1,0:T(8,128)(2,1)S(1)}, bf16[192,768]{1,0:T(8,128)(2,1)S(1)}, u32[]{:S(2)}, u32[]{:S(2)}) %collective-permute-start.12) | collective-permute-done | bytes 294944 | tf_op jit(solution)/shard_map/ppermute | solution.py:358
  95.6 0.8 shard_map.74.rest_0_
  96.3 0.7 shard_map.75.rest_0_
  97.1 0.8 shard_map.76
  (11 shorter events, 0.0 us)
Async XLA Ops:
  1.3 23.4 %copy-start = (bf16[768,768]{1,0:T(8,128)(2,1)S(1)}, bf16[768,768]{1,0:T(8,128)(2,1)}, u32[]{:S(2)}) copy-start(bf16[768,768]{1,0:T(8,128)(2,1)} %query.11) | copy-start | bytes 3538948
  1.3 23.4 %copy-start.1 = (s32[6]{0:T(128)S(1)}, s32[6]{0:T(128)}, u32[]{:S(2)}) copy-start(s32[6]{0:T(128)} %span_ref.11) | copy-start | bytes 76
  1.3 17.7 %collective-permute-start.3 = (bf16[768,768]{1,0:T(8,128)(2,1)S(1)}, bf16[768,768]{1,0:T(8,128)(2,1)S(1)}, u32[]{:S(2)}, u32[]{:S(2)}) collective-permute-start(bf16[768,768]{1,0:T(8,128)(2,1)S(1)} %shard_map.56.refs_0_), channel_id=1, source_target_pairs={{1,2},{3,4},{5,6},{2,1},{4,3},{6,5},{9,10},{11,12},{13,14},{10,9},... | collective-permute-start | bytes 3538952 | tf_op jit(solution)/shard_map/ppermute | solution.py:342
  4.6 16.8 %collective-permute-start = (bf16[768,768]{1,0:T(8,128)(2,1)S(1)}, bf16[768,768]{1,0:T(8,128)(2,1)S(1)}, u32[]{:S(2)}, u32[]{:S(2)}) collective-permute-start(bf16[768,768]{1,0:T(8,128)(2,1)S(1)} %shard_map.55.refs_1_), channel_id=1, source_target_pairs={{0,1},{1,0},{2,3},{3,2},{4,5},{5,4},{6,7},{7,6},{8,9},{9,8},{10,11... | collective-permute-start | bytes 3538952 | tf_op jit(solution)/shard_map/ppermute | solution.py:338
  6.4 18.3 %collective-permute-start.5 = (bf16[768,768]{1,0:T(8,128)(2,1)S(1)}, bf16[768,768]{1,0:T(8,128)(2,1)S(1)}, u32[]{:S(2)}, u32[]{:S(2)}) collective-permute-start(bf16[768,768]{1,0:T(8,128)(2,1)S(1)} %shard_map.56.refs_0_), channel_id=1, source_target_pairs={{0,1},{1,0},{2,3},{3,2},{4,5},{5,4},{6,7},{7,6},{8,9},{9,8},{10,11... | collective-permute-start | bytes 3538952 | tf_op jit(solution)/shard_map/ppermute | solution.py:338
  18.9 22.8 %collective-permute-start.4 = (bf16[768,768]{1,0:T(8,128)(2,1)S(1)}, bf16[768,768]{1,0:T(8,128)(2,1)S(1)}, u32[]{:S(2)}, u32[]{:S(2)}) collective-permute-start(bf16[768,768]{1,0:T(8,128)(2,1)S(1)} %collective-permute-done.3.refs_0_), channel_id=1, source_target_pairs={{0,1},{1,0},{2,3},{3,2},{4,5},{5,4},{6,7},{7,6},{8,9},{9,8},{10,11... | collective-permute-start | bytes 3538952 | tf_op jit(solution)/shard_map/ppermute | solution.py:338
  19.1 24.5 %collective-permute-start.2 = (bf16[768,768]{1,0:T(8,128)(2,1)S(1)}, bf16[768,768]{1,0:T(8,128)(2,1)S(1)}, u32[]{:S(2)}, u32[]{:S(2)}) collective-permute-start(bf16[768,768]{1,0:T(8,128)(2,1)S(1)} %shard_map.55.refs_1_), channel_id=1, source_target_pairs={{1,2},{3,4},{5,6},{2,1},{4,3},{6,5},{9,10},{11,12},{13,14},{10,9},... | collective-permute-start | bytes 3538952 | tf_op jit(solution)/shard_map/ppermute | solution.py:342
  21.4 27.8 %collective-permute-start.1 = (bf16[768,768]{1,0:T(8,128)(2,1)S(1)}, bf16[768,768]{1,0:T(8,128)(2,1)S(1)}, u32[]{:S(2)}, u32[]{:S(2)}) collective-permute-start(bf16[768,768]{1,0:T(8,128)(2,1)S(1)} %collective-permute-done.refs_2_), channel_id=1, source_target_pairs={{1,2},{3,4},{5,6},{2,1},{4,3},{6,5},{9,10},{11,12},{13,14},{10,9},... | collective-permute-start | bytes 3538952 | tf_op jit(solution)/shard_map/ppermute | solution.py:342
  41.7 9.1 %slice-start = ((s8[4718592]{0:T(1024)(128)(4,1)}), s8[524288]{0:T(1024)(128)(4,1)S(1)}, s32[]{:S(2)}) async-start(s8[4718592]{0:T(1024)(128)(4,1)} %bitcast), calls=%async_computation | async-start | bytes 1048576
  43.5 7.3 %slice-start.1 = ((s8[4718592]{0:T(1024)(128)(4,1)}), s8[4194304]{0:T(1024)(128)(4,1)S(1)}, s32[]{:S(2)}) async-start(s8[4718592]{0:T(1024)(128)(4,1)} %bitcast), calls=%async_computation.1 | async-start | bytes 8388608
  51.7 18.4 %collective-permute-start.6 = (bf16[224,1536]{1,0:T(8,128)(2,1)S(1)}, bf16[224,1536]{1,0:T(8,128)(2,1)S(1)}, u32[]{:S(2)}, u32[]{:S(2)}) collective-permute-start(bf16[224,1536]{1,0:T(8,128)(2,1)S(1)} %shard_map.62), channel_id=1, source_target_pairs={{0,8},{8,0},{16,24},{24,16},{1,9},{9,1},{17,25},{25,17},{2,10},{10... | collective-permute-start | bytes 2064392 | tf_op jit(solution)/shard_map/ppermute | solution.py:358
  55.9 16.3 %collective-permute-start.11 = (bf16[192,1536]{1,0:T(8,128)(2,1)S(1)}, bf16[192,1536]{1,0:T(8,128)(2,1)S(1)}, u32[]{:S(2)}, u32[]{:S(2)}) collective-permute-start(bf16[192,1536]{1,0:T(8,128)(2,1)S(1)} %shard_map.69), channel_id=1, source_target_pairs={{0,16},{8,24},{16,0},{24,8},{1,17},{9,25},{17,1},{25,9},{2,18},{10... | collective-permute-start | bytes 1769480 | tf_op jit(solution)/shard_map/ppermute | solution.py:358
  56.7 26.1 %collective-permute-start.10 = (bf16[192,1536]{1,0:T(8,128)(2,1)S(1)}, bf16[192,1536]{1,0:T(8,128)(2,1)S(1)}, u32[]{:S(2)}, u32[]{:S(2)}) collective-permute-start(bf16[192,1536]{1,0:T(8,128)(2,1)S(1)} %shard_map.68), channel_id=1, source_target_pairs={{0,8},{8,0},{16,24},{24,16},{1,9},{9,1},{17,25},{25,17},{2,10},{10... | collective-permute-start | bytes 1769480 | tf_op jit(solution)/shard_map/ppermute | solution.py:358
  57.9 25.8 %collective-permute-start.7 = (bf16[160,1536]{1,0:T(8,128)(2,1)S(1)}, bf16[160,1536]{1,0:T(8,128)(2,1)S(1)}, u32[]{:S(2)}, u32[]{:S(2)}) collective-permute-start(bf16[160,1536]{1,0:T(8,128)(2,1)S(1)} %shard_map.63), channel_id=1, source_target_pairs={{0,16},{8,24},{16,0},{24,8},{1,17},{9,25},{17,1},{25,9},{2,18},{10... | collective-permute-start | bytes 1474568 | tf_op jit(solution)/shard_map/ppermute | solution.py:358
  70.5 26.6 %collective-permute-start.8 = (bf16[224,768]{1,0:T(8,128)(2,1)S(1)}, bf16[224,768]{1,0:T(8,128)(2,1)S(1)}, u32[]{:S(2)}, u32[]{:S(2)}) collective-permute-start(bf16[224,768]{1,0:T(8,128)(2,1)S(1)} %shard_map.65), channel_id=1, source_target_pairs={{0,16},{8,24},{16,0},{24,8},{1,17},{9,25},{17,1},{25,9},{2,18},{10... | collective-permute-start | bytes 1032200 | tf_op jit(solution)/shard_map/ppermute | solution.py:358
  72.6 16.4 %collective-permute-start.13 = (bf16[192,768]{1,0:T(8,128)(2,1)S(1)}, bf16[192,768]{1,0:T(8,128)(2,1)S(1)}, u32[]{:S(2)}, u32[]{:S(2)}) collective-permute-start(bf16[192,768]{1,0:T(8,128)(2,1)S(1)} %shard_map.72), channel_id=1, source_target_pairs={{0,8},{8,0},{16,24},{24,16},{1,9},{9,1},{17,25},{25,17},{2,10},{10... | collective-permute-start | bytes 884744 | tf_op jit(solution)/shard_map/ppermute | solution.py:358
  83.1 12.4 %collective-permute-start.12 = (bf16[192,768]{1,0:T(8,128)(2,1)S(1)}, bf16[192,768]{1,0:T(8,128)(2,1)S(1)}, u32[]{:S(2)}, u32[]{:S(2)}) collective-permute-start(bf16[192,768]{1,0:T(8,128)(2,1)S(1)} %shard_map.71), channel_id=1, source_target_pairs={{0,16},{8,24},{16,0},{24,8},{1,17},{9,25},{17,1},{25,9},{2,18},{10... | collective-permute-start | bytes 884744 | tf_op jit(solution)/shard_map/ppermute | solution.py:358
  84.0 12.3 %collective-permute-start.9 = (bf16[160,768]{1,0:T(8,128)(2,1)S(1)}, bf16[160,768]{1,0:T(8,128)(2,1)S(1)}, u32[]{:S(2)}, u32[]{:S(2)}) collective-permute-start(bf16[160,768]{1,0:T(8,128)(2,1)S(1)} %shard_map.66), channel_id=1, source_target_pairs={{0,8},{8,0},{16,24},{24,16},{1,9},{9,1},{17,25},{25,17},{2,10},{10... | collective-permute-start | bytes 737288 | tf_op jit(solution)/shard_map/ppermute | solution.py:358

commit v10 on v7

--- a/solution.py
+++ b/solution.py
@@ -13,7 +13,6 @@
 BF16 = jnp.bfloat16
 VMEM_LIMIT = 16 << 20
 CHUNK = 384
-LEAN = 16
 
 
 def params():
@@ -126,7 +125,7 @@
 
                 lax.fori_loop(0, count // 2, pair, 0)
                 pl.when(count % 2 == 1)(
-                    lambda items=items, close=close, count=count: take((chosen[count - 1],), items, close)
+                    lambda items=items, close=close, count=count: take((chosen[jnp.maximum(count - 1, 0)],), items, close)
                 )
             else:
 
@@ -219,7 +218,15 @@
 
 
 def row_edges(parts):
-    return [0] + [part * FRAME_TOK // parts + LEAN for part in range(1, parts)] + [FRAME_TOK]
+    return [part * FRAME_TOK // parts for part in range(parts + 1)]
+
+
+def mesh_bit(stage, part, core, bits):
+    return (stage + part + core) % bits
+
+
+def owner_of(slot, part, core, bits):
+    return sum(1 << mesh_bit(stage, part, core, bits) for stage in range(bits) if slot >> stage & 1)
 
 
 def project(attended, part, parts, out_weight, slots, received):
@@ -231,8 +238,12 @@
     def kernel(left, right, *rest):
         out = rest[-1]
         group = lax.axis_index("head")
+        core = lax.axis_index("frame") % 2
         for index, slot in enumerate(slots):
-            column = pl.ds(pl.multiple_of((group ^ slot) * width, width), width)
+            toward = jnp.where(
+                core == 0, owner_of(slot, part, 0, parts), owner_of(slot, part, 1, parts)
+            )
+            column = pl.ds(pl.multiple_of((group ^ toward) * width, width), width)
             sums = jnp.dot(
                 left[start:stop, :], right[:, column], preferred_element_type=F32
             )
@@ -277,7 +288,7 @@
     )(*operands)
 
 
-def finish(own, received, is_edge, frames_here, into):
+def finish(role, own, received, frames_here, into):
     parts = len(received)
     edges = row_edges(parts)
     width = own.shape[1]
@@ -285,7 +296,7 @@
     def kernel(terms, *rest):
         out, buffer, sems = rest[-3:]
         parity = lax.axis_index("frame") % 2
-        frame = parity if is_edge else 1 - parity
+        frame = parity if role == "E" else 1 - parity
         copies = []
         for part in range(parts):
             start, rows = edges[part], edges[part + 1] - edges[part]
@@ -346,8 +357,13 @@
     state, attended = attend_beyond(head_span, query_tok, state, beyond)
     attended["I"] = attend_inner(head_span, query_tok, state["I"], second, attended["I"])
 
-    def exchange(value, bit):
-        return lax.ppermute(value, "head", [(i, i ^ (1 << bit)) for i in range(groups)])
+    def exchange(value, stage, part):
+        pairs = []
+        for head in range(groups):
+            for place in range(frames):
+                other = head ^ (1 << mesh_bit(stage, part, place % 2, bits))
+                pairs.append((head * frames + place, other * frames + place))
+        return lax.ppermute(value, ("head", "frame"), pairs)
 
     held = {role: [list(range(groups)) for _ in range(bits)] for role in "IE"}
     received = {role: [[] for _ in range(bits)] for role in "IE"}
@@ -357,11 +373,10 @@
 
     def halve(role, stage):
         for part in range(bits):
-            bit = (part + stage) % bits
-            sent = [s for s in held[role][part] if s >> bit & 1]
-            kept = [s for s in held[role][part] if not s >> bit & 1]
+            sent = [s for s in held[role][part] if s >> stage & 1]
+            kept = [s for s in held[role][part] if not s >> stage & 1]
             terms = project(attended[role], part, bits, out_weight, sent, gathered(role, part, sent))
-            received[role][part].append((exchange(terms, bit), kept))
+            received[role][part].append((exchange(terms, stage, part), kept))
             held[role][part] = kept
 
     halve("I", 0)
@@ -375,7 +390,7 @@
     for role in "IE":
         terms = [gathered(role, part, [0]) for part in range(bits)]
         own = sum_own(attended[role], bits, out_weight, [t[:-1] for t in terms])
-        result = finish(own, [t[-1][0] for t in terms], role == "E", local_frames, result)
+        result = finish(role, own, [t[-1][0] for t in terms], local_frames, result)
     return result
 
 

time: 95.5 us -> 88.8 us (0.930)
  waiting for transfers between devices: 45.1 us -> 36.7 us
  starting transfers between devices: 14.6 us -> 16.2 us
    ppermute x8, waiting for transfers between devices: 32.5 us -> 24.4 us  [exchange(): return lax.ppermute(value, ('head', 'frame'), pairs)]
    ppermute x8, starting transfers between devices: 5.05 us -> 6.68 us  [exchange(): return lax.ppermute(value, ('head', 'frame'), pairs)]
  transfers between devices with their start and end apart: 14 -> 14, of which waited for: 9 -> 6; matrix products, arithmetic and copies ran while one was open for 0% -> 0% of each run, Pallas kernels for 33% -> 35%
where the time goes in v10:
time: 88.8 us; the launch traced here: 88.6 us
  waiting for transfers between devices  36.7 us (41%)
  Pallas kernels  32.3 us (36%)
  starting transfers between devices  16.2 us (18%)
  local copies, waits for them, and re-layouts  2.65 us (3%)
    pallas_call x6, Pallas kernels, attend_step(): pl.pallas_call(kernel, out_shape=tuple(shapes), in_specs=[SMEM] + [VMEM]...  24.8 us
    ppermute x8, waiting for transfers between devices, exchange(): return lax.ppermute(value, ('head', 'frame'), pairs)  24.4 us
    ppermute x3, waiting for transfers between devices, across(): return lax.ppermute(value, 'frame', pairs + [(b, a) for a, b in pairs])  12.3 us
    ppermute x3, starting transfers between devices, across(): return lax.ppermute(value, 'frame', pairs + [(b, a) for a, b in pairs])  7.6 us
    ppermute x8, starting transfers between devices, exchange(): return lax.ppermute(value, ('head', 'frame'), pairs)  6.68 us
    pallas_call x8, Pallas kernels, project(): pl.pallas_call(kernel, out_shape=jax.ShapeDtypeStruct((rows, len(slots) *...  4.38 us
    ppermute x3, starting transfers between devices, swap(): return lax.ppermute(value, 'frame', [(i, i ^ 1) for i in range(frames)])  1.94 us
  transfers between devices with their start and end apart: 14, of which 6 were waited for; matrix products, arithmetic and copies ran while one was open for 0% of the time, Pallas kernels for 35%

profile of v10, /device:TPU:20, one launch (start us, length us, event | category | flops | bytes accessed | tf_op | source)
XLA Modules:
  0.0 88.6 jit_solution(13570366617839924874)
XLA Ops:
  0.0 1.3 %constant_dynamic-slice_fusion.2 = (bf16[384,768]{1,0:T(8,128)(2,1)S(1)}, bf16[384,768]{1,0:T(8,128)(2,1)S(1)}) fusion(bf16[768,768]{1,0:T(8,128)(2,1)} %param.7, s32[]{:T(128)S(6)} %select_n.16, bf16[768,768]{1,0:T(8,128)(2,1)} %param.6), kind=kLoop, calls=%fused_computation.4 | loop fusion | bytes 2359300 | tf_op jit(solution)/shard_map/dynamic_slice | solution.py:31
  1.3 0.0 copy-start.2
  1.3 0.1 pad_maximum_fusion.refs_0_
  1.4 2.1 %collective-permute-start.3 = (bf16[768,768]{1,0:T(8,128)(2,1)S(1)}, bf16[768,768]{1,0:T(8,128)(2,1)S(1)}, u32[]{:S(2)}, u32[]{:S(2)}) collective-permute-start(bf16[768,768]{1,0:T(8,128)(2,1)S(1)} %pad_maximum_fusion.refs_0_), channel_id=1, source_target_pairs={{1,2},{3,4},{5,6},{2,1},{4,3},{6,5},{9,10},{11,12},{13,14},{10,9},... | collective-permute-start | bytes 3538952 | tf_op jit(solution)/shard_map/ppermute | solution.py:346
  3.5 0.0 copy-start.3
  3.6 1.2 %copy-done.3 = bf16[768,768]{1,0:T(8,128)(2,1)S(1)} copy-done((bf16[768,768]{1,0:T(8,128)(2,1)S(1)}, bf16[768,768]{1,0:T(8,128)(2,1)}, u32[]{:S(2)}) %copy-start.3) | copy-done | bytes 1179672
  4.8 0.0 copy-start
  4.8 0.0 copy-start.1
  4.8 0.1 pad_maximum_fusion.1.refs_1_
  4.9 1.7 %collective-permute-start = (bf16[768,768]{1,0:T(8,128)(2,1)S(1)}, bf16[768,768]{1,0:T(8,128)(2,1)S(1)}, u32[]{:S(2)}, u32[]{:S(2)}) collective-permute-start(bf16[768,768]{1,0:T(8,128)(2,1)S(1)} %pad_maximum_fusion.1.refs_1_), channel_id=1, source_target_pairs={{0,1},{1,0},{2,3},{3,2},{4,5},{5,4},{6,7},{7,6},{8,9},{9,8},{10,11... | collective-permute-start | bytes 3538952 | tf_op jit(solution)/shard_map/ppermute | solution.py:342
  6.7 0.1 collective-permute-start.5
  6.8 12.3 %collective-permute-done.3.refs_0_ = bf16[768,768]{1,0:T(8,128)(2,1)S(1)} collective-permute-done((bf16[768,768]{1,0:T(8,128)(2,1)S(1)}, bf16[768,768]{1,0:T(8,128)(2,1)S(1)}, u32[]{:S(2)}, u32[]{:S(2)}) %collective-permute-start.3) | collective-permute-done | bytes 1179680 | tf_op jit(solution)/shard_map/ppermute | solution.py:346
  19.1 0.1 collective-permute-start.4
  19.2 2.3 %collective-permute-start.2 = (bf16[768,768]{1,0:T(8,128)(2,1)S(1)}, bf16[768,768]{1,0:T(8,128)(2,1)S(1)}, u32[]{:S(2)}, u32[]{:S(2)}) collective-permute-start(bf16[768,768]{1,0:T(8,128)(2,1)S(1)} %pad_maximum_fusion.1.refs_1_), channel_id=1, source_target_pairs={{1,2},{3,4},{5,6},{2,1},{4,3},{6,5},{9,10},{11,12},{13,14},{10,9},... | collective-permute-start | bytes 3538952 | tf_op jit(solution)/shard_map/ppermute | solution.py:346
  21.6 3.2 %collective-permute-start.1 = (bf16[768,768]{1,0:T(8,128)(2,1)S(1)}, bf16[768,768]{1,0:T(8,128)(2,1)S(1)}, u32[]{:S(2)}, u32[]{:S(2)}) collective-permute-start(bf16[768,768]{1,0:T(8,128)(2,1)S(1)} %collective-permute-done.refs_2_), channel_id=1, source_target_pairs={{1,2},{3,4},{5,6},{2,1},{4,3},{6,5},{9,10},{11,12},{13,14},{10,9},... | collective-permute-start | bytes 3538952 | tf_op jit(solution)/shard_map/ppermute | solution.py:346
  24.8 12.2 %shard_map.55 = (f32[384,768]{1,0:T(8,128)S(1)}, f32[384,768]{1,0:T(8,128)S(1)}, f32[384,768]{1,0:T(8,128)S(1)}, f32[384,768]{1,0:T(8,128)S(1)}, f32[384,768]{1,0:T(8,128)S(1)}, /*index=5*/f32[384,768]{1,0:T(8,128)S(1)}) custom-call(s32[6]{0:T(128)S(1)} %copy-done.1, bf16[768,768]{1,0:T(8,128)(2,1)S(1)} %copy-done, ...), custom_call_target="tpu_custom_call" | custom-call | tf_op jit(solution)/shard_map/pallas_call | solution.py:154
  37.0 0.0 slice-start
  37.0 4.9 %shard_map.56 = (f32[384,768]{1,0:T(8,128)S(1)}, f32[384,768]{1,0:T(8,128)S(1)}, f32[384,768]{1,0:T(8,128)S(1)}, f32[384,768]{1,0:T(8,128)S(1)}, f32[384,768]{1,0:T(8,128)S(1)}, /*index=5*/f32[384,768]{1,0:T(8,128)S(1)}) custom-call(s32[6]{0:T(128)S(1)} %copy-done.1, ...), custom_call_target="tpu_custom_call", output_to_operand_aliasing={{0}: (3, {}), {1}: (4, {}), {2}: (5, {}), {3}: (6, {}), {4}... | custom-call | tf_op jit(solution)/shard_map/pallas_call | solution.py:154
  41.9 0.0 slice-start.1
  41.9 1.8 %shard_map.57 = (f32[384,768]{1,0:T(8,128)S(1)}, f32[384,768]{1,0:T(8,128)S(1)}, f32[384,768]{1,0:T(8,128)S(1)}, f32[384,768]{1,0:T(8,128)S(1)}, f32[384,768]{1,...) custom-call(s32[6]{0:T(128)S(1)} %copy-done.1, ...), custom_call_target="tpu_custom_call", output_to_operand_aliasing={{0}: (3, {}), {1}: (4, {}), {2}: (5, {}), {3}: (6, {}), {4}... | custom-call | tf_op jit(solution)/shard_map/pallas_call | solution.py:154
  43.7 1.4 %shard_map.65.left = bf16[384,768]{1,0:T(8,128)(2,1)S(1)} custom-call(s32[6]{0:T(128)S(1)} %copy-done.1, bf16[768,768]{1,0:T(8,128)(2,1)S(1)} %copy-done, bf16[768,768]{1,0:T(8,128)(2,1)S(1)} %collective-permute-done.2.refs_0_, f32[384,768]{1,0:T(8,128)S(1)} %get-tuple-element.55.refs_1_, ...), custom_call_target="tpu_custom_call", output_to_operand_aliasing={{}: (6, {})} | custom-call | tf_op jit(solution)/shard_map/pallas_call | solution.py:154
  45.1 0.7 shard_map.67
  45.8 0.7 shard_map.66
  46.5 0.1 collective-permute-start.10
  46.6 0.1 collective-permute-start.11
  46.7 3.1 %shard_map.58 = (f32[384,768]{1,0:T(8,128)S(1)}, f32[384,768]{1,0:T(8,128)S(1)}, f32[384,768]{1,0:T(8,128)S(1)}, bf16[384,768]{1,0:T(8,128)(2,1)S(1)}) custom-call(s32[6]{0:T(128)S(1)} %copy-done.1, bf16[768,768]{1,0:T(8,128)(2,1)S(1)} %copy-done, ...), custom_call_target="tpu_custom_call", output_to_operand_aliasing={{0}: (3, {}), {1}: (4, {}), {2}: (5, {}), {3}: (6, {})} | custom-call | tf_op jit(solution)/shard_map/pallas_call | solution.py:154
  49.8 1.4 %shard_map.59.left = bf16[384,768]{1,0:T(8,128)(2,1)S(1)} custom-call(s32[6]{0:T(128)S(1)} %copy-done.1, bf16[768,768]{1,0:T(8,128)(2,1)S(1)} %copy-done, bf16[768,768]{1,0:T(8,128)(2,1)S(1)} %collective-permute-done.1.refs_0_, f32[384,768]{1,0:T(8,128)S(1)} %get-tuple-element.51.refs_1_, ...), custom_call_target="tpu_custom_call", output_to_operand_aliasing={{}: (6, {})} | custom-call | tf_op jit(solution)/shard_map/pallas_call | solution.py:154
  51.3 0.7 shard_map.60
  52.0 2.4 %collective-permute-start.6 = (bf16[192,1536]{1,0:T(8,128)(2,1)S(1)}, bf16[192,1536]{1,0:T(8,128)(2,1)S(1)}, u32[]{:S(2)}, u32[]{:S(2)}) collective-permute-start(bf16[192,1536]{1,0:T(8,128)(2,1)S(1)} %shard_map.60), channel_id=1, source_target_pairs={{0,8},{1,17},{2,10},{3,19},{4,12},{5,21},{6,14},{7,23},{8,0},{9,25... | collective-permute-start | bytes 1769480 | tf_op jit(solution)/shard_map/ppermute | solution.py:366
  54.4 0.6 shard_map.61
  55.0 0.9 collective-permute-start.7
  55.9 6.9 %collective-permute-done.10.rest_0_ = bf16[192,1536]{1,0:T(8,128)(2,1)S(1)} collective-permute-done((bf16[192,1536]{1,0:T(8,128)(2,1)S(1)}, bf16[192,1536]{1,0:T(8,128)(2,1)S(1)}, u32[]{:S(2)}, u32[]{:S(2)}) %collective-permute-start.10) | collective-permute-done | bytes 589856 | tf_op jit(solution)/shard_map/ppermute | solution.py:366
  62.8 0.4 shard_map.69
  63.2 0.1 collective-permute-start.12
  63.3 0.4 shard_map.70
  63.7 1.6 %collective-permute-start.13 = (bf16[192,768]{1,0:T(8,128)(2,1)S(1)}, bf16[192,768]{1,0:T(8,128)(2,1)S(1)}, u32[]{:S(2)}, u32[]{:S(2)}) collective-permute-start(bf16[192,768]{1,0:T(8,128)(2,1)S(1)} %shard_map.70), channel_id=1, source_target_pairs={{0,8},{1,17},{2,10},{3,19},{4,12},{5,21},{6,14},{7,23},{8,0},{9,25... | collective-permute-start | bytes 884744 | tf_op jit(solution)/shard_map/ppermute | solution.py:366
  65.3 10.1 %collective-permute-done.6.rest_0_ = bf16[192,1536]{1,0:T(8,128)(2,1)S(1)} collective-permute-done((bf16[192,1536]{1,0:T(8,128)(2,1)S(1)}, bf16[192,1536]{1,0:T(8,128)(2,1)S(1)}, u32[]{:S(2)}, u32[]{:S(2)}) %collective-permute-start.6) | collective-permute-done | bytes 589856 | tf_op jit(solution)/shard_map/ppermute | solution.py:366
  75.4 0.4 shard_map.63
  75.8 0.1 collective-permute-start.8
  75.9 0.4 shard_map.64
  76.4 1.5 %collective-permute-start.9 = (bf16[192,768]{1,0:T(8,128)(2,1)S(1)}, bf16[192,768]{1,0:T(8,128)(2,1)S(1)}, u32[]{:S(2)}, u32[]{:S(2)}) collective-permute-start(bf16[192,768]{1,0:T(8,128)(2,1)S(1)} %shard_map.64), channel_id=1, source_target_pairs={{0,8},{1,17},{2,10},{3,19},{4,12},{5,21},{6,14},{7,23},{8,0},{9,25... | collective-permute-start | bytes 884744 | tf_op jit(solution)/shard_map/ppermute | solution.py:366
  77.9 0.7 shard_map.68.terms
  78.6 0.7 shard_map.62.terms
  79.3 2.6 %collective-permute-done.12.rest_0_ = bf16[192,768]{1,0:T(8,128)(2,1)S(1)} collective-permute-done((bf16[192,768]{1,0:T(8,128)(2,1)S(1)}, bf16[192,768]{1,0:T(8,128)(2,1)S(1)}, u32[]{:S(2)}, u32[]{:S(2)}) %collective-permute-start.12) | collective-permute-done | bytes 294944 | tf_op jit(solution)/shard_map/ppermute | solution.py:366
  81.8 0.9 shard_map.71.rest_2_
  82.7 4.8 %collective-permute-done.8.rest_0_ = bf16[192,768]{1,0:T(8,128)(2,1)S(1)} collective-permute-done((bf16[192,768]{1,0:T(8,128)(2,1)S(1)}, bf16[192,768]{1,0:T(8,128)(2,1)S(1)}, u32[]{:S(2)}, u32[]{:S(2)}) %collective-permute-start.8) | collective-permute-done | bytes 294944 | tf_op jit(solution)/shard_map/ppermute | solution.py:366
  87.5 0.1 collective-permute-done.9.rest_1_
  87.6 0.9 shard_map.72
  (16 shorter events, 0.1 us)
Async XLA Ops:
  1.3 2.2 %copy-start.2 = (bf16[768,768]{1,0:T(8,128)(2,1)S(1)}, bf16[768,768]{1,0:T(8,128)(2,1)}, u32[]{:S(2)}) copy-start(bf16[768,768]{1,0:T(8,128)(2,1)} %param.6) | copy-start | bytes 3538948
  1.4 17.7 %collective-permute-start.3 = (bf16[768,768]{1,0:T(8,128)(2,1)S(1)}, bf16[768,768]{1,0:T(8,128)(2,1)S(1)}, u32[]{:S(2)}, u32[]{:S(2)}) collective-permute-start(bf16[768,768]{1,0:T(8,128)(2,1)S(1)} %pad_maximum_fusion.refs_0_), channel_id=1, source_target_pairs={{1,2},{3,4},{5,6},{2,1},{4,3},{6,5},{9,10},{11,12},{13,14},{10,9},... | collective-permute-start | bytes 3538952 | tf_op jit(solution)/shard_map/ppermute | solution.py:346
  3.5 1.3 %copy-start.3 = (bf16[768,768]{1,0:T(8,128)(2,1)S(1)}, bf16[768,768]{1,0:T(8,128)(2,1)}, u32[]{:S(2)}) copy-start(bf16[768,768]{1,0:T(8,128)(2,1)} %param.7) | copy-start | bytes 3538948
  4.8 20.0 %copy-start = (bf16[768,768]{1,0:T(8,128)(2,1)S(1)}, bf16[768,768]{1,0:T(8,128)(2,1)}, u32[]{:S(2)}) copy-start(bf16[768,768]{1,0:T(8,128)(2,1)} %query.11) | copy-start | bytes 3538948
  4.8 20.0 %copy-start.1 = (s32[6]{0:T(128)S(1)}, s32[6]{0:T(128)}, u32[]{:S(2)}) copy-start(s32[6]{0:T(128)} %span_ref.11) | copy-start | bytes 76
  4.9 16.6 %collective-permute-start = (bf16[768,768]{1,0:T(8,128)(2,1)S(1)}, bf16[768,768]{1,0:T(8,128)(2,1)S(1)}, u32[]{:S(2)}, u32[]{:S(2)}) collective-permute-start(bf16[768,768]{1,0:T(8,128)(2,1)S(1)} %pad_maximum_fusion.1.refs_1_), channel_id=1, source_target_pairs={{0,1},{1,0},{2,3},{3,2},{4,5},{5,4},{6,7},{7,6},{8,9},{9,8},{10,11... | collective-permute-start | bytes 3538952 | tf_op jit(solution)/shard_map/ppermute | solution.py:342
  6.7 18.1 %collective-permute-start.5 = (bf16[768,768]{1,0:T(8,128)(2,1)S(1)}, bf16[768,768]{1,0:T(8,128)(2,1)S(1)}, u32[]{:S(2)}, u32[]{:S(2)}) collective-permute-start(bf16[768,768]{1,0:T(8,128)(2,1)S(1)} %pad_maximum_fusion.refs_0_), channel_id=1, source_target_pairs={{0,1},{1,0},{2,3},{3,2},{4,5},{5,4},{6,7},{7,6},{8,9},{9,8},{10,11... | collective-permute-start | bytes 3538952 | tf_op jit(solution)/shard_map/ppermute | solution.py:342
  19.1 22.8 %collective-permute-start.4 = (bf16[768,768]{1,0:T(8,128)(2,1)S(1)}, bf16[768,768]{1,0:T(8,128)(2,1)S(1)}, u32[]{:S(2)}, u32[]{:S(2)}) collective-permute-start(bf16[768,768]{1,0:T(8,128)(2,1)S(1)} %collective-permute-done.3.refs_0_), channel_id=1, source_target_pairs={{0,1},{1,0},{2,3},{3,2},{4,5},{5,4},{6,7},{7,6},{8,9},{9,8},{10,11... | collective-permute-start | bytes 3538952 | tf_op jit(solution)/shard_map/ppermute | solution.py:342
  19.2 24.5 %collective-permute-start.2 = (bf16[768,768]{1,0:T(8,128)(2,1)S(1)}, bf16[768,768]{1,0:T(8,128)(2,1)S(1)}, u32[]{:S(2)}, u32[]{:S(2)}) collective-permute-start(bf16[768,768]{1,0:T(8,128)(2,1)S(1)} %pad_maximum_fusion.1.refs_1_), channel_id=1, source_target_pairs={{1,2},{3,4},{5,6},{2,1},{4,3},{6,5},{9,10},{11,12},{13,14},{10,9},... | collective-permute-start | bytes 3538952 | tf_op jit(solution)/shard_map/ppermute | solution.py:346
  21.6 28.3 %collective-permute-start.1 = (bf16[768,768]{1,0:T(8,128)(2,1)S(1)}, bf16[768,768]{1,0:T(8,128)(2,1)S(1)}, u32[]{:S(2)}, u32[]{:S(2)}) collective-permute-start(bf16[768,768]{1,0:T(8,128)(2,1)S(1)} %collective-permute-done.refs_2_), channel_id=1, source_target_pairs={{1,2},{3,4},{5,6},{2,1},{4,3},{6,5},{9,10},{11,12},{13,14},{10,9},... | collective-permute-start | bytes 3538952 | tf_op jit(solution)/shard_map/ppermute | solution.py:346
  37.0 8.1 %slice-start = ((s8[4718592]{0:T(1024)(128)(4,1)}), s8[4194304]{0:T(1024)(128)(4,1)S(1)}, s32[]{:S(2)}) async-start(s8[4718592]{0:T(1024)(128)(4,1)} %bitcast), calls=%async_computation | async-start | bytes 8388608
  41.9 3.3 %slice-start.1 = ((s8[4718592]{0:T(1024)(128)(4,1)}), s8[524288]{0:T(1024)(128)(4,1)S(1)}, s32[]{:S(2)}) async-start(s8[4718592]{0:T(1024)(128)(4,1)} %bitcast), calls=%async_computation.1 | async-start | bytes 1048576
  46.5 16.3 %collective-permute-start.10 = (bf16[192,1536]{1,0:T(8,128)(2,1)S(1)}, bf16[192,1536]{1,0:T(8,128)(2,1)S(1)}, u32[]{:S(2)}, u32[]{:S(2)}) collective-permute-start(bf16[192,1536]{1,0:T(8,128)(2,1)S(1)} %shard_map.66), channel_id=1, source_target_pairs={{0,8},{1,17},{2,10},{3,19},{4,12},{5,21},{6,14},{7,23},{8,0},{9,25... | collective-permute-start | bytes 1769480 | tf_op jit(solution)/shard_map/ppermute | solution.py:366
  46.6 16.7 %collective-permute-start.11 = (bf16[192,1536]{1,0:T(8,128)(2,1)S(1)}, bf16[192,1536]{1,0:T(8,128)(2,1)S(1)}, u32[]{:S(2)}, u32[]{:S(2)}) collective-permute-start(bf16[192,1536]{1,0:T(8,128)(2,1)S(1)} %shard_map.67), channel_id=1, source_target_pairs={{0,16},{1,9},{2,18},{3,11},{4,20},{5,13},{6,22},{7,15},{8,24},{9,1... | collective-permute-start | bytes 1769480 | tf_op jit(solution)/shard_map/ppermute | solution.py:366
  52.0 23.4 %collective-permute-start.6 = (bf16[192,1536]{1,0:T(8,128)(2,1)S(1)}, bf16[192,1536]{1,0:T(8,128)(2,1)S(1)}, u32[]{:S(2)}, u32[]{:S(2)}) collective-permute-start(bf16[192,1536]{1,0:T(8,128)(2,1)S(1)} %shard_map.60), channel_id=1, source_target_pairs={{0,8},{1,17},{2,10},{3,19},{4,12},{5,21},{6,14},{7,23},{8,0},{9,25... | collective-permute-start | bytes 1769480 | tf_op jit(solution)/shard_map/ppermute | solution.py:366
  55.0 20.9 %collective-permute-start.7 = (bf16[192,1536]{1,0:T(8,128)(2,1)S(1)}, bf16[192,1536]{1,0:T(8,128)(2,1)S(1)}, u32[]{:S(2)}, u32[]{:S(2)}) collective-permute-start(bf16[192,1536]{1,0:T(8,128)(2,1)S(1)} %shard_map.61), channel_id=1, source_target_pairs={{0,16},{1,9},{2,18},{3,11},{4,20},{5,13},{6,22},{7,15},{8,24},{9,1... | collective-permute-start | bytes 1769480 | tf_op jit(solution)/shard_map/ppermute | solution.py:366
  63.2 18.6 %collective-permute-start.12 = (bf16[192,768]{1,0:T(8,128)(2,1)S(1)}, bf16[192,768]{1,0:T(8,128)(2,1)S(1)}, u32[]{:S(2)}, u32[]{:S(2)}) collective-permute-start(bf16[192,768]{1,0:T(8,128)(2,1)S(1)} %shard_map.69), channel_id=1, source_target_pairs={{0,16},{1,9},{2,18},{3,11},{4,20},{5,13},{6,22},{7,15},{8,24},{9,1... | collective-permute-start | bytes 884744 | tf_op jit(solution)/shard_map/ppermute | solution.py:366
  63.7 18.1 %collective-permute-start.13 = (bf16[192,768]{1,0:T(8,128)(2,1)S(1)}, bf16[192,768]{1,0:T(8,128)(2,1)S(1)}, u32[]{:S(2)}, u32[]{:S(2)}) collective-permute-start(bf16[192,768]{1,0:T(8,128)(2,1)S(1)} %shard_map.70), channel_id=1, source_target_pairs={{0,8},{1,17},{2,10},{3,19},{4,12},{5,21},{6,14},{7,23},{8,0},{9,25... | collective-permute-start | bytes 884744 | tf_op jit(solution)/shard_map/ppermute | solution.py:366
  75.8 11.6 %collective-permute-start.8 = (bf16[192,768]{1,0:T(8,128)(2,1)S(1)}, bf16[192,768]{1,0:T(8,128)(2,1)S(1)}, u32[]{:S(2)}, u32[]{:S(2)}) collective-permute-start(bf16[192,768]{1,0:T(8,128)(2,1)S(1)} %shard_map.63), channel_id=1, source_target_pairs={{0,16},{1,9},{2,18},{3,11},{4,20},{5,13},{6,22},{7,15},{8,24},{9,1... | collective-permute-start | bytes 884744 | tf_op jit(solution)/shard_map/ppermute | solution.py:366
  76.4 11.2 %collective-permute-start.9 = (bf16[192,768]{1,0:T(8,128)(2,1)S(1)}, bf16[192,768]{1,0:T(8,128)(2,1)S(1)}, u32[]{:S(2)}, u32[]{:S(2)}) collective-permute-start(bf16[192,768]{1,0:T(8,128)(2,1)S(1)} %shard_map.64), channel_id=1, source_target_pairs={{0,8},{1,17},{2,10},{3,19},{4,12},{5,21},{6,14},{7,23},{8,0},{9,25... | collective-permute-start | bytes 884744 | tf_op jit(solution)/shard_map/ppermute | solution.py:366

commit v11 on v10

--- a/solution.py
+++ b/solution.py
@@ -24,16 +24,31 @@
 HBM = pl.BlockSpec(memory_space=pltpu.HBM)
 
 
-def pack_frames(key_tok, value_tok):
-    parity = lax.axis_index("frame") % 2
-
-    def packed(key, value, frame):
-        rows = [lax.dynamic_slice_in_dim(array, frame * FRAME_TOK, FRAME_TOK, 0) for array in (key, value)]
-        return jnp.concatenate(rows, axis=0)
-
-    edge = packed(key_tok, value_tok, parity)
-    edge, key_tok, value_tok = lax.optimization_barrier((edge, key_tok, value_tok))
-    return edge, packed(key_tok, value_tok, 1 - parity)
+def pack_frame(key_tok, value_tok, is_edge):
+    def kernel(key, value, out, sems):
+        parity = lax.axis_index("frame") % 2
+        frame = parity if is_edge else 1 - parity
+        copies = [
+            pltpu.make_async_copy(
+                source.at[pl.ds(pl.multiple_of(frame * FRAME_TOK, FRAME_TOK), FRAME_TOK)],
+                out.at[pl.ds(place * FRAME_TOK, FRAME_TOK)],
+                sems.at[place],
+            )
+            for place, source in enumerate((key, value))
+        ]
+        for copy in copies:
+            copy.start()
+        for copy in copies:
+            copy.wait()
+
+    return pl.pallas_call(
+        kernel,
+        out_shape=jax.ShapeDtypeStruct((2 * FRAME_TOK, key_tok.shape[1]), BF16),
+        in_specs=[HBM, HBM],
+        out_specs=VMEM,
+        scratch_shapes=[pltpu.SemaphoreType.DMA((2,))],
+        compiler_params=params(),
+    )(pltpu.with_memory_space_constraint(key_tok, pltpu.HBM), pltpu.with_memory_space_constraint(value_tok, pltpu.HBM))
 
 
 def attend_step(head_span, query_tok, sources, states, cases, first=False, closed=None):
@@ -345,7 +360,8 @@
         pairs = [(i, i + 1) for i in range(1, frames - 1, 2)]
         return lax.ppermute(value, "frame", pairs + [(b, a) for a, b in pairs])
 
-    edge, inner = pack_frames(key_tok, value_tok)
+    edge = pack_frame(key_tok, value_tok, True)
+    inner = pack_frame(key_tok, value_tok, False)
     near = across(edge)
     partner_inner = swap(inner)
     partner_edge = swap(edge)

time: 88.8 us -> 88.7 us (level)
  local copies, waits for them, and re-layouts: 2.65 us -> 0.03 us
  Pallas kernels: 32.3 us -> 34.8 us
    pallas_call x0 -> x2, Pallas kernels: none -> 2.53 us  [pack_frame(): pl.pallas_call(kernel, out_shape=jax.ShapeDtypeStruct((2 * FRAME_TOK, key...]
    dynamic_slice x3 -> x0, local copies, waits for them, and re-layouts: 1.4 us -> none  [packed(): lax.dynamic_slice_in_dim(array, frame * FRAME_TOK, FRAME_TOK, 0)]
    unnamed x12 -> x8, local copies, waits for them, and re-layouts: 1.25 us -> 0.03 us
  transfers between devices with their start and end apart: 14 -> 14, of which waited for: 6 -> 6; matrix products, arithmetic and copies ran while one was open for 0% -> 0% of each run, Pallas kernels for 35% -> 37%
where the time goes in v11:
time: 88.7 us; the launch traced here: 88.5 us
  waiting for transfers between devices  36.9 us (42%)
  Pallas kernels  34.8 us (39%)
  starting transfers between devices  16.2 us (18%)
    pallas_call x6, Pallas kernels, attend_step(): pl.pallas_call(kernel, out_shape=tuple(shapes), in_specs=[SMEM] + [VMEM]...  24.8 us
    ppermute x8, waiting for transfers between devices, exchange(): return lax.ppermute(value, ('head', 'frame'), pairs)  24.4 us
    ppermute x3, waiting for transfers between devices, across(): return lax.ppermute(value, 'frame', pairs + [(b, a) for a, b in pairs])  12.5 us
    ppermute x3, starting transfers between devices, across(): return lax.ppermute(value, 'frame', pairs + [(b, a) for a, b in pairs])  7.6 us
    ppermute x8, starting transfers between devices, exchange(): return lax.ppermute(value, ('head', 'frame'), pairs)  6.69 us
    pallas_call x8, Pallas kernels, project(): pl.pallas_call(kernel, out_shape=jax.ShapeDtypeStruct((rows, len(slots) *...  4.38 us
    pallas_call x2, Pallas kernels, pack_frame(): pl.pallas_call(kernel, out_shape=jax.ShapeDtypeStruct((2 * FRAME_TOK, key...  2.53 us
    ppermute x3, starting transfers between devices, swap(): return lax.ppermute(value, 'frame', [(i, i ^ 1) for i in range(frames)])  1.94 us
  transfers between devices with their start and end apart: 14, of which 6 were waited for; matrix products, arithmetic and copies ran while one was open for 0% of the time, Pallas kernels for 37%

profile of v11, /device:TPU:20, one launch (start us, length us, event | category | flops | bytes accessed | tf_op | source)
XLA Modules:
  0.0 88.5 jit_solution(12242367658834214681)
XLA Ops:
  0.0 1.3 %shard_map.56.refs_0_ = bf16[768,768]{1,0:T(8,128)(2,1)S(1)} custom-call(bf16[768,768]{1,0:T(8,128)(2,1)} %key.3, bf16[768,768]{1,0:T(8,128)(2,1)} %value.3), custom_call_target="tpu_custom_call" | custom-call | tf_op jit(solution)/shard_map/pallas_call | solution.py:44
  1.3 0.0 copy-start
  1.3 0.0 copy-start.1
  1.3 2.1 %collective-permute-start.3 = (bf16[768,768]{1,0:T(8,128)(2,1)S(1)}, bf16[768,768]{1,0:T(8,128)(2,1)S(1)}, u32[]{:S(2)}, u32[]{:S(2)}) collective-permute-start(bf16[768,768]{1,0:T(8,128)(2,1)S(1)} %shard_map.56.refs_0_), channel_id=1, source_target_pairs={{1,2},{3,4},{5,6},{2,1},{4,3},{6,5},{9,10},{11,12},{13,14},{10,9},... | collective-permute-start | bytes 3538952 | tf_op jit(solution)/shard_map/ppermute | solution.py:361
  3.4 1.3 %shard_map.55.refs_1_ = bf16[768,768]{1,0:T(8,128)(2,1)S(1)} custom-call(bf16[768,768]{1,0:T(8,128)(2,1)} %key.3, bf16[768,768]{1,0:T(8,128)(2,1)} %value.3), custom_call_target="tpu_custom_call" | custom-call | tf_op jit(solution)/shard_map/pallas_call | solution.py:44
  4.6 1.7 %collective-permute-start = (bf16[768,768]{1,0:T(8,128)(2,1)S(1)}, bf16[768,768]{1,0:T(8,128)(2,1)S(1)}, u32[]{:S(2)}, u32[]{:S(2)}) collective-permute-start(bf16[768,768]{1,0:T(8,128)(2,1)S(1)} %shard_map.55.refs_1_), channel_id=1, source_target_pairs={{0,1},{1,0},{2,3},{3,2},{4,5},{5,4},{6,7},{7,6},{8,9},{9,8},{10,11... | collective-permute-start | bytes 3538952 | tf_op jit(solution)/shard_map/ppermute | solution.py:357
  6.4 0.1 collective-permute-start.5
  6.5 12.5 %collective-permute-done.3.refs_0_ = bf16[768,768]{1,0:T(8,128)(2,1)S(1)} collective-permute-done((bf16[768,768]{1,0:T(8,128)(2,1)S(1)}, bf16[768,768]{1,0:T(8,128)(2,1)S(1)}, u32[]{:S(2)}, u32[]{:S(2)}) %collective-permute-start.3) | collective-permute-done | bytes 1179680 | tf_op jit(solution)/shard_map/ppermute | solution.py:361
  18.9 0.1 collective-permute-start.4
  19.1 2.3 %collective-permute-start.2 = (bf16[768,768]{1,0:T(8,128)(2,1)S(1)}, bf16[768,768]{1,0:T(8,128)(2,1)S(1)}, u32[]{:S(2)}, u32[]{:S(2)}) collective-permute-start(bf16[768,768]{1,0:T(8,128)(2,1)S(1)} %shard_map.55.refs_1_), channel_id=1, source_target_pairs={{1,2},{3,4},{5,6},{2,1},{4,3},{6,5},{9,10},{11,12},{13,14},{10,9},... | collective-permute-start | bytes 3538952 | tf_op jit(solution)/shard_map/ppermute | solution.py:361
  21.4 0.0 collective-permute-done.refs_2_
  21.4 3.2 %collective-permute-start.1 = (bf16[768,768]{1,0:T(8,128)(2,1)S(1)}, bf16[768,768]{1,0:T(8,128)(2,1)S(1)}, u32[]{:S(2)}, u32[]{:S(2)}) collective-permute-start(bf16[768,768]{1,0:T(8,128)(2,1)S(1)} %collective-permute-done.refs_2_), channel_id=1, source_target_pairs={{1,2},{3,4},{5,6},{2,1},{4,3},{6,5},{9,10},{11,12},{13,14},{10,9},... | collective-permute-start | bytes 3538952 | tf_op jit(solution)/shard_map/ppermute | solution.py:361
  24.7 12.2 %shard_map.57 = (f32[384,768]{1,0:T(8,128)S(1)}, f32[384,768]{1,0:T(8,128)S(1)}, f32[384,768]{1,0:T(8,128)S(1)}, f32[384,768]{1,0:T(8,128)S(1)}, f32[384,768]{1,0:T(8,128)S(1)}, /*index=5*/f32[384,768]{1,0:T(8,128)S(1)}) custom-call(s32[6]{0:T(128)S(1)} %copy-done.1, bf16[768,768]{1,0:T(8,128)(2,1)S(1)} %copy-done, bf16[768,768]{1,0:T(8,128)(2,1)S(1)} %shard_map.56.refs_0_, ...), custom_call_target="tpu_custom_call" | custom-call | tf_op jit(solution)/shard_map/pallas_call | solution.py:169
  36.8 0.0 slice-start
  36.9 4.9 %shard_map.58 = (f32[384,768]{1,0:T(8,128)S(1)}, f32[384,768]{1,0:T(8,128)S(1)}, f32[384,768]{1,0:T(8,128)S(1)}, f32[384,768]{1,0:T(8,128)S(1)}, f32[384,768]{1,0:T(8,128)S(1)}, /*index=5*/f32[384,768]{1,0:T(8,128)S(1)}) custom-call(s32[6]{0:T(128)S(1)} %copy-done.1, ...), custom_call_target="tpu_custom_call", output_to_operand_aliasing={{0}: (3, {}), {1}: (4, {}), {2}: (5, {}), {3}: (6, {}), {4}... | custom-call | tf_op jit(solution)/shard_map/pallas_call | solution.py:169
  41.7 0.0 slice-start.1
  41.8 1.8 %shard_map.59 = (f32[384,768]{1,0:T(8,128)S(1)}, f32[384,768]{1,0:T(8,128)S(1)}, f32[384,768]{1,0:T(8,128)S(1)}, f32[384,768]{1,0:T(8,128)S(1)}, f32[384,768]{1,...) custom-call(s32[6]{0:T(128)S(1)} %copy-done.1, ...), custom_call_target="tpu_custom_call", output_to_operand_aliasing={{0}: (3, {}), {1}: (4, {}), {2}: (5, {}), {3}: (6, {}), {4}... | custom-call | tf_op jit(solution)/shard_map/pallas_call | solution.py:169
  43.5 0.0 collective-permute-done.2.refs_0_
  43.5 1.4 %shard_map.67.left = bf16[384,768]{1,0:T(8,128)(2,1)S(1)} custom-call(s32[6]{0:T(128)S(1)} %copy-done.1, bf16[768,768]{1,0:T(8,128)(2,1)S(1)} %copy-done, bf16[768,768]{1,0:T(8,128)(2,1)S(1)} %collective-permute-done.2.refs_0_, f32[384,768]{1,0:T(8,128)S(1)} %get-tuple-element.49.refs_1_, ...), custom_call_target="tpu_custom_call", output_to_operand_aliasing={{}: (6, {})} | custom-call | tf_op jit(solution)/shard_map/pallas_call | solution.py:169
  45.0 0.7 shard_map.69
  45.7 0.7 shard_map.68
  46.4 0.1 collective-permute-start.10
  46.5 0.1 collective-permute-start.11
  46.5 3.1 %shard_map.60 = (f32[384,768]{1,0:T(8,128)S(1)}, f32[384,768]{1,0:T(8,128)S(1)}, f32[384,768]{1,0:T(8,128)S(1)}, bf16[384,768]{1,0:T(8,128)(2,1)S(1)}) custom-call(s32[6]{0:T(128)S(1)} %copy-done.1, bf16[768,768]{1,0:T(8,128)(2,1)S(1)} %copy-done, ...), custom_call_target="tpu_custom_call", output_to_operand_aliasing={{0}: (3, {}), {1}: (4, {}), {2}: (5, {}), {3}: (6, {})} | custom-call | tf_op jit(solution)/shard_map/pallas_call | solution.py:169
  49.7 0.0 collective-permute-done.1.refs_0_
  49.7 1.4 %shard_map.61.left = bf16[384,768]{1,0:T(8,128)(2,1)S(1)} custom-call(s32[6]{0:T(128)S(1)} %copy-done.1, bf16[768,768]{1,0:T(8,128)(2,1)S(1)} %copy-done, bf16[768,768]{1,0:T(8,128)(2,1)S(1)} %collective-permute-done.1.refs_0_, f32[384,768]{1,0:T(8,128)S(1)} %get-tuple-element.45.refs_1_, ...), custom_call_target="tpu_custom_call", output_to_operand_aliasing={{}: (6, {})} | custom-call | tf_op jit(solution)/shard_map/pallas_call | solution.py:169
  51.1 0.7 shard_map.62
  51.8 2.4 %collective-permute-start.6 = (bf16[192,1536]{1,0:T(8,128)(2,1)S(1)}, bf16[192,1536]{1,0:T(8,128)(2,1)S(1)}, u32[]{:S(2)}, u32[]{:S(2)}) collective-permute-start(bf16[192,1536]{1,0:T(8,128)(2,1)S(1)} %shard_map.62), channel_id=1, source_target_pairs={{0,8},{1,17},{2,10},{3,19},{4,12},{5,21},{6,14},{7,23},{8,0},{9,25... | collective-permute-start | bytes 1769480 | tf_op jit(solution)/shard_map/ppermute | solution.py:382
  54.2 0.6 shard_map.63
  54.9 0.9 collective-permute-start.7
  55.8 6.9 %collective-permute-done.10.rest_0_ = bf16[192,1536]{1,0:T(8,128)(2,1)S(1)} collective-permute-done((bf16[192,1536]{1,0:T(8,128)(2,1)S(1)}, bf16[192,1536]{1,0:T(8,128)(2,1)S(1)}, u32[]{:S(2)}, u32[]{:S(2)}) %collective-permute-start.10) | collective-permute-done | bytes 589856 | tf_op jit(solution)/shard_map/ppermute | solution.py:382
  62.6 0.4 shard_map.71
  63.1 0.1 collective-permute-start.12
  63.1 0.4 shard_map.72
  63.6 1.6 %collective-permute-start.13 = (bf16[192,768]{1,0:T(8,128)(2,1)S(1)}, bf16[192,768]{1,0:T(8,128)(2,1)S(1)}, u32[]{:S(2)}, u32[]{:S(2)}) collective-permute-start(bf16[192,768]{1,0:T(8,128)(2,1)S(1)} %shard_map.72), channel_id=1, source_target_pairs={{0,8},{1,17},{2,10},{3,19},{4,12},{5,21},{6,14},{7,23},{8,0},{9,25... | collective-permute-start | bytes 884744 | tf_op jit(solution)/shard_map/ppermute | solution.py:382
  65.2 10.1 %collective-permute-done.6.rest_0_ = bf16[192,1536]{1,0:T(8,128)(2,1)S(1)} collective-permute-done((bf16[192,1536]{1,0:T(8,128)(2,1)S(1)}, bf16[192,1536]{1,0:T(8,128)(2,1)S(1)}, u32[]{:S(2)}, u32[]{:S(2)}) %collective-permute-start.6) | collective-permute-done | bytes 589856 | tf_op jit(solution)/shard_map/ppermute | solution.py:382
  75.3 0.4 shard_map.65
  75.7 0.1 collective-permute-start.8
  75.8 0.0 collective-permute-done.7.rest_1_.rest_0_
  75.8 0.4 shard_map.66
  76.2 1.5 %collective-permute-start.9 = (bf16[192,768]{1,0:T(8,128)(2,1)S(1)}, bf16[192,768]{1,0:T(8,128)(2,1)S(1)}, u32[]{:S(2)}, u32[]{:S(2)}) collective-permute-start(bf16[192,768]{1,0:T(8,128)(2,1)S(1)} %shard_map.66), channel_id=1, source_target_pairs={{0,8},{1,17},{2,10},{3,19},{4,12},{5,21},{6,14},{7,23},{8,0},{9,25... | collective-permute-start | bytes 884744 | tf_op jit(solution)/shard_map/ppermute | solution.py:382
  77.8 0.7 shard_map.70.terms
  78.5 0.7 shard_map.64.terms
  79.1 2.5 %collective-permute-done.12.rest_0_ = bf16[192,768]{1,0:T(8,128)(2,1)S(1)} collective-permute-done((bf16[192,768]{1,0:T(8,128)(2,1)S(1)}, bf16[192,768]{1,0:T(8,128)(2,1)S(1)}, u32[]{:S(2)}, u32[]{:S(2)}) %collective-permute-start.12) | collective-permute-done | bytes 294944 | tf_op jit(solution)/shard_map/ppermute | solution.py:382
  81.7 0.9 shard_map.73.rest_2_
  82.6 4.8 %collective-permute-done.8.rest_0_ = bf16[192,768]{1,0:T(8,128)(2,1)S(1)} collective-permute-done((bf16[192,768]{1,0:T(8,128)(2,1)S(1)}, bf16[192,768]{1,0:T(8,128)(2,1)S(1)}, u32[]{:S(2)}, u32[]{:S(2)}) %collective-permute-start.8) | collective-permute-done | bytes 294944 | tf_op jit(solution)/shard_map/ppermute | solution.py:382
  87.3 0.1 collective-permute-done.9.rest_1_
  87.4 0.9 shard_map.74
  (9 shorter events, 0.0 us)
Async XLA Ops:
  1.3 23.4 %copy-start = (bf16[768,768]{1,0:T(8,128)(2,1)S(1)}, bf16[768,768]{1,0:T(8,128)(2,1)}, u32[]{:S(2)}) copy-start(bf16[768,768]{1,0:T(8,128)(2,1)} %query.11) | copy-start | bytes 3538948
  1.3 23.4 %copy-start.1 = (s32[6]{0:T(128)S(1)}, s32[6]{0:T(128)}, u32[]{:S(2)}) copy-start(s32[6]{0:T(128)} %span_ref.11) | copy-start | bytes 76
  1.3 17.7 %collective-permute-start.3 = (bf16[768,768]{1,0:T(8,128)(2,1)S(1)}, bf16[768,768]{1,0:T(8,128)(2,1)S(1)}, u32[]{:S(2)}, u32[]{:S(2)}) collective-permute-start(bf16[768,768]{1,0:T(8,128)(2,1)S(1)} %shard_map.56.refs_0_), channel_id=1, source_target_pairs={{1,2},{3,4},{5,6},{2,1},{4,3},{6,5},{9,10},{11,12},{13,14},{10,9},... | collective-permute-start | bytes 3538952 | tf_op jit(solution)/shard_map/ppermute | solution.py:361
  4.6 16.8 %collective-permute-start = (bf16[768,768]{1,0:T(8,128)(2,1)S(1)}, bf16[768,768]{1,0:T(8,128)(2,1)S(1)}, u32[]{:S(2)}, u32[]{:S(2)}) collective-permute-start(bf16[768,768]{1,0:T(8,128)(2,1)S(1)} %shard_map.55.refs_1_), channel_id=1, source_target_pairs={{0,1},{1,0},{2,3},{3,2},{4,5},{5,4},{6,7},{7,6},{8,9},{9,8},{10,11... | collective-permute-start | bytes 3538952 | tf_op jit(solution)/shard_map/ppermute | solution.py:357
  6.4 18.3 %collective-permute-start.5 = (bf16[768,768]{1,0:T(8,128)(2,1)S(1)}, bf16[768,768]{1,0:T(8,128)(2,1)S(1)}, u32[]{:S(2)}, u32[]{:S(2)}) collective-permute-start(bf16[768,768]{1,0:T(8,128)(2,1)S(1)} %shard_map.56.refs_0_), channel_id=1, source_target_pairs={{0,1},{1,0},{2,3},{3,2},{4,5},{5,4},{6,7},{7,6},{8,9},{9,8},{10,11... | collective-permute-start | bytes 3538952 | tf_op jit(solution)/shard_map/ppermute | solution.py:357
  18.9 22.8 %collective-permute-start.4 = (bf16[768,768]{1,0:T(8,128)(2,1)S(1)}, bf16[768,768]{1,0:T(8,128)(2,1)S(1)}, u32[]{:S(2)}, u32[]{:S(2)}) collective-permute-start(bf16[768,768]{1,0:T(8,128)(2,1)S(1)} %collective-permute-done.3.refs_0_), channel_id=1, source_target_pairs={{0,1},{1,0},{2,3},{3,2},{4,5},{5,4},{6,7},{7,6},{8,9},{9,8},{10,11... | collective-permute-start | bytes 3538952 | tf_op jit(solution)/shard_map/ppermute | solution.py:357
  19.1 24.5 %collective-permute-start.2 = (bf16[768,768]{1,0:T(8,128)(2,1)S(1)}, bf16[768,768]{1,0:T(8,128)(2,1)S(1)}, u32[]{:S(2)}, u32[]{:S(2)}) collective-permute-start(bf16[768,768]{1,0:T(8,128)(2,1)S(1)} %shard_map.55.refs_1_), channel_id=1, source_target_pairs={{1,2},{3,4},{5,6},{2,1},{4,3},{6,5},{9,10},{11,12},{13,14},{10,9},... | collective-permute-start | bytes 3538952 | tf_op jit(solution)/shard_map/ppermute | solution.py:361
  21.4 28.3 %collective-permute-start.1 = (bf16[768,768]{1,0:T(8,128)(2,1)S(1)}, bf16[768,768]{1,0:T(8,128)(2,1)S(1)}, u32[]{:S(2)}, u32[]{:S(2)}) collective-permute-start(bf16[768,768]{1,0:T(8,128)(2,1)S(1)} %collective-permute-done.refs_2_), channel_id=1, source_target_pairs={{1,2},{3,4},{5,6},{2,1},{4,3},{6,5},{9,10},{11,12},{13,14},{10,9},... | collective-permute-start | bytes 3538952 | tf_op jit(solution)/shard_map/ppermute | solution.py:361
  36.8 8.1 %slice-start = ((s8[4718592]{0:T(1024)(128)(4,1)}), s8[4194304]{0:T(1024)(128)(4,1)S(1)}, s32[]{:S(2)}) async-start(s8[4718592]{0:T(1024)(128)(4,1)} %bitcast), calls=%async_computation | async-start | bytes 8388608
  41.7 3.3 %slice-start.1 = ((s8[4718592]{0:T(1024)(128)(4,1)}), s8[524288]{0:T(1024)(128)(4,1)S(1)}, s32[]{:S(2)}) async-start(s8[4718592]{0:T(1024)(128)(4,1)} %bitcast), calls=%async_computation.1 | async-start | bytes 1048576
  46.4 16.3 %collective-permute-start.10 = (bf16[192,1536]{1,0:T(8,128)(2,1)S(1)}, bf16[192,1536]{1,0:T(8,128)(2,1)S(1)}, u32[]{:S(2)}, u32[]{:S(2)}) collective-permute-start(bf16[192,1536]{1,0:T(8,128)(2,1)S(1)} %shard_map.68), channel_id=1, source_target_pairs={{0,8},{1,17},{2,10},{3,19},{4,12},{5,21},{6,14},{7,23},{8,0},{9,25... | collective-permute-start | bytes 1769480 | tf_op jit(solution)/shard_map/ppermute | solution.py:382
  46.5 16.7 %collective-permute-start.11 = (bf16[192,1536]{1,0:T(8,128)(2,1)S(1)}, bf16[192,1536]{1,0:T(8,128)(2,1)S(1)}, u32[]{:S(2)}, u32[]{:S(2)}) collective-permute-start(bf16[192,1536]{1,0:T(8,128)(2,1)S(1)} %shard_map.69), channel_id=1, source_target_pairs={{0,16},{1,9},{2,18},{3,11},{4,20},{5,13},{6,22},{7,15},{8,24},{9,1... | collective-permute-start | bytes 1769480 | tf_op jit(solution)/shard_map/ppermute | solution.py:382
  51.8 23.4 %collective-permute-start.6 = (bf16[192,1536]{1,0:T(8,128)(2,1)S(1)}, bf16[192,1536]{1,0:T(8,128)(2,1)S(1)}, u32[]{:S(2)}, u32[]{:S(2)}) collective-permute-start(bf16[192,1536]{1,0:T(8,128)(2,1)S(1)} %shard_map.62), channel_id=1, source_target_pairs={{0,8},{1,17},{2,10},{3,19},{4,12},{5,21},{6,14},{7,23},{8,0},{9,25... | collective-permute-start | bytes 1769480 | tf_op jit(solution)/shard_map/ppermute | solution.py:382
  54.9 20.9 %collective-permute-start.7 = (bf16[192,1536]{1,0:T(8,128)(2,1)S(1)}, bf16[192,1536]{1,0:T(8,128)(2,1)S(1)}, u32[]{:S(2)}, u32[]{:S(2)}) collective-permute-start(bf16[192,1536]{1,0:T(8,128)(2,1)S(1)} %shard_map.63), channel_id=1, source_target_pairs={{0,16},{1,9},{2,18},{3,11},{4,20},{5,13},{6,22},{7,15},{8,24},{9,1... | collective-permute-start | bytes 1769480 | tf_op jit(solution)/shard_map/ppermute | solution.py:382
  63.1 18.6 %collective-permute-start.12 = (bf16[192,768]{1,0:T(8,128)(2,1)S(1)}, bf16[192,768]{1,0:T(8,128)(2,1)S(1)}, u32[]{:S(2)}, u32[]{:S(2)}) collective-permute-start(bf16[192,768]{1,0:T(8,128)(2,1)S(1)} %shard_map.71), channel_id=1, source_target_pairs={{0,16},{1,9},{2,18},{3,11},{4,20},{5,13},{6,22},{7,15},{8,24},{9,1... | collective-permute-start | bytes 884744 | tf_op jit(solution)/shard_map/ppermute | solution.py:382
  63.6 18.1 %collective-permute-start.13 = (bf16[192,768]{1,0:T(8,128)(2,1)S(1)}, bf16[192,768]{1,0:T(8,128)(2,1)S(1)}, u32[]{:S(2)}, u32[]{:S(2)}) collective-permute-start(bf16[192,768]{1,0:T(8,128)(2,1)S(1)} %shard_map.72), channel_id=1, source_target_pairs={{0,8},{1,17},{2,10},{3,19},{4,12},{5,21},{6,14},{7,23},{8,0},{9,25... | collective-permute-start | bytes 884744 | tf_op jit(solution)/shard_map/ppermute | solution.py:382
  75.7 11.6 %collective-permute-start.8 = (bf16[192,768]{1,0:T(8,128)(2,1)S(1)}, bf16[192,768]{1,0:T(8,128)(2,1)S(1)}, u32[]{:S(2)}, u32[]{:S(2)}) collective-permute-start(bf16[192,768]{1,0:T(8,128)(2,1)S(1)} %shard_map.65), channel_id=1, source_target_pairs={{0,16},{1,9},{2,18},{3,11},{4,20},{5,13},{6,22},{7,15},{8,24},{9,1... | collective-permute-start | bytes 884744 | tf_op jit(solution)/shard_map/ppermute | solution.py:382
  76.2 11.2 %collective-permute-start.9 = (bf16[192,768]{1,0:T(8,128)(2,1)S(1)}, bf16[192,768]{1,0:T(8,128)(2,1)S(1)}, u32[]{:S(2)}, u32[]{:S(2)}) collective-permute-start(bf16[192,768]{1,0:T(8,128)(2,1)S(1)} %shard_map.66), channel_id=1, source_target_pairs={{0,8},{1,17},{2,10},{3,19},{4,12},{5,21},{6,14},{7,23},{8,0},{9,25... | collective-permute-start | bytes 884744 | tf_op jit(solution)/shard_map/ppermute | solution.py:382
